TPU v7x, 32 devices: a whole 2x2x4 slice. The times are simulated.
32 devices in a mesh: dp: 2 (over x), feat: 16 (over z, y, core).
Axes of the slice: x: 2, y: 2, z: 4, core: 2. Of those that a mesh axis runs over, the one named last changes fastest.
Arguments:
- inputs: bfloat16 [1024, 8192], P('dp', 'feat'), may hold values from -6 to 6
- bfly: bfloat16 [64, 7, 128, 512], P('feat'), may hold values from -0.1875 to 0.1875
- lr_u: bfloat16 [8192, 256], P('feat'), may hold values from -0.0625 to 0.0625
- lr_v: bfloat16 [256, 32768], P(None, 'feat'), may hold values from -0.375 to 0.375
- cotangent: bfloat16 [1024, 32768], P('dp', 'feat'), may hold values from -6 to 6
Outputs:
- activated: bfloat16 [1024, 32768], P('dp', 'feat')
- d_inputs: bfloat16 [1024, 8192], P('dp', 'feat')
- d_bfly: float32 [64, 7, 128, 512], P('feat')
- d_u: float32 [8192, 256], P('feat')
- d_v: float32 [256, 32768], P(None, 'feat')
All inputs are finite; a program needn't handle non-finite values.
Results may differ from a plain program's by a relative error of at most 0.0065.
Values may be sent and summed in bfloat16 or wider, within the bound.
No kernel may reach another device: no remote copies, remote signals or barrier semaphores. Data moves between devices by JAX's collectives and lax.ppermute only.
A program may use at most 128 MiB of HBM per device.

v0:
```python
import jax
import jax.numpy as jnp
from jax import lax
from jax.sharding import PartitionSpec as P


def swapped(block, axis, distance):
    count = lax.axis_size(axis)
    route = []
    for low in range(count):
        high = low | 1 << distance
        if high != low and high < count:
            route += [(low, high), (high, low)]
    return lax.ppermute(block, axis, route)


def gelu_tanh(value):
    return jax.nn.gelu(value, approximate=True)


def flip_blocks(array, step):
    lead = array.shape[0]
    count = array.shape[1]
    rest = array.shape[2:]
    split = array.reshape((lead, count // (2 * step), 2, step) + rest)
    return split[:, :, ::-1].reshape(array.shape)


def local(inputs, bfly, lr_u, lr_v, cotangent):
    tokens = inputs.shape[0]
    per_dev = bfly.shape[0]
    sections = bfly.shape[1]
    width = bfly.shape[2]
    group = bfly.shape[3]
    levels = sections - 1
    local_bits = per_dev.bit_length() - 1
    blocks = inputs.reshape(tokens, per_dev, width)

    def fetch_input(section):
        if 1 << section < per_dev:
            return flip_blocks(blocks, 1 << section)
        return swapped(blocks, "feat", section - local_bits)

    partners = [fetch_input(section) for section in range(levels)] + [blocks]
    butterfly = jnp.zeros((tokens, per_dev, group), jnp.float32)
    for section in range(sections):
        butterfly = butterfly + jnp.einsum(
            "tbi,bio->tbo", partners[section], bfly[:, section], preferred_element_type=jnp.float32
        )
    low = lax.psum(jnp.dot(inputs, lr_u, preferred_element_type=jnp.float32), "feat").astype(
        jnp.bfloat16
    )
    pre = butterfly.reshape(tokens, per_dev * group) + jnp.dot(
        low, lr_v, preferred_element_type=jnp.float32
    )
    activated, backward = jax.vjp(gelu_tanh, pre)
    d_pre = backward(cotangent.astype(jnp.float32))[0].astype(jnp.bfloat16)
    d_low = lax.psum(jnp.dot(d_pre, lr_v.T, preferred_element_type=jnp.float32), "feat").astype(
        jnp.bfloat16
    )
    grad_groups = d_pre.reshape(tokens, per_dev, group)
    d_inputs = jnp.dot(d_low, lr_u.T, preferred_element_type=jnp.float32).reshape(
        tokens, per_dev, width
    )
    for section in range(sections):
        if section == levels:
            term = jnp.einsum(
                "tbo,bio->tbi", grad_groups, bfly[:, section], preferred_element_type=jnp.float32
            ).astype(jnp.bfloat16)
        else:
            mine = jnp.einsum(
                "tbo,bio->tbi", grad_groups, bfly[:, section], preferred_element_type=jnp.float32
            ).astype(jnp.bfloat16)
            if 1 << section < per_dev:
                term = flip_blocks(mine, 1 << section)
            else:
                term = swapped(mine, "feat", section - local_bits)
        d_inputs = d_inputs + lax.optimization_barrier(term).astype(jnp.float32)
    tiles = [
        jnp.einsum(
            "tbi,tbo->bio", partners[section], grad_groups, preferred_element_type=jnp.float32
        )
        for section in range(sections)
    ]
    d_bfly = jnp.stack(tiles, axis=1)
    d_u = jnp.dot(inputs.T, d_low, preferred_element_type=jnp.float32)
    d_v = jnp.dot(low.T, d_pre, preferred_element_type=jnp.float32)
    d_bfly, d_u, d_v = lax.psum((d_bfly, d_u, d_v), "dp")
    scale = 1.0 / jnp.sqrt(jnp.float32(tokens * lax.axis_size("dp")))
    return (
        activated.astype(jnp.bfloat16),
        d_inputs.reshape(tokens, per_dev * width).astype(jnp.bfloat16),
        d_bfly * scale,
        d_u * scale,
        d_v * scale,
    )


def solution(mesh):
    return jax.shard_map(
        local,
        mesh=mesh,
        in_specs=(
            P("dp", "feat"),
            P("feat", None, None, None),
            P("feat", None),
            P(None, "feat"),
            P("dp", "feat"),
        ),
        out_specs=(
            P("dp", "feat"),
            P("dp", "feat"),
            P("feat", None, None, None),
            P("feat", None),
            P(None, "feat"),
        ),
        check_vma=False,
    )
```

profile of v0, /device:TPU:0, one launch (start us, length us, event | category | flops | bytes accessed | tf_op | source)
XLA Modules:
  0.0 474.9 jit_solution(3302909418055266698)
XLA Ops:
  9.6 3.0 collective-permute-start.2
  14.1 2.6 collective-permute-start.3
  16.7 2.0 reshape_reshape.7
  18.7 2.0 reshape_reshape.6
  20.6 3.8 fusion.23
  24.4 2.2 rev.13
  28.5 3.8 fusion.40
  32.4 5.6 %rev.12 = bf16[512,2,2,1,128]{4,2,1,0,3:T(2,128)(2,1)} reverse(bf16[512,2,2,1,128]{4,2,1,0,3:T(2,128)(2,1)} %reshape_reshape.6), dimensions={2} | reverse | bytes 1048576 | tf_op jit(solution)/shard_map/rev | solution.py:26
  40.3 3.9 fusion.43
  44.2 63.2 %all-reduce.6 = bf16[512,256]{1,0:T(8,128)(2,1)S(1)} all-reduce(f32[512,256]{1,0:T(8,128)S(1)} %copy-done.23), channel_id=1, replica_groups=mesh['dp'=2,'feat'=16] {'feat'}, use_global_device_ids=true, to_apply=%region_0.0 | all-reduce | flops 131072 | bytes 786432 | tf_op jit(solution)/shard_map/psum | solution.py:50
  107.4 2.0 fusion.31
  109.5 2.0 fusion.34
  111.5 4.0 fusion.37
  115.6 6.4 %add_add_fusion = f32[4,512,512]{2,1,0:T(8,128)} fusion(f32[4,512,512]{2,1,0:T(8,128)S(1)} %copy-done.2, f32[4,512,512]{2,1,0:T(8,128)S(1)} %fusion.31, f32[4,512,512]{2,1,0:T(8,128)S(1)} %fusion.34, f32[4,512,512]{2,1,0:T(8,128)} %fusion.37, f32[4,512,512]{2,1,0:T(8,128)S(1)} %copy-done.4, f32[4,512,512]{2,1,0:T(8,128)S(1)} %copy-done.3, ...), kind=kOutput, calls=%fused_computation.14 | convolution fusion | flops 274726912 | bytes 30408704 | tf_op jit(solution)/shard_map/tbi,bio->tbo/dot_general | solution.py:47
  122.0 5.6 %copy.59 = f32[512,2048]{1,0:T(8,128)} copy(f32[512,2048]{0,1:T(8,128)} %bitcast.176) | data formatting | bytes 8388608 | tf_op jit(solution)/shard_map/reshape | solution.py:53
  127.6 6.7 %fusion.2 = (bf16[512,2048]{1,0:T(8,128)(2,1)}, bf16[512,2048]{1,0:T(8,128)(2,1)}) fusion(bf16[512,2048]{1,0:T(8,128)(2,1)S(1)} %copy-done.27, f32[512,2048]{1,0:T(8,128)} %copy.59, bf16[512,256]{1,0:T(8,128)(2,1)S(1)} %all-reduce.6, bf16[256,2048]{1,0:T(8,128)(2,1)S(1)} %copy-done), kind=kOutput, calls=%fused_computation.6 | convolution fusion | flops 562036736 | bytes 11796480 | tf_op jit(solution)/shard_map/dot_general | solution.py:53
  134.4 2.9 copy.103
  137.3 3.9 fusion.68
  151.1 2.8 fusion.11
  155.6 63.6 %all-reduce.7 = bf16[512,256]{1,0:T(8,128)(2,1)S(1)} all-reduce(f32[512,256]{1,0:T(8,128)} %fusion.66), channel_id=1, replica_groups=mesh['dp'=2,'feat'=16] {'feat'}, use_global_device_ids=true, to_apply=%region_1.0 | all-reduce | flops 131072 | bytes 786432 | tf_op jit(solution)/shard_map/psum | solution.py:58
  220.3 2.8 fusion.17
  223.1 2.9 fusion.18
  225.9 2.7 fusion.19
  228.7 2.7 fusion.20
  235.7 2.0 convolution_convert_fusion.5
  238.6 2.7 fusion.21
  242.0 7.4 %collective-permute-done.6 = bf16[512,4,128]{2,0,1:T(8,128)(2,1)} collective-permute-done((bf16[512,4,128]{2,0,1:T(8,128)(2,1)}, bf16[512,4,128]{2,0,1:T(8,128)(2,1)}, u32[]{:S(2)}, u32[]{:S(2)}) %collective-permute-start.6) | collective-permute-done | bytes 524320 | tf_op jit(solution)/shard_map/ppermute | solution.py:14
  249.4 8.8 %collective-permute-done.7 = bf16[512,4,128]{2,0,1:T(8,128)(2,1)} collective-permute-done((bf16[512,4,128]{2,0,1:T(8,128)(2,1)}, bf16[512,4,128]{2,0,1:T(8,128)(2,1)}, u32[]{:S(2)}, u32[]{:S(2)}) %collective-permute-start.7) | collective-permute-done | bytes 524320 | tf_op jit(solution)/shard_map/ppermute | solution.py:14
  258.2 2.2 add_convert_fusion
  261.6 189.0 %all-reduce.5.cloned.1.call-done = (f32[4,7,128,512]{2,3,0,1:T(8,128)}, f32[512,256]{0,1:T(8,128)}, f32[256,2048]{1,0:T(8,128)}) async-done(((f32[4,7,128,512]{2,3,0,1:T(8,128)}, f32[512,256]{0,1:T(8,128)}, f32[256,2048]{1,0:T(8,128)}), (f32[4,7,128,512]{2,3,0,1:T(8,128)}, f32[512,256]{0,1:T(8,128)}, f32[256,2048]{1,0:T(8,128)})) %all-reduce.5.cloned.1.call-update) | async-done | bytes 9961488 | tf_op jit(solution)/shard_map/psum | solution.py:88
  450.7 6.8 %broadcast_multiply_fusion = f32[4,7,128,512]{2,3,0,1:T(8,128)} fusion(f32[4,7,128,512]{2,3,0,1:T(8,128)} %get-tuple-element.15), kind=kLoop, calls=%fused_computation.16 | loop fusion | flops 1835008 | bytes 14680064 | tf_op jit(solution)/shard_map/mul | solution.py:93
  457.5 8.1 %copy.85 = f32[4,7,128,512]{3,2,1,0:T(8,128)} copy(f32[4,7,128,512]{2,3,0,1:T(8,128)} %broadcast_multiply_fusion) | data formatting | bytes 14680064
  (93 shorter events, 30.4 us)
Async XLA Ops:
  7.2 120.5 %copy-start = (bf16[256,2048]{1,0:T(8,128)(2,1)S(1)}, bf16[256,2048]{1,0:T(8,128)(2,1)}, u32[]{:S(2)}) copy-start(bf16[256,2048]{1,0:T(8,128)(2,1)} %param.8) | copy-start | bytes 3145732
  7.2 443.5 %all-reduce.5.cloned.1.call-start = ((), (), s32[]{:S(2)}) async-start(), calls=%async_computation | async-start | bytes 19922944 | tf_op jit(solution)/shard_map/psum | solution.py:88
  8.6 15.9 %copy-start.7 = (bf16[512,512]{0,1:T(8,128)(2,1)}, bf16[512,512]{0,1:T(8,128)(2,1)S(1)}, u32[]{:S(2)}) copy-start(bf16[512,512]{0,1:T(8,128)(2,1)S(1)} %copy.49) | copy-start | bytes 1572868
  9.6 97.8 %collective-permute-start.2 = (bf16[512,4,128]{2,0,1:T(8,128)(2,1)}, bf16[512,4,128]{2,0,1:T(8,128)(2,1)S(1)}, u32[]{:S(2)}, u32[]{:S(2)}) collective-permute-start(bf16[512,4,128]{2,0,1:T(8,128)(2,1)} %copy.50), channel_id=1, source_target_pairs={{0,4},{4,0},{1,5},{5,1},{2,6},{6,2},{3,7},{7,3},{8,12},{12,8},{9,1... | collective-permute-start | bytes 1572872 | tf_op jit(solution)/shard_map/ppermute | solution.py:14
  12.6 96.9 %collective-permute-start.1 = (bf16[512,4,128]{2,0,1:T(8,128)(2,1)}, bf16[512,4,128]{2,0,1:T(8,128)(2,1)S(1)}, u32[]{:S(2)}, u32[]{:S(2)}) collective-permute-start(bf16[512,4,128]{2,0,1:T(8,128)(2,1)} %copy.50), channel_id=1, source_target_pairs={{0,2},{2,0},{1,3},{3,1},{4,6},{6,4},{5,7},{7,5},{8,10},{10,8},{9,1... | collective-permute-start | bytes 1572872 | tf_op jit(solution)/shard_map/ppermute | solution.py:14
  14.1 97.4 %collective-permute-start = (bf16[512,4,128]{2,0,1:T(8,128)(2,1)}, bf16[512,4,128]{2,0,1:T(8,128)(2,1)S(1)}, u32[]{:S(2)}, u32[]{:S(2)}) collective-permute-start(bf16[512,4,128]{2,0,1:T(8,128)(2,1)} %copy.50), channel_id=1, source_target_pairs={{0,1},{1,0},{2,3},{3,2},{4,5},{5,4},{6,7},{7,6},{8,9},{9,8},{10,11... | collective-permute-start | bytes 1572872 | tf_op jit(solution)/shard_map/ppermute | solution.py:14
  14.1 101.5 %collective-permute-start.3 = (bf16[512,4,128]{2,0,1:T(8,128)(2,1)}, bf16[512,4,128]{2,0,1:T(8,128)(2,1)}, u32[]{:S(2)}, u32[]{:S(2)}) collective-permute-start(bf16[512,4,128]{2,0,1:T(8,128)(2,1)} %copy.50), channel_id=1, source_target_pairs={{0,8},{8,0},{1,9},{9,1},{2,10},{10,2},{3,11},{11,3},{4,12},{12,4},... | collective-permute-start | bytes 1572872 | tf_op jit(solution)/shard_map/ppermute | solution.py:14
  28.5 10.6 %copy-start.5 = (bf16[512,512]{1,0:T(8,128)(2,1)S(1)}, bf16[512,512]{1,0:T(8,128)(2,1)}, u32[]{:S(2)}) copy-start(bf16[512,512]{1,0:T(8,128)(2,1)} %param.5) | copy-start | bytes 1572868
  28.5 10.6 %copy-start.24 = (bf16[512,256]{1,0:T(8,128)(2,1)S(1)}, bf16[512,256]{1,0:T(8,128)(2,1)}, u32[]{:S(2)}) copy-start(bf16[512,256]{1,0:T(8,128)(2,1)} %param.7) | copy-start | bytes 786436
  40.3 3.9 copy-start.23
  107.4 4.1 copy-start.12
  107.4 8.2 %copy-start.4 = (f32[4,512,512]{2,1,0:T(8,128)S(1)}, f32[4,512,512]{2,1,0:T(8,128)}, u32[]{:S(2)}) copy-start(f32[4,512,512]{2,1,0:T(8,128)} %fusion.43) | copy-start | bytes 12582916
  109.5 6.1 %copy-start.14 = (bf16[512,4,128]{2,0,1:T(8,128)(2,1)}, bf16[512,4,128]{2,0,1:T(8,128)(2,1)S(1)}, u32[]{:S(2)}) copy-start(bf16[512,4,128]{2,0,1:T(8,128)(2,1)S(1)} %collective-permute-done.1) | copy-start | bytes 1572868
  109.5 6.1 %copy-start.3 = (f32[4,512,512]{2,1,0:T(8,128)S(1)}, f32[4,512,512]{2,1,0:T(8,128)}, u32[]{:S(2)}) copy-start(f32[4,512,512]{2,1,0:T(8,128)} %fusion.40) | copy-start | bytes 12582916
  111.5 4.1 copy-start.2
  111.5 10.5 %copy-start.16 = (bf16[512,4,128]{2,0,1:T(8,128)(2,1)}, bf16[512,4,128]{2,0,1:T(8,128)(2,1)S(1)}, u32[]{:S(2)}) copy-start(bf16[512,4,128]{2,0,1:T(8,128)(2,1)S(1)} %collective-permute-done) | copy-start | bytes 1572868
  122.0 5.6 %copy-start.27 = (bf16[512,2048]{1,0:T(8,128)(2,1)S(1)}, bf16[512,2048]{1,0:T(8,128)(2,1)}, u32[]{:S(2)}) copy-start(bf16[512,2048]{1,0:T(8,128)(2,1)} %param.9) | copy-start | bytes 6291460
  137.3 3.9 copy-start.9
  142.7 3.4 copy-start.17
  144.4 3.4 copy-start.15
  146.1 3.4 copy-start.13
  149.4 4.5 copy-start.8
  151.1 68.0 %copy-start.6 = (bf16[512,512]{1,0:T(8,128)(2,1)S(1)}, bf16[512,512]{1,0:T(8,128)(2,1)}, u32[]{:S(2)}) copy-start(bf16[512,512]{1,0:T(8,128)(2,1)} %param.5) | copy-start | bytes 1572868
  223.1 18.9 %collective-permute-start.4 = (bf16[512,4,128]{2,0,1:T(8,128)(2,1)}, bf16[512,4,128]{2,0,1:T(8,128)(2,1)}, u32[]{:S(2)}, u32[]{:S(2)}) collective-permute-start(bf16[512,4,128]{2,0,1:T(8,128)(2,1)} %fusion.17), channel_id=1, source_target_pairs={{0,1},{1,0},{2,3},{3,2},{4,5},{5,4},{6,7},{7,6},{8,9},{9,8},{10,11... | collective-permute-start | bytes 1572872 | tf_op jit(solution)/shard_map/ppermute | solution.py:14
  225.9 16.1 %collective-permute-start.5 = (bf16[512,4,128]{2,0,1:T(8,128)(2,1)}, bf16[512,4,128]{2,0,1:T(8,128)(2,1)}, u32[]{:S(2)}, u32[]{:S(2)}) collective-permute-start(bf16[512,4,128]{2,0,1:T(8,128)(2,1)} %fusion.18), channel_id=1, source_target_pairs={{0,2},{2,0},{1,3},{3,1},{4,6},{6,4},{5,7},{7,5},{8,10},{10,8},{9,1... | collective-permute-start | bytes 1572872 | tf_op jit(solution)/shard_map/ppermute | solution.py:14
  228.7 20.8 %collective-permute-start.6 = (bf16[512,4,128]{2,0,1:T(8,128)(2,1)}, bf16[512,4,128]{2,0,1:T(8,128)(2,1)}, u32[]{:S(2)}, u32[]{:S(2)}) collective-permute-start(bf16[512,4,128]{2,0,1:T(8,128)(2,1)} %fusion.19), channel_id=1, source_target_pairs={{0,4},{4,0},{1,5},{5,1},{2,6},{6,2},{3,7},{7,3},{8,12},{12,8},{9,1... | collective-permute-start | bytes 1572872 | tf_op jit(solution)/shard_map/ppermute | solution.py:14
  231.4 26.8 %collective-permute-start.7 = (bf16[512,4,128]{2,0,1:T(8,128)(2,1)}, bf16[512,4,128]{2,0,1:T(8,128)(2,1)}, u32[]{:S(2)}, u32[]{:S(2)}) collective-permute-start(bf16[512,4,128]{2,0,1:T(8,128)(2,1)} %fusion.20), channel_id=1, source_target_pairs={{0,8},{8,0},{1,9},{9,1},{2,10},{10,2},{3,11},{11,3},{4,12},{12,4},... | collective-permute-start | bytes 1572872 | tf_op jit(solution)/shard_map/ppermute | solution.py:14
  235.7 5.6 %copy-start.25 = (bf16[512,256]{1,0:T(8,128)(2,1)S(1)}, bf16[512,256]{1,0:T(8,128)(2,1)}, u32[]{:S(2)}) copy-start(bf16[512,256]{1,0:T(8,128)(2,1)} %param.7) | copy-start | bytes 786436
  241.3 16.9 %copy-start.20 = (bf16[512,1,2,2,128]{4,0,3,2,1:T(8,128)(2,1)S(1)}, bf16[512,1,2,2,128]{4,0,3,2,1:T(8,128)(2,1)}, u32[]{:S(2)}) copy-start(bf16[512,1,2,2,128]{4,0,3,2,1:T(8,128)(2,1)} %rev.15) | copy-start | bytes 1572868
  241.3 16.9 %copy-start.22 = (bf16[512,4,128]{2,0,1:T(8,128)(2,1)S(1)}, bf16[512,4,128]{2,0,1:T(8,128)(2,1)}, u32[]{:S(2)}) copy-start(bf16[512,4,128]{2,0,1:T(8,128)(2,1)} %fusion.21) | copy-start | bytes 1572868
  457.5 8.1 %copy-start.21 = (f32[256,2048]{1,0:T(8,128)S(1)}, f32[256,2048]{1,0:T(8,128)}, u32[]{:S(2)}) copy-start(f32[256,2048]{1,0:T(8,128)} %get-tuple-element.17) | copy-start | bytes 6291460
  457.5 10.6 %copy-start.1 = (bf16[256,2048]{1,0:T(8,128)(2,1)S(1)}, bf16[256,2048]{1,0:T(8,128)(2,1)}, u32[]{:S(2)}) copy-start(bf16[256,2048]{1,0:T(8,128)(2,1)} %param.8) | copy-start | bytes 3145732
  (5 other events, 8.2 us)
Sparse Core Ops, SparseCore 0:
  220.4 230.2 all-reduce.4
where the time goes:
time: 476 us; the launch traced here: 475 us
  waiting for transfers between devices  205 us (43%)
  blocking collectives  127 us (27%)
  matrix products  71.3 us (15%)
  local copies, waits for them, and re-layouts  38 us (8%)
  between operations  14.3 us (3%)
  other arithmetic  10.5 us (2%)
  starting transfers between devices  8.7 us (2%)
    psum x1, waiting for transfers between devices, local(): d_bfly, d_u, d_v = lax.psum((d_bfly, d_u, d_v), 'dp')  189 us
    psum x1, blocking collectives, local(): lax.psum(jnp.dot(d_pre, lr_v.T, preferred_element_type=jnp.float32), 'feat')  63.6 us
    psum x1, blocking collectives, local(): lax.psum(jnp.dot(inputs, lr_u, preferred_element_type=jnp.float32), 'feat')  63.2 us
    dot_general x7, matrix products, local(): jnp.einsum('tbi,bio->tbo', partners[section], bfly[:, section], preferred...  26 us
    dot_general x7, matrix products, local(): jnp.einsum('tbo,bio->tbi', grad_groups, bfly[:, section], preferred_eleme...  17.8 us
    ppermute x8, waiting for transfers between devices, swapped(): return lax.ppermute(block, axis, route)  16.2 us
    dot_general x7, matrix products, local(): jnp.einsum('tbi,tbo->bio', partners[section], grad_groups, preferred_elem...  12.9 us
    unnamed x60, local copies, waits for them, and re-layouts  12.3 us
  transfers between devices with their start and end apart: 9, of which 3 were waited for; matrix products, arithmetic and copies ran while one was open for 12% of the time, Pallas kernels for 0%

commit v1 on v0

v1 whole, which is shorter than its diff:
```python
import functools

import jax
import jax.numpy as jnp
import numpy as np
from jax import lax
from jax.experimental import pallas as pl
from jax.experimental.pallas import tpu as pltpu
from jax.sharding import PartitionSpec as P

BF = jnp.bfloat16
F32 = jnp.float32
VMEM_LIMIT = 48 * 1024 * 1024
GELU_C = float(np.sqrt(2.0 / np.pi))
GELU_A = 0.044715


def crossed(block, axis, mask):
    count = lax.axis_size(axis)
    return lax.ppermute(block, axis, [(i, i ^ mask) for i in range(count)])


def rolled(block, axis, shift):
    count = lax.axis_size(axis)
    return lax.ppermute(block, axis, [(i, (i + shift) % count) for i in range(count)])


def scatter_half(part, bit, axis):
    rows = part.shape[0] // 2
    mine = (lax.axis_index(axis) >> bit) & 1
    keep = lax.dynamic_slice_in_dim(part, mine * rows, rows, 0)
    send = lax.dynamic_slice_in_dim(part, (1 - mine) * rows, rows, 0)
    return keep + crossed(send.astype(BF), axis, 1 << bit).astype(F32)


def gather_half(part, bit, axis):
    mine = (lax.axis_index(axis) >> bit) & 1
    other = crossed(part, axis, 1 << bit)
    low = jnp.where(mine == 0, part, other)
    high = jnp.where(mine == 0, other, part)
    return jnp.concatenate([low, high], 0)


def reduce_feat(part, axis):
    bits = lax.axis_size(axis).bit_length() - 1
    near = min(bits, 2)
    for bit in range(near):
        part = scatter_half(part, bit, axis)
    sent = part.astype(BF)
    for other in range(1, 1 << (bits - near)):
        part = part + crossed(sent, axis, other << near).astype(F32)
    part = part.astype(BF)
    for bit in range(near - 1, 0, -1):
        part = gather_half(part, bit, axis)
    return part


def finish_feat(part, axis):
    if lax.axis_size(axis) > 1:
        part = gather_half(part, 0, axis)
    return part


def gelu_parts(pre):
    square = pre * pre
    tanh = jnp.tanh(GELU_C * (pre + GELU_A * (square * pre)))
    half = 0.5 * (1.0 + tanh)
    slope = half + (0.5 * GELU_C) * pre * (1.0 - tanh * tanh) * (1.0 + (3.0 * GELU_A) * square)
    return pre * half, slope


def nt(a, b):
    return lax.dot_general(a, b, (((1,), (1,)), ((), ())), preferred_element_type=F32)


def tn(a, b):
    return lax.dot_general(a, b, (((0,), (0,)), ((), ())), preferred_element_type=F32)


def forward_kernel(sections, *refs):
    x = refs[:sections]
    bfly, low, lr_v, cot, act, d_pre, d_low = refs[sections : sections + 7]
    terms = refs[sections + 7 :]
    width = bfly.shape[2]
    tiles = bfly[0].reshape(sections * width, bfly.shape[3])
    block = jnp.concatenate([ref[...] for ref in x], axis=1)
    pre = jnp.dot(block, tiles, preferred_element_type=F32) + jnp.dot(
        low[...], lr_v[...], preferred_element_type=F32
    )
    value, slope = gelu_parts(pre)
    act[...] = value.astype(BF)
    grad = (cot[...].astype(F32) * slope).astype(BF)
    d_pre[...] = grad
    part = nt(grad, lr_v[...])

    @pl.when(pl.program_id(0) == 0)
    def _():
        d_low[...] = part

    @pl.when(pl.program_id(0) > 0)
    def _():
        d_low[...] += part

    back = nt(grad, tiles).astype(BF)
    for section in range(sections):
        terms[section][...] = back[:, section * width : (section + 1) * width]


def own_grad_kernel(sections, *refs):
    x = refs[:sections]
    low, d_pre, d_bfly, d_v = refs[sections:]
    block = jnp.concatenate([ref[...] for ref in x], axis=1)
    d_bfly[0] = tn(block, d_pre[...]).reshape(d_bfly.shape[1:])
    d_v[...] = tn(low[...], d_pre[...])


def other_grad_kernel(sections, scale, *refs):
    x = refs[:sections]
    bfly, low, lr_v, cot, d_bfly_in, d_v_in, d_bfly, d_v = refs[sections:]
    width = bfly.shape[2]
    tiles = bfly[0].reshape(sections * width, bfly.shape[3])
    block = jnp.concatenate([ref[...] for ref in x], axis=1)
    pre = jnp.dot(block, tiles, preferred_element_type=F32) + jnp.dot(
        low[...], lr_v[...], preferred_element_type=F32
    )
    _, slope = gelu_parts(pre)
    grad = (cot[...].astype(F32) * slope).astype(BF)
    d_bfly[0] = (d_bfly_in[0] + tn(block, grad).reshape(d_bfly.shape[1:])) * scale
    d_v[...] = (d_v_in[...] + tn(low[...], grad)) * scale


def column(rows, width, flip):
    return pl.BlockSpec((rows, width), lambda g: (0, g ^ flip))


def resident(*shape):
    return pl.BlockSpec(shape, lambda g: (0,) * len(shape))


def call(kernel, grid, in_specs, out_specs, out_shape, cost, aliases=None, name=None):
    return pl.pallas_call(
        kernel,
        grid=(grid,),
        in_specs=in_specs,
        out_specs=out_specs,
        out_shape=out_shape,
        input_output_aliases=aliases or {},
        cost_estimate=pl.CostEstimate(flops=cost[0], bytes_accessed=cost[1], transcendentals=0),
        compiler_params=pltpu.CompilerParams(vmem_limit_bytes=VMEM_LIMIT),
        name=name,
    )


def local(inputs, bfly, lr_u, lr_v, cotangent):
    tokens = inputs.shape[0]
    per_dev, sections, width, group = bfly.shape
    levels = sections - 1
    rank = lr_v.shape[0]
    local_bits = per_dev.bit_length() - 1
    data_groups = lax.axis_size("dp")
    scale = float(1.0 / np.sqrt(np.float32(tokens * data_groups)))
    remote = range(local_bits, levels)

    flips = [(1 << s) if s < local_bits else 0 for s in range(sections)]
    x_specs = [column(tokens, width, flip) for flip in flips]
    bfly_spec = pl.BlockSpec((1, sections, width, group), lambda g: (g, 0, 0, 0))
    low_spec = resident(tokens, rank)
    lr_v_spec = pl.BlockSpec((rank, group), lambda g: (0, g))
    wide_spec = column(tokens, group, 0)

    def fetch(block):
        got = {s: crossed(block, "feat", 1 << (s - local_bits)) for s in reversed(remote)}
        return [got.get(s, block) for s in range(sections)]

    low_part = jnp.dot(inputs, lr_u, preferred_element_type=F32)
    others = range(1, data_groups)
    x_others = [rolled(inputs, "dp", d) for d in others]
    partners = fetch(inputs)
    cot_others = [rolled(cotangent, "dp", d) for d in others]
    low_half = reduce_feat(low_part, "feat")
    low = finish_feat(low_half, "feat")
    low_others = [finish_feat(rolled(low_half, "dp", d), "feat") for d in others]
    partners_others = [fetch(x) for x in x_others]

    wide = jax.ShapeDtypeStruct((tokens, per_dev * group), BF)
    narrow = jax.ShapeDtypeStruct((tokens, per_dev * width), BF)
    unit = 2 * tokens * group * per_dev
    depth = sections * width
    out = call(
        functools.partial(forward_kernel, sections),
        per_dev,
        x_specs + [bfly_spec, low_spec, lr_v_spec, wide_spec],
        [wide_spec, wide_spec, resident(tokens, rank)] + x_specs,
        [wide, wide, jax.ShapeDtypeStruct((tokens, rank), F32)] + [narrow] * sections,
        (unit * 2 * (depth + rank), 20 * 2**20),
        name="forward",
    )(*partners, bfly, low, lr_v, cotangent)
    activated, d_pre, d_low_part = out[:3]
    terms = list(out[3:])
    for s in reversed(remote):
        terms[s] = crossed(terms[s], "feat", 1 << (s - local_bits))

    d_low_half = reduce_feat(d_low_part, "feat")
    d_low = finish_feat(d_low_half, "feat")
    d_low_others = [finish_feat(rolled(d_low_half, "dp", d), "feat") for d in others]

    tile_spec = bfly_spec
    tile_shape = jax.ShapeDtypeStruct(bfly.shape, F32)
    v_shape = jax.ShapeDtypeStruct(lr_v.shape, F32)
    d_bfly, d_v = call(
        functools.partial(own_grad_kernel, sections),
        per_dev,
        x_specs + [low_spec, wide_spec],
        [tile_spec, lr_v_spec],
        [tile_shape, v_shape],
        (unit * (depth + rank), 15 * 2**20),
        name="own_grad",
    )(*partners, low, d_pre)
    for d in others:
        last = scale if d == data_groups - 1 else 1.0
        d_bfly, d_v = call(
            functools.partial(other_grad_kernel, sections, last),
            per_dev,
            x_specs + [bfly_spec, low_spec, lr_v_spec, wide_spec, tile_spec, lr_v_spec],
            [tile_spec, lr_v_spec],
            [tile_shape, v_shape],
            (unit * 2 * (depth + rank), 30 * 2**20),
            aliases={sections + 4: 0, sections + 5: 1},
            name="other_grad",
        )(*partners_others[d - 1], bfly, low_others[d - 1], lr_v, cot_others[d - 1], d_bfly, d_v)
    if data_groups == 1:
        d_bfly, d_v = d_bfly * scale, d_v * scale

    d_inputs = nt(d_low, lr_u)
    for term in terms:
        d_inputs = d_inputs + term.astype(F32)
    d_u = tn(inputs, d_low)
    for d in others:
        d_u = d_u + tn(x_others[d - 1], d_low_others[d - 1])
    return activated, d_inputs.astype(BF), d_bfly, d_u * scale, d_v


def solution(mesh):
    return jax.shard_map(
        local,
        mesh=mesh,
        in_specs=(
            P("dp", "feat"),
            P("feat", None, None, None),
            P("feat", None),
            P(None, "feat"),
            P("dp", "feat"),
        ),
        out_specs=(
            P("dp", "feat"),
            P("dp", "feat"),
            P("feat", None, None, None),
            P("feat", None),
            P(None, "feat"),
        ),
        check_vma=False,
    )
```

time: 476 us -> 181 us (0.38)
  blocking collectives: 127 us -> 0 us
  waiting for transfers between devices: 205 us -> 105 us
  matrix products: 71.3 us -> 4.26 us
  Pallas kernels: 0 us -> 29.7 us
  local copies, waits for them, and re-layouts: 38 us -> 8.43 us
  starting transfers between devices: 8.7 us -> 32.1 us
  between operations: 14.3 us -> 0.91 us
  other arithmetic: 10.5 us -> 1.08 us
    psum x1 -> x0, waiting for transfers between devices: 189 us -> none  [local(): d_bfly, d_u, d_v = lax.psum((d_bfly, d_u, d_v), 'dp')]
    psum x2 -> x0, blocking collectives: 127 us -> none  [the longest x1 63.6 us: local(): lax.psum(jnp.dot(d_pre, lr_v.T, preferred_element_type=jnp.float32), 'feat')]
    ppermute x8 -> x32, waiting for transfers between devices: 16.2 us -> 105 us  [the longest x28 58.9 us: crossed(): return lax.ppermute(block, axis, [(i, i ^ mask) for i in range(count)])]
    dot_general x27 -> x4, matrix products: 71.3 us -> 4.26 us  [the longest x1 1.49 us: nt(): lax.dot_general(a, b, (((1,), (1,)), ((), ())), preferred_element_type=F32)]
    pallas_call x0 -> x3, Pallas kernels: none -> 29.7 us  [the longest x1 12.5 us: local(): call(functools.partial(other_grad_kernel, sections, last), per_dev, x_spe...]
    ppermute x8 -> x32, starting transfers between devices: 8.67 us -> 32.1 us  [the longest x28 27 us: crossed(): return lax.ppermute(block, axis, [(i, i ^ mask) for i in range(count)])]
    rev x6 -> x0, local copies, waits for them, and re-layouts: 11.7 us -> none  [flip_blocks(): return split[:, :, ::-1].reshape(array.shape)]
    reshape x4 -> x0, local copies, waits for them, and re-layouts: 9.81 us -> none  [the longest x1 5.62 us: local(): butterfly.reshape(tokens, per_dev * group)]
  transfers between devices with their start and end apart: 9 -> 32, of which waited for: 3 -> 18; matrix products, arithmetic and copies ran while one was open for 12% -> 3% of each run, Pallas kernels for 0% -> 3%
where the time goes in v1:
time: 181 us
  waiting for transfers between devices  105 us (58%)
  starting transfers between devices  32.1 us (18%)
  Pallas kernels  29.7 us (16%)
  local copies, waits for them, and re-layouts  8.43 us (5%)
  matrix products  4.26 us (2%)
    ppermute x28, waiting for transfers between devices, crossed(): return lax.ppermute(block, axis, [(i, i ^ mask) for i in range(count)])  58.9 us
    ppermute x4, waiting for transfers between devices, rolled(): lax.ppermute(block, axis, [(i, (i + shift) % count) for i in range(count)])  45.8 us
    ppermute x28, starting transfers between devices, crossed(): return lax.ppermute(block, axis, [(i, i ^ mask) for i in range(count)])  27 us
    pallas_call x1, Pallas kernels, local(): call(functools.partial(other_grad_kernel, sections, last), per_dev, x_spe...  12.5 us
    pallas_call x1, Pallas kernels, local(): call(functools.partial(forward_kernel, sections), per_dev, x_specs + [bfl...  11.6 us
    unnamed x27, local copies, waits for them, and re-layouts  8.35 us
    pallas_call x1, Pallas kernels, local(): call(functools.partial(own_grad_kernel, sections), per_dev, x_specs + [lo...  5.57 us
    ppermute x4, starting transfers between devices, rolled(): lax.ppermute(block, axis, [(i, (i + shift) % count) for i in range(count)])  5.07 us
  transfers between devices with their start and end apart: 32, of which 18 were waited for; matrix products, arithmetic and copies ran while one was open for 3% of the time, Pallas kernels for 3%

profile of v1, /device:TPU:0, one launch (start us, length us, event | category | flops | bytes accessed | tf_op | source)
XLA Modules:
  0.0 181.1 jit_solution(14725219057566412046)
XLA Ops:
  1.6 1.3 fusion.18
  4.5 2.9 %collective-permute-start.5 = (bf16[128,256]{1,0:T(8,128)(2,1)S(1)}, bf16[128,256]{1,0:T(8,128)(2,1)S(1)}, u32[]{:S(2)}, u32[]{:S(2)}) collective-permute-start(bf16[128,256]{1,0:T(8,128)(2,1)S(1)} %dynamic-slice_convert_fusion.3), channel_id=1, source_target_pairs={{0,2},{1,3},{2,0},{3,1},{4,6},{5,7},{6,4},{7,5},{8,10},{9,11},{10,... | collective-permute-start | bytes 196616 | tf_op jit(solution)/shard_map/ppermute | solution.py:20
  7.5 2.4 %collective-permute-done.5 = bf16[128,256]{1,0:T(8,128)(2,1)S(1)} collective-permute-done((bf16[128,256]{1,0:T(8,128)(2,1)S(1)}, bf16[128,256]{1,0:T(8,128)(2,1)S(1)}, u32[]{:S(2)}, u32[]{:S(2)}) %collective-permute-start.5) | collective-permute-done | bytes 65568 | tf_op jit(solution)/shard_map/ppermute | solution.py:20
  9.9 4.0 %collective-permute-start.8 = (bf16[128,256]{1,0:T(8,128)(2,1)S(1)}, bf16[128,256]{1,0:T(8,128)(2,1)S(1)}, u32[]{:S(2)}, u32[]{:S(2)}) collective-permute-start(bf16[128,256]{1,0:T(8,128)(2,1)S(1)} %fusion.13), channel_id=1, source_target_pairs={{0,12},{1,13},{2,14},{3,15},{4,8},{5,9},{6,10},{7,11},{8,4},{9,5},... | collective-permute-start | bytes 196616 | tf_op jit(solution)/shard_map/ppermute | solution.py:20
  14.5 2.1 %collective-permute-done.8 = bf16[128,256]{1,0:T(8,128)(2,1)S(1)} collective-permute-done((bf16[128,256]{1,0:T(8,128)(2,1)S(1)}, bf16[128,256]{1,0:T(8,128)(2,1)S(1)}, u32[]{:S(2)}, u32[]{:S(2)}) %collective-permute-start.8) | collective-permute-done | bytes 65568 | tf_op jit(solution)/shard_map/ppermute | solution.py:20
  16.6 2.6 %collective-permute-done.7 = bf16[128,256]{1,0:T(8,128)(2,1)S(1)} collective-permute-done((bf16[128,256]{1,0:T(8,128)(2,1)S(1)}, bf16[128,256]{1,0:T(8,128)(2,1)S(1)}, u32[]{:S(2)}, u32[]{:S(2)}) %collective-permute-start.7) | collective-permute-done | bytes 65568 | tf_op jit(solution)/shard_map/ppermute | solution.py:20
  19.3 1.6 collective-permute-start.9
  21.9 2.3 %collective-permute-start.3 = (bf16[512,512]{1,0:T(8,128)(2,1)S(1)}, bf16[512,512]{1,0:T(8,128)(2,1)S(1)}, u32[]{:S(2)}, u32[]{:S(2)}) collective-permute-start(bf16[512,512]{1,0:T(8,128)(2,1)S(1)} %copy-done.1), channel_id=1, source_target_pairs={{0,8},{1,9},{2,10},{3,11},{4,12},{5,13},{6,14},{7,15},{8,0},{9,1},... | collective-permute-start | bytes 1572872 | tf_op jit(solution)/shard_map/ppermute | solution.py:20
  25.8 9.4 %collective-permute-done.1.refs_3_ = bf16[512,512]{1,0:T(8,128)(2,1)S(1)} collective-permute-done((bf16[512,512]{1,0:T(8,128)(2,1)S(1)}, bf16[512,512]{1,0:T(8,128)(2,1)S(1)}, u32[]{:S(2)}, u32[]{:S(2)}) %collective-permute-start.1) | collective-permute-done | bytes 524320 | tf_op jit(solution)/shard_map/ppermute | solution.py:20
  35.2 11.5 %collective-permute-done.2.refs_4_ = bf16[512,512]{1,0:T(8,128)(2,1)S(1)} collective-permute-done((bf16[512,512]{1,0:T(8,128)(2,1)S(1)}, bf16[512,512]{1,0:T(8,128)(2,1)S(1)}, u32[]{:S(2)}, u32[]{:S(2)}) %collective-permute-start.2) | collective-permute-done | bytes 524320 | tf_op jit(solution)/shard_map/ppermute | solution.py:20
  48.3 11.6 %forward.1 = (bf16[512,2048]{1,0:T(8,128)(2,1)}, bf16[512,2048]{1,0:T(8,128)(2,1)}, f32[512,256]{1,0:T(8,128)S(1)}, bf16[512,512]{1,0:T(8,128)(2,1)S(1)}, bf16[5...) custom-call(bf16[512,512]{1,0:T(8,128)(2,1)S(1)} %copy-done.1, ...), custom_call_target="tpu_custom_call" | custom-call | flops 4831838208 | bytes 20971520 | tf_op jit(solution)/shard_map/forward/pallas_call | solution.py:189
  60.1 1.3 collective-permute-done.11
  61.5 1.6 collective-permute-start.12
  63.1 2.7 %collective-permute-done.12 = bf16[128,256]{1,0:T(8,128)(2,1)S(1)} collective-permute-done((bf16[128,256]{1,0:T(8,128)(2,1)S(1)}, bf16[128,256]{1,0:T(8,128)(2,1)S(1)}, u32[]{:S(2)}, u32[]{:S(2)}) %collective-permute-start.12) | collective-permute-done | bytes 65568 | tf_op jit(solution)/shard_map/ppermute | solution.py:20
  65.8 3.2 %collective-permute-start.15 = (bf16[128,256]{1,0:T(8,128)(2,1)S(1)}, bf16[128,256]{1,0:T(8,128)(2,1)S(1)}, u32[]{:S(2)}, u32[]{:S(2)}) collective-permute-start(bf16[128,256]{1,0:T(8,128)(2,1)S(1)} %fusion.14), channel_id=1, source_target_pairs={{0,12},{1,13},{2,14},{3,15},{4,8},{5,9},{6,10},{7,11},{8,4},{9,5},... | collective-permute-start | bytes 196616 | tf_op jit(solution)/shard_map/ppermute | solution.py:20
  70.3 1.5 collective-permute-start.27
  72.1 2.2 %collective-permute-done.14 = bf16[128,256]{1,0:T(8,128)(2,1)S(1)} collective-permute-done((bf16[128,256]{1,0:T(8,128)(2,1)S(1)}, bf16[128,256]{1,0:T(8,128)(2,1)S(1)}, u32[]{:S(2)}, u32[]{:S(2)}) %collective-permute-start.14) | collective-permute-done | bytes 65568 | tf_op jit(solution)/shard_map/ppermute | solution.py:20
  74.8 1.6 collective-permute-start.16
  76.3 1.5 collective-permute-start.22
  79.2 1.5 collective-permute-start.30
  80.8 1.6 copy-done.12
  82.4 5.6 %own_grad.1 = (f32[4,7,128,512]{3,2,1,0:T(8,128)}, f32[256,2048]{1,0:T(8,128)}) custom-call(bf16[512,512]{1,0:T(8,128)(2,1)S(1)} %copy-done.1, bf16[512,512]{1,0:T(8,128)(2,1)S(1)} %copy-done.1, bf16[512,512]{1,0:T(8,128)(2,1)S(1)} %copy-done.5, bf16[512,512]{1,0:T(8,128)(2,1)S(1)} %copy-done.7, bf16[512,512]{1,0:T(8,128)(2,1)S(1)} %copy-done.9, ...), custom_call_target="tpu_custom_call" | custom-call | flops 2415919104 | bytes 15728640 | tf_op jit(solution)/shard_map/own_grad/pallas_call | solution.py:210
  87.9 3.3 %collective-permute-done.22.refs_0_.refs_1_.refs_6_ = bf16[512,512]{1,0:T(8,128)(2,1)S(1)} collective-permute-done((bf16[512,512]{1,0:T(8,128)(2,1)S(1)}, bf16[512,512]{1,0:T(8,128)(2,1)S(1)}, u32[]{:S(2)}, u32[]{:S(2)}) %collective-permute-start.22) | collective-permute-done | bytes 524320 | tf_op jit(solution)/shard_map/ppermute | solution.py:25
  91.2 1.6 collective-permute-start.21
  93.9 42.5 %collective-permute-done.30 = bf16[256,256]{1,0:T(8,128)(2,1)S(1)} collective-permute-done((bf16[256,256]{1,0:T(8,128)(2,1)S(1)}, bf16[256,256]{1,0:T(8,128)(2,1)S(1)}, u32[]{:S(2)}, u32[]{:S(2)}) %collective-permute-start.30) | collective-permute-done | bytes 131104 | tf_op jit(solution)/shard_map/ppermute | solution.py:25
  138.4 1.5 fusion.6
  139.9 2.2 %collective-permute-start.26 = (bf16[512,512]{1,0:T(8,128)(2,1)S(1)}, bf16[512,512]{1,0:T(8,128)(2,1)}, u32[]{:S(2)}, u32[]{:S(2)}) collective-permute-start(bf16[512,512]{1,0:T(8,128)(2,1)S(1)} %collective-permute-done.22.refs_0_.refs_1_.refs_6_), channel_id=1, source_target_pairs={{0,8},{1,9},{2,10},{3,11},{4,12},{5,13},{6,14},{7,15},{8,0},{9,1},... | collective-permute-start | bytes 1572872 | tf_op jit(solution)/shard_map/ppermute | solution.py:20
  143.6 2.0 %copy.12 = f32[512,256]{1,0:T(8,128)} copy(f32[512,256]{0,1:T(8,128)} %fusion.8) | data formatting | bytes 1048576
  145.7 6.1 %collective-permute-done.24.refs_3_ = bf16[512,512]{1,0:T(8,128)(2,1)} collective-permute-done((bf16[512,512]{1,0:T(8,128)(2,1)S(1)}, bf16[512,512]{1,0:T(8,128)(2,1)}, u32[]{:S(2)}, u32[]{:S(2)}) %collective-permute-start.24) | collective-permute-done | bytes 524320 | tf_op jit(solution)/shard_map/ppermute | solution.py:20
  151.8 8.4 %collective-permute-done.25.refs_4_ = bf16[512,512]{1,0:T(8,128)(2,1)} collective-permute-done((bf16[512,512]{1,0:T(8,128)(2,1)S(1)}, bf16[512,512]{1,0:T(8,128)(2,1)}, u32[]{:S(2)}, u32[]{:S(2)}) %collective-permute-start.25) | collective-permute-done | bytes 524320 | tf_op jit(solution)/shard_map/ppermute | solution.py:20
  160.2 6.2 %collective-permute-done.26.refs_5_ = bf16[512,512]{1,0:T(8,128)(2,1)} collective-permute-done((bf16[512,512]{1,0:T(8,128)(2,1)S(1)}, bf16[512,512]{1,0:T(8,128)(2,1)}, u32[]{:S(2)}, u32[]{:S(2)}) %collective-permute-start.26) | collective-permute-done | bytes 524320 | tf_op jit(solution)/shard_map/ppermute | solution.py:20
  168.6 12.5 %other_grad.1 = (f32[4,7,128,512]{3,2,1,0:T(8,128)}, f32[256,2048]{1,0:T(8,128)}) custom-call(bf16[512,512]{1,0:T(8,128)(2,1)S(1)} %collective-permute-done.22.refs_0_.refs_1_.refs_6_, bf16[512,512]{1,0:T(8,128)(2,1)S(1)} %collective-permute-done.22.refs_0_.refs_1_.refs_6_, ...), custom_call_target="tpu_custom_call", output_to_operand_aliasing={{0}: (11, {}), {1}: (12, {})} | custom-call | flops 4831838208 | bytes 31457280 | tf_op jit(solution)/shard_map/other_grad/pallas_call | solution.py:221
  (86 shorter events, 17.6 us)
Async XLA Ops:
  3.0 1.5 collective-permute-start.4
  4.5 5.3 %collective-permute-start.5 = (bf16[128,256]{1,0:T(8,128)(2,1)S(1)}, bf16[128,256]{1,0:T(8,128)(2,1)S(1)}, u32[]{:S(2)}, u32[]{:S(2)}) collective-permute-start(bf16[128,256]{1,0:T(8,128)(2,1)S(1)} %dynamic-slice_convert_fusion.3), channel_id=1, source_target_pairs={{0,2},{1,3},{2,0},{3,1},{4,6},{5,7},{6,4},{7,5},{8,10},{9,11},{10,... | collective-permute-start | bytes 196616 | tf_op jit(solution)/shard_map/ppermute | solution.py:20
  9.9 6.7 %collective-permute-start.8 = (bf16[128,256]{1,0:T(8,128)(2,1)S(1)}, bf16[128,256]{1,0:T(8,128)(2,1)S(1)}, u32[]{:S(2)}, u32[]{:S(2)}) collective-permute-start(bf16[128,256]{1,0:T(8,128)(2,1)S(1)} %fusion.13), channel_id=1, source_target_pairs={{0,12},{1,13},{2,14},{3,15},{4,8},{5,9},{6,10},{7,11},{8,4},{9,5},... | collective-permute-start | bytes 196616 | tf_op jit(solution)/shard_map/ppermute | solution.py:20
  13.9 5.4 %collective-permute-start.7 = (bf16[128,256]{1,0:T(8,128)(2,1)S(1)}, bf16[128,256]{1,0:T(8,128)(2,1)S(1)}, u32[]{:S(2)}, u32[]{:S(2)}) collective-permute-start(bf16[128,256]{1,0:T(8,128)(2,1)S(1)} %fusion.13), channel_id=1, source_target_pairs={{0,8},{1,9},{2,10},{3,11},{4,12},{5,13},{6,14},{7,15},{8,0},{9,1},... | collective-permute-start | bytes 196616 | tf_op jit(solution)/shard_map/ppermute | solution.py:20
  13.9 5.4 %collective-permute-start.6 = (bf16[128,256]{1,0:T(8,128)(2,1)S(1)}, bf16[128,256]{1,0:T(8,128)(2,1)S(1)}, u32[]{:S(2)}, u32[]{:S(2)}) collective-permute-start(bf16[128,256]{1,0:T(8,128)(2,1)S(1)} %fusion.13), channel_id=1, source_target_pairs={{0,4},{1,5},{2,6},{3,7},{4,0},{5,1},{6,2},{7,3},{8,12},{9,13},{10,... | collective-permute-start | bytes 196616 | tf_op jit(solution)/shard_map/ppermute | solution.py:20
  19.3 5.0 %collective-permute-start.9 = (bf16[128,256]{1,0:T(8,128)(2,1)S(1)}, bf16[128,256]{1,0:T(8,128)(2,1)S(1)}, u32[]{:S(2)}, u32[]{:S(2)}) collective-permute-start(bf16[128,256]{1,0:T(8,128)(2,1)S(1)} %add_convert_fusion.1), channel_id=1, source_target_pairs={{0,2},{1,3},{2,0},{3,1},{4,6},{5,7},{6,4},{7,5},{8,10},{9,11},{10,... | collective-permute-start | bytes 196616 | tf_op jit(solution)/shard_map/ppermute | solution.py:20
  20.9 4.9 %collective-permute-start = (bf16[512,512]{1,0:T(8,128)(2,1)S(1)}, bf16[512,512]{1,0:T(8,128)(2,1)S(1)}, u32[]{:S(2)}, u32[]{:S(2)}) collective-permute-start(bf16[512,512]{1,0:T(8,128)(2,1)S(1)} %copy-done.1), channel_id=1, source_target_pairs={{0,1},{1,0},{2,3},{3,2},{4,5},{5,4},{6,7},{7,6},{8,9},{9,8},{10,11... | collective-permute-start | bytes 1572872 | tf_op jit(solution)/shard_map/ppermute | solution.py:20
  20.9 14.3 %collective-permute-start.1 = (bf16[512,512]{1,0:T(8,128)(2,1)S(1)}, bf16[512,512]{1,0:T(8,128)(2,1)S(1)}, u32[]{:S(2)}, u32[]{:S(2)}) collective-permute-start(bf16[512,512]{1,0:T(8,128)(2,1)S(1)} %copy-done.1), channel_id=1, source_target_pairs={{0,2},{1,3},{2,0},{3,1},{4,6},{5,7},{6,4},{7,5},{8,10},{9,11},{10,... | collective-permute-start | bytes 1572872 | tf_op jit(solution)/shard_map/ppermute | solution.py:20
  21.4 25.3 %collective-permute-start.2 = (bf16[512,512]{1,0:T(8,128)(2,1)S(1)}, bf16[512,512]{1,0:T(8,128)(2,1)S(1)}, u32[]{:S(2)}, u32[]{:S(2)}) collective-permute-start(bf16[512,512]{1,0:T(8,128)(2,1)S(1)} %copy-done.1), channel_id=1, source_target_pairs={{0,4},{1,5},{2,6},{3,7},{4,0},{5,1},{6,2},{7,3},{8,12},{9,13},{10,... | collective-permute-start | bytes 1572872 | tf_op jit(solution)/shard_map/ppermute | solution.py:20
  21.9 24.8 %collective-permute-start.3 = (bf16[512,512]{1,0:T(8,128)(2,1)S(1)}, bf16[512,512]{1,0:T(8,128)(2,1)S(1)}, u32[]{:S(2)}, u32[]{:S(2)}) collective-permute-start(bf16[512,512]{1,0:T(8,128)(2,1)S(1)} %copy-done.1), channel_id=1, source_target_pairs={{0,8},{1,9},{2,10},{3,11},{4,12},{5,13},{6,14},{7,15},{8,0},{9,1},... | collective-permute-start | bytes 1572872 | tf_op jit(solution)/shard_map/ppermute | solution.py:20
  24.3 1.4 collective-permute-start.10
  60.0 1.4 collective-permute-start.11
  61.5 4.3 %collective-permute-start.12 = (bf16[128,256]{1,0:T(8,128)(2,1)S(1)}, bf16[128,256]{1,0:T(8,128)(2,1)S(1)}, u32[]{:S(2)}, u32[]{:S(2)}) collective-permute-start(bf16[128,256]{1,0:T(8,128)(2,1)S(1)} %dynamic-slice_convert_fusion.2), channel_id=1, source_target_pairs={{0,2},{1,3},{2,0},{3,1},{4,6},{5,7},{6,4},{7,5},{8,10},{9,11},{10,... | collective-permute-start | bytes 196616 | tf_op jit(solution)/shard_map/ppermute | solution.py:20
  65.8 6.2 %collective-permute-start.15 = (bf16[128,256]{1,0:T(8,128)(2,1)S(1)}, bf16[128,256]{1,0:T(8,128)(2,1)S(1)}, u32[]{:S(2)}, u32[]{:S(2)}) collective-permute-start(bf16[128,256]{1,0:T(8,128)(2,1)S(1)} %fusion.14), channel_id=1, source_target_pairs={{0,12},{1,13},{2,14},{3,15},{4,8},{5,9},{6,10},{7,11},{8,4},{9,5},... | collective-permute-start | bytes 196616 | tf_op jit(solution)/shard_map/ppermute | solution.py:20
  69.1 5.2 %collective-permute-start.14 = (bf16[128,256]{1,0:T(8,128)(2,1)S(1)}, bf16[128,256]{1,0:T(8,128)(2,1)S(1)}, u32[]{:S(2)}, u32[]{:S(2)}) collective-permute-start(bf16[128,256]{1,0:T(8,128)(2,1)S(1)} %fusion.14), channel_id=1, source_target_pairs={{0,8},{1,9},{2,10},{3,11},{4,12},{5,13},{6,14},{7,15},{8,0},{9,1},... | collective-permute-start | bytes 196616 | tf_op jit(solution)/shard_map/ppermute | solution.py:20
  69.1 5.6 %collective-permute-start.13 = (bf16[128,256]{1,0:T(8,128)(2,1)S(1)}, bf16[128,256]{1,0:T(8,128)(2,1)S(1)}, u32[]{:S(2)}, u32[]{:S(2)}) collective-permute-start(bf16[128,256]{1,0:T(8,128)(2,1)S(1)} %fusion.14), channel_id=1, source_target_pairs={{0,4},{1,5},{2,6},{3,7},{4,0},{5,1},{6,2},{7,3},{8,12},{9,13},{10,... | collective-permute-start | bytes 196616 | tf_op jit(solution)/shard_map/ppermute | solution.py:20
  70.3 8.1 %collective-permute-start.27 = (bf16[256,256]{1,0:T(8,128)(2,1)S(1)}, bf16[256,256]{1,0:T(8,128)(2,1)S(1)}, u32[]{:S(2)}, u32[]{:S(2)}) collective-permute-start(bf16[256,256]{1,0:T(8,128)(2,1)S(1)} %pad_maximum_fusion.5), channel_id=1, source_target_pairs={{0,16},{16,0},{1,17},{17,1},{2,18},{18,2},{3,19},{19,3},{4,20},{20... | collective-permute-start | bytes 393224 | tf_op jit(solution)/shard_map/ppermute | solution.py:25
  74.8 4.3 %collective-permute-start.16 = (bf16[128,256]{1,0:T(8,128)(2,1)S(1)}, bf16[128,256]{1,0:T(8,128)(2,1)S(1)}, u32[]{:S(2)}, u32[]{:S(2)}) collective-permute-start(bf16[128,256]{1,0:T(8,128)(2,1)S(1)} %add_convert_fusion), channel_id=1, source_target_pairs={{0,2},{1,3},{2,0},{3,1},{4,6},{5,7},{6,4},{7,5},{8,10},{9,11},{10,... | collective-permute-start | bytes 196616 | tf_op jit(solution)/shard_map/ppermute | solution.py:20
  76.3 14.9 %collective-permute-start.22 = (bf16[512,512]{1,0:T(8,128)(2,1)S(1)}, bf16[512,512]{1,0:T(8,128)(2,1)S(1)}, u32[]{:S(2)}, u32[]{:S(2)}) collective-permute-start(bf16[512,512]{1,0:T(8,128)(2,1)S(1)} %copy-done.1), channel_id=1, source_target_pairs={{0,16},{16,0},{1,17},{17,1},{2,18},{18,2},{3,19},{19,3},{4,20},{20... | collective-permute-start | bytes 1572872 | tf_op jit(solution)/shard_map/ppermute | solution.py:25
  77.8 88.6 %collective-permute-start.29 = (bf16[512,2048]{1,0:T(8,128)(2,1)}, bf16[512,2048]{1,0:T(8,128)(2,1)S(1)}, u32[]{:S(2)}, u32[]{:S(2)}) collective-permute-start(bf16[512,2048]{1,0:T(8,128)(2,1)} %refs_10_.1), channel_id=1, source_target_pairs={{0,16},{16,0},{1,17},{17,1},{2,18},{18,2},{3,19},{19,3},{4,20},{20... | collective-permute-start | bytes 6291464 | tf_op jit(solution)/shard_map/ppermute | solution.py:25
  78.4 14.4 %collective-permute-start.28 = (bf16[256,256]{1,0:T(8,128)(2,1)S(1)}, bf16[256,256]{1,0:T(8,128)(2,1)S(1)}, u32[]{:S(2)}, u32[]{:S(2)}) collective-permute-start(bf16[256,256]{1,0:T(8,128)(2,1)S(1)} %collective-permute-done.27), channel_id=1, source_target_pairs={{0,1},{1,0},{2,3},{3,2},{4,5},{5,4},{6,7},{7,6},{8,9},{9,8},{10,11... | collective-permute-start | bytes 393224 | tf_op jit(solution)/shard_map/ppermute | solution.py:20
  79.1 14.2 %collective-permute-start.17 = (bf16[256,256]{1,0:T(8,128)(2,1)S(1)}, bf16[256,256]{1,0:T(8,128)(2,1)S(1)}, u32[]{:S(2)}, u32[]{:S(2)}) collective-permute-start(bf16[256,256]{1,0:T(8,128)(2,1)S(1)} %pad_maximum_fusion.6), channel_id=1, source_target_pairs={{0,1},{1,0},{2,3},{3,2},{4,5},{5,4},{6,7},{7,6},{8,9},{9,8},{10,11... | collective-permute-start | bytes 393224 | tf_op jit(solution)/shard_map/ppermute | solution.py:20
  79.2 57.2 %collective-permute-start.30 = (bf16[256,256]{1,0:T(8,128)(2,1)S(1)}, bf16[256,256]{1,0:T(8,128)(2,1)S(1)}, u32[]{:S(2)}, u32[]{:S(2)}) collective-permute-start(bf16[256,256]{1,0:T(8,128)(2,1)S(1)} %pad_maximum_fusion.6), channel_id=1, source_target_pairs={{0,16},{16,0},{1,17},{17,1},{2,18},{18,2},{3,19},{19,3},{4,20},{20... | collective-permute-start | bytes 393224 | tf_op jit(solution)/shard_map/ppermute | solution.py:25
  91.2 46.0 %collective-permute-start.21 = (bf16[512,512]{1,0:T(8,128)(2,1)S(1)}, bf16[512,512]{1,0:T(8,128)(2,1)S(1)}, u32[]{:S(2)}, u32[]{:S(2)}) collective-permute-start(bf16[512,512]{1,0:T(8,128)(2,1)S(1)} %get-tuple-element.26), channel_id=1, source_target_pairs={{0,8},{1,9},{2,10},{3,11},{4,12},{5,13},{6,14},{7,15},{8,0},{9,1},... | collective-permute-start | bytes 1572872 | tf_op jit(solution)/shard_map/ppermute | solution.py:20
  92.7 45.0 %collective-permute-start.20 = (bf16[512,512]{1,0:T(8,128)(2,1)S(1)}, bf16[512,512]{1,0:T(8,128)(2,1)S(1)}, u32[]{:S(2)}, u32[]{:S(2)}) collective-permute-start(bf16[512,512]{1,0:T(8,128)(2,1)S(1)} %get-tuple-element.25), channel_id=1, source_target_pairs={{0,4},{1,5},{2,6},{3,7},{4,0},{5,1},{6,2},{7,3},{8,12},{9,13},{10,... | collective-permute-start | bytes 1572872 | tf_op jit(solution)/shard_map/ppermute | solution.py:20
  93.4 44.9 %collective-permute-start.19 = (bf16[512,512]{1,0:T(8,128)(2,1)S(1)}, bf16[512,512]{1,0:T(8,128)(2,1)S(1)}, u32[]{:S(2)}, u32[]{:S(2)}) collective-permute-start(bf16[512,512]{1,0:T(8,128)(2,1)S(1)} %get-tuple-element.24), channel_id=1, source_target_pairs={{0,2},{1,3},{2,0},{3,1},{4,6},{5,7},{6,4},{7,5},{8,10},{9,11},{10,... | collective-permute-start | bytes 1572872 | tf_op jit(solution)/shard_map/ppermute | solution.py:20
  136.4 1.9 %collective-permute-start.18 = (bf16[512,512]{1,0:T(8,128)(2,1)S(1)}, bf16[512,512]{1,0:T(8,128)(2,1)S(1)}, u32[]{:S(2)}, u32[]{:S(2)}) collective-permute-start(bf16[512,512]{1,0:T(8,128)(2,1)S(1)} %get-tuple-element.23), channel_id=1, source_target_pairs={{0,1},{1,0},{2,3},{3,2},{4,5},{5,4},{6,7},{7,6},{8,9},{9,8},{10,11... | collective-permute-start | bytes 1572872 | tf_op jit(solution)/shard_map/ppermute | solution.py:20
  137.2 8.5 %collective-permute-start.23 = (bf16[512,512]{1,0:T(8,128)(2,1)S(1)}, bf16[512,512]{1,0:T(8,128)(2,1)}, u32[]{:S(2)}, u32[]{:S(2)}) collective-permute-start(bf16[512,512]{1,0:T(8,128)(2,1)S(1)} %collective-permute-done.22.refs_0_.refs_1_.refs_6_), channel_id=1, source_target_pairs={{0,1},{1,0},{2,3},{3,2},{4,5},{5,4},{6,7},{7,6},{8,9},{9,8},{10,11... | collective-permute-start | bytes 1572872 | tf_op jit(solution)/shard_map/ppermute | solution.py:20
  137.7 14.0 %collective-permute-start.24 = (bf16[512,512]{1,0:T(8,128)(2,1)S(1)}, bf16[512,512]{1,0:T(8,128)(2,1)}, u32[]{:S(2)}, u32[]{:S(2)}) collective-permute-start(bf16[512,512]{1,0:T(8,128)(2,1)S(1)} %collective-permute-done.22.refs_0_.refs_1_.refs_6_), channel_id=1, source_target_pairs={{0,2},{1,3},{2,0},{3,1},{4,6},{5,7},{6,4},{7,5},{8,10},{9,11},{10,... | collective-permute-start | bytes 1572872 | tf_op jit(solution)/shard_map/ppermute | solution.py:20
  138.2 22.0 %collective-permute-start.25 = (bf16[512,512]{1,0:T(8,128)(2,1)S(1)}, bf16[512,512]{1,0:T(8,128)(2,1)}, u32[]{:S(2)}, u32[]{:S(2)}) collective-permute-start(bf16[512,512]{1,0:T(8,128)(2,1)S(1)} %collective-permute-done.22.refs_0_.refs_1_.refs_6_), channel_id=1, source_target_pairs={{0,4},{1,5},{2,6},{3,7},{4,0},{5,1},{6,2},{7,3},{8,12},{9,13},{10,... | collective-permute-start | bytes 1572872 | tf_op jit(solution)/shard_map/ppermute | solution.py:20
  138.3 1.6 collective-permute-start.31
  139.9 26.5 %collective-permute-start.26 = (bf16[512,512]{1,0:T(8,128)(2,1)S(1)}, bf16[512,512]{1,0:T(8,128)(2,1)}, u32[]{:S(2)}, u32[]{:S(2)}) collective-permute-start(bf16[512,512]{1,0:T(8,128)(2,1)S(1)} %collective-permute-done.22.refs_0_.refs_1_.refs_6_), channel_id=1, source_target_pairs={{0,8},{1,9},{2,10},{3,11},{4,12},{5,13},{6,14},{7,15},{8,0},{9,1},... | collective-permute-start | bytes 1572872 | tf_op jit(solution)/shard_map/ppermute | solution.py:20
  (13 other events, 168.6 us)

commit v2 on v1

v2 whole, which is shorter than its diff:
```python
import functools

import jax
import jax.numpy as jnp
import numpy as np
from jax import lax
from jax.experimental import pallas as pl
from jax.experimental.pallas import tpu as pltpu
from jax.sharding import PartitionSpec as P

BF = jnp.bfloat16
F32 = jnp.float32
VMEM_LIMIT = 24 * 1024 * 1024
GELU_C = float(np.sqrt(2.0 / np.pi))
GELU_A = 0.044715


def crossed(block, axis, mask):
    count = lax.axis_size(axis)
    return lax.ppermute(block, axis, [(i, i ^ mask) for i in range(count)])


def rolled(block, axis, shift):
    count = lax.axis_size(axis)
    return lax.ppermute(block, axis, [(i, (i + shift) % count) for i in range(count)])


def scatter_half(part, bit, axis):
    rows = part.shape[0] // 2
    mine = (lax.axis_index(axis) >> bit) & 1
    keep = lax.dynamic_slice_in_dim(part, mine * rows, rows, 0)
    send = lax.dynamic_slice_in_dim(part, (1 - mine) * rows, rows, 0)
    return keep + crossed(send.astype(BF), axis, 1 << bit).astype(F32)


def gather_half(part, bit, axis):
    mine = (lax.axis_index(axis) >> bit) & 1
    other = crossed(part, axis, 1 << bit)
    low = jnp.where(mine == 0, part, other)
    high = jnp.where(mine == 0, other, part)
    return jnp.concatenate([low, high], 0)


def tie(value, *others):
    return lax.optimization_barrier((value, *others))


def no_hooks(step, value):
    return value


def reduce_feat(part, axis, hooks):
    bits = lax.axis_size(axis).bit_length() - 1
    near = min(bits, 2)
    for bit in range(near):
        part = hooks(f"scatter{bit}", scatter_half(part, bit, axis))
    for bit in range(near, bits):
        got = hooks(f"got{bits - 1 - bit}", crossed(part.astype(BF), axis, 1 << bit))
        part = hooks(f"far{bits - 1 - bit}", part + got.astype(F32))
    return part.astype(BF)


def gather_feat(part, axis, hooks=no_hooks):
    near = min(lax.axis_size(axis).bit_length() - 1, 2)
    for bit in range(near - 1, -1, -1):
        part = hooks(f"gather{bit}", gather_half(part, bit, axis))
    return part


def gelu_parts(pre):
    square = pre * pre
    tanh = jnp.tanh(GELU_C * (pre + GELU_A * (square * pre)))
    half = 0.5 * (1.0 + tanh)
    slope = half + (0.5 * GELU_C) * pre * (1.0 - tanh * tanh) * (1.0 + (3.0 * GELU_A) * square)
    return pre * half, slope


def nt(a, b):
    return lax.dot_general(a, b, (((1,), (1,)), ((), ())), preferred_element_type=F32)


def tn(a, b):
    return lax.dot_general(a, b, (((0,), (0,)), ((), ())), preferred_element_type=F32)


def gathered(refs, pieces):
    refs = iter(refs)
    columns = []
    for count in pieces:
        rows = [next(refs)[...] for _ in range(count)]
        columns.append(rows[0] if count == 1 else jnp.concatenate(rows, axis=0))
    return columns[0] if len(columns) == 1 else jnp.concatenate(columns, axis=1)


def forward_kernel(pieces, *refs):
    sections, count = len(pieces), sum(pieces)
    x = refs[:count]
    bfly, low, lr_v, cot, act, d_pre, d_low = refs[count : count + 7]
    terms = refs[count + 7 :]
    width = bfly.shape[2]
    tiles = bfly[0].reshape(sections * width, bfly.shape[3])
    block = gathered(x, pieces)
    pre = jnp.dot(block, tiles, preferred_element_type=F32) + jnp.dot(
        low[...], lr_v[...], preferred_element_type=F32
    )
    value, slope = gelu_parts(pre)
    act[...] = value.astype(BF)
    grad = (cot[...].astype(F32) * slope).astype(BF)
    d_pre[...] = grad
    part = nt(grad, lr_v[...])

    @pl.when(pl.program_id(0) == 0)
    def _():
        d_low[...] = part

    @pl.when(pl.program_id(0) > 0)
    def _():
        d_low[...] += part

    back = nt(grad, tiles).astype(BF)
    for section in range(sections):
        terms[section][...] = back[:, section * width : (section + 1) * width]


def own_grad_kernel(pieces, *refs):
    count = sum(pieces)
    x = refs[:count]
    low, d_pre, d_bfly, d_v = refs[count:]
    block = gathered(x, pieces)
    d_bfly[0] = tn(block, d_pre[...]).reshape(d_bfly.shape[1:])
    d_v[...] = tn(low[...], d_pre[...])


def other_grad_kernel(pieces, scale, *refs):
    sections, count = len(pieces), sum(pieces)
    x = refs[:count]
    bfly, low, lr_v, cot, d_bfly_in, d_v_in, d_bfly, d_v = refs[count:]
    width = bfly.shape[2]
    tiles = bfly[0].reshape(sections * width, bfly.shape[3])
    block = gathered(x, pieces)
    pre = jnp.dot(block, tiles, preferred_element_type=F32) + jnp.dot(
        low[...], lr_v[...], preferred_element_type=F32
    )
    _, slope = gelu_parts(pre)
    grad = (cot[...].astype(F32) * slope).astype(BF)
    d_bfly[0] = (d_bfly_in[0] + tn(block, grad).reshape(d_bfly.shape[1:])) * scale
    d_v[...] = (d_v_in[...] + tn(low[...], grad)) * scale


def column(rows, width, flip, base=0):
    return pl.BlockSpec((rows, width), lambda g: (0, (g + base) ^ flip))


def row(rows, width, base=0):
    return pl.BlockSpec((rows, width), lambda g: (0, g + base))


def resident(*shape):
    return pl.BlockSpec(shape, lambda g: (0,) * len(shape))


def call(kernel, grid, in_specs, out_specs, out_shape, cost, aliases=None, name=None):
    return pl.pallas_call(
        kernel,
        grid=(grid,),
        in_specs=in_specs,
        out_specs=out_specs,
        out_shape=out_shape,
        input_output_aliases=aliases or {},
        cost_estimate=pl.CostEstimate(flops=cost[0], bytes_accessed=cost[1], transcendentals=0),
        compiler_params=pltpu.CompilerParams(vmem_limit_bytes=VMEM_LIMIT),
        name=name,
    )


def local(inputs, bfly, lr_u, lr_v, cotangent):
    tokens = inputs.shape[0]
    per_dev, sections, width, group = bfly.shape
    levels = sections - 1
    rank = lr_v.shape[0]
    local_bits = per_dev.bit_length() - 1
    data_groups = lax.axis_size("dp")
    scale = float(1.0 / np.sqrt(np.float32(tokens * data_groups)))
    remote = list(range(local_bits, levels))
    others = range(1, data_groups)

    flips = [(1 << s) if s < local_bits else 0 for s in range(sections)]

    def tile_spec(base=0):
        return pl.BlockSpec((1, sections, width, group), lambda g: (g + base, 0, 0, 0))

    low_spec = resident(tokens, rank)
    wide = jax.ShapeDtypeStruct((tokens, per_dev * group), BF)
    narrow = jax.ShapeDtypeStruct((tokens, per_dev * width), BF)
    tile_shape = jax.ShapeDtypeStruct(bfly.shape, F32)
    v_shape = jax.ShapeDtypeStruct(lr_v.shape, F32)

    def to_partner(block, section):
        return crossed(block, "feat", 1 << (section - local_bits))

    env = {}
    seen = set()

    def pin(value, *names):
        names = [n for n in names if n in env]
        if names:
            value, *rest = tie(value, *[env[n] for n in names])
            env.update(zip(names, rest))
        return value

    def each(prefix, *tails):
        return [f"{prefix}{d}{t}" for d in others for t in tails or ("",)]

    far = remote[-1:]
    near = remote[:-1]
    lead = 1
    parts = [(0, lead), (lead, per_dev)] if per_dev > lead else [(0, lead)]

    low_part = jnp.dot(inputs, lr_u, preferred_element_type=F32)
    for s in reversed(near[1:] + far):
        env[f"x{s}"] = to_partner(inputs, s)
    joined = jnp.concatenate([cotangent[:, : lead * group], inputs], axis=1)
    for d in others:
        env[f"in{d}"] = rolled(joined, "dp", d)

    def send_cot(value, index):
        first, last = parts[index]
        piece = tie(cotangent[:, first * group : last * group], value)[0]
        for d in others:
            env[f"cot{d}{index}"] = rolled(piece, "dp", d)

    def low_hooks(step, value):
        if step == "scatter1":
            value = pin(value, *[f"x{s}" for s in near[1:] + far])
        if step == "far0":
            value = pin(value, *each("in"))
        return value

    low = reduce_feat(low_part, "feat", low_hooks)
    for s in near[:1]:
        env[f"x{s}"] = to_partner(tie(inputs, low)[0], s)
    for d in others:
        env[f"low{d}"] = rolled(low, "dp", d)
    low = gather_feat(low, "feat")
    for d in others:
        env[f"cot{d}0"] = env[f"in{d}"]
        env[f"in{d}"] = env[f"in{d}"][:, lead * group :]
        for s in near:
            env[f"xo{d}{s}"] = to_partner(env[f"in{d}"], s)
        for s in far:
            env[f"xo{d}{s}"] = rolled(env[f"x{s}"], "dp", d)
    for index in range(1, len(parts)):
        send_cot(env["low1"] if others else low, index)
    low = pin(low, *[f"x{s}" for s in remote])

    def x_blocks(base_block, prefix, base):
        arrays = [env.get(f"{prefix}{s}", base_block) for s in range(sections)]
        return arrays, [column(tokens, width, flip, base) for flip in flips]

    arrays, specs = x_blocks(inputs, "x", 0)
    term_specs = [column(tokens, width, flip) for flip in flips]
    out = call(
        functools.partial(forward_kernel, [1] * sections),
        per_dev,
        specs + [tile_spec(), low_spec, row(rank, group), row(tokens, group)],
        [row(tokens, group), row(tokens, group), resident(tokens, rank)] + term_specs,
        [wide, wide, jax.ShapeDtypeStruct((tokens, rank), F32)] + [narrow] * sections,
        (1000, 1000),
        name="forward",
    )(*arrays, bfly, low, lr_v, cotangent)
    activated, d_pre, d_low_part = out[:3]
    terms = list(out[3:])
    for s in reversed(near[2:] + far):
        env[f"t{s}"] = to_partner(terms[s], s)
    grads = []

    def own_grad(gate):
        d_bfly, env["own"] = call(
            functools.partial(own_grad_kernel, [1] * sections),
            per_dev,
            specs + [low_spec, row(tokens, group)],
            [tile_spec(), row(rank, group)],
            [tile_shape, v_shape],
            (1000, 1000),
            name="own_grad",
        )(*arrays, low, tie(d_pre, gate)[0])
        grads.append(d_bfly)

    def add_other(d, index):
        base, end = parts[index]
        last = scale if d == data_groups - 1 else 1.0
        arrays, specs = x_blocks(env[f"in{d}"], f"xo{d}", base)
        count = len(arrays) + 4
        grads[0], env["own"] = call(
            functools.partial(other_grad_kernel, [1] * sections, last),
            end - base,
            specs
            + [tile_spec(base), low_spec, row(rank, group, base), row(tokens, group)]
            + [tile_spec(base), row(rank, group, base)],
            [tile_spec(base), row(rank, group, base)],
            [tile_shape, v_shape],
            (1000, 1000),
            aliases={count: 0, count + 1: 1},
            name="other_grad",
        )(*arrays, bfly, env[f"low{d}"], lr_v, env[f"cot{d}{index}"], grads[0], env["own"])

    def d_low_hooks(step, value):
        seen.add(step)
        if step == "scatter0":
            value = pin(value, *each("xo", *near))
            own_grad(value)
            for d in others:
                env[f"low{d}"] = gather_feat(tie(env[f"low{d}"], value)[0], "feat")
            value = pin(value, *each("cot", 1))
        if step == "scatter1":
            for s in near[1:2]:
                env[f"t{s}"] = to_partner(tie(terms[s], value)[0], s)
            for d in others:
                for index in range(len(parts)):
                    add_other(d, index)
            value = pin(value, "own", *[f"t{s}" for s in near[2:] + far])
        if step == "got0":
            value = pin(value, *[f"t{s}" for s in near[1:2]])
        return value

    d_low = reduce_feat(d_low_part, "feat", d_low_hooks)
    d_low_others = [gather_feat(rolled(d_low, "dp", d), "feat") for d in others]
    d_low = gather_feat(d_low, "feat", d_low_hooks)
    if not grads:
        own_grad(d_low)
    if "scatter1" not in seen:
        for d in others:
            for index in range(len(parts)):
                add_other(d, index)
    d_bfly, d_v = grads[0], env["own"]
    if data_groups == 1:
        d_bfly, d_v = d_bfly * scale, d_v * scale

    for s in near[:1]:
        env[f"t{s}"] = to_partner(terms[s], s)
    d_inputs = nt(d_low, lr_u)
    for s in range(sections):
        d_inputs = d_inputs + env.get(f"t{s}", terms[s]).astype(F32)
    d_u = tn(inputs, d_low)
    for d in others:
        d_u = d_u + tn(env[f"in{d}"], d_low_others[d - 1])
    return activated, d_inputs.astype(BF), d_bfly, d_u * scale, d_v


def solution(mesh):
    return jax.shard_map(
        local,
        mesh=mesh,
        in_specs=(
            P("dp", "feat"),
            P("feat", None, None, None),
            P("feat", None),
            P(None, "feat"),
            P("dp", "feat"),
        ),
        out_specs=(
            P("dp", "feat"),
            P("dp", "feat"),
            P("feat", None, None, None),
            P("feat", None),
            P(None, "feat"),
        ),
        check_vma=False,
    )
```

time: 181 us -> 130 us (0.72)
  waiting for transfers between devices: 105 us -> 45.6 us
  other arithmetic: 1.08 us -> 5.98 us
  Pallas kernels: 29.7 us -> 32.2 us
    ppermute x4 -> x5, waiting for transfers between devices: 45.8 us -> 12.6 us  [rolled(): lax.ppermute(block, axis, [(i, (i + shift) % count) for i in range(count)])]
    ppermute x28 -> x27, waiting for transfers between devices: 58.9 us -> 33 us  [crossed(): return lax.ppermute(block, axis, [(i, i ^ mask) for i in range(count)])]
    slice x0 -> x4, local copies, waits for them, and re-layouts: none -> 2.73 us  [the longest x1 2.69 us: send_cot(): piece = tie(cotangent[:, first * group:last * group], value)[0]]
    pallas_call x3 -> x4, Pallas kernels: 29.7 us -> 32.2 us  [the longest x2 14.7 us: add_other(): call(functools.partial(other_grad_kernel, [1] * sections, last), end - ba...]
    add x2 -> x4, other arithmetic: 0.05 us -> 2 us  [scatter_half(): return keep + crossed(send.astype(BF), axis, 1 << bit).astype(F32)]
    select_n x6 -> x8, other arithmetic: 0.16 us -> 2.02 us  [gather_half(): low = jnp.where(mine == 0, part, other)]
    unnamed x27 -> x31, local copies, waits for them, and re-layouts: 8.35 us -> 6.88 us
    ppermute x28 -> x27, starting transfers between devices: 27 us -> 25.9 us  [crossed(): return lax.ppermute(block, axis, [(i, i ^ mask) for i in range(count)])]
  transfers between devices with their start and end apart: 32 -> 32, of which waited for: 18 -> 14; matrix products, arithmetic and copies ran while one was open for 3% -> 9% of each run, Pallas kernels for 3% -> 25%
where the time goes in v2:
time: 130 us; the launch traced here: 129 us
  waiting for transfers between devices  45.6 us (35%)
  Pallas kernels  32.2 us (25%)
  starting transfers between devices  31.3 us (24%)
  local copies, waits for them, and re-layouts  9.67 us (7%)
  other arithmetic  5.98 us (5%)
  matrix products  3.52 us (3%)
    ppermute x27, waiting for transfers between devices, crossed(): return lax.ppermute(block, axis, [(i, i ^ mask) for i in range(count)])  33 us
    ppermute x27, starting transfers between devices, crossed(): return lax.ppermute(block, axis, [(i, i ^ mask) for i in range(count)])  25.9 us
    pallas_call x2, Pallas kernels, add_other(): call(functools.partial(other_grad_kernel, [1] * sections, last), end - ba...  14.7 us
    ppermute x5, waiting for transfers between devices, rolled(): lax.ppermute(block, axis, [(i, (i + shift) % count) for i in range(count)])  12.6 us
    pallas_call x1, Pallas kernels, local(): call(functools.partial(forward_kernel, [1] * sections), per_dev, specs +...  11.2 us
    unnamed x31, local copies, waits for them, and re-layouts  6.88 us
    pallas_call x1, Pallas kernels, own_grad(): call(functools.partial(own_grad_kernel, [1] * sections), per_dev, specs +...  6.31 us
    ppermute x5, starting transfers between devices, rolled(): lax.ppermute(block, axis, [(i, (i + shift) % count) for i in range(count)])  5.43 us
  transfers between devices with their start and end apart: 32, of which 14 were waited for; matrix products, arithmetic and copies ran while one was open for 9% of the time, Pallas kernels for 25%

profile of v2, /device:TPU:0, one launch (start us, length us, event | category | flops | bytes accessed | tf_op | source)
XLA Modules:
  0.0 129.3 jit_solution(5199689822131837158)
XLA Ops:
  0.7 4.1 %collective-permute-start.4 = (bf16[512,512]{1,0:T(8,128)(2,1)}, bf16[512,512]{1,0:T(8,128)(2,1)S(1)}, u32[]{:S(2)}, u32[]{:S(2)}) collective-permute-start(bf16[512,512]{1,0:T(8,128)(2,1)} %refs_6_.3), channel_id=1, source_target_pairs={{0,8},{1,9},{2,10},{3,11},{4,12},{5,13},{6,14},{7,15},{8,0},{9,1},... | collective-permute-start | bytes 1572872 | tf_op jit(solution)/shard_map/ppermute | solution.py:20
  4.8 1.6 %collective-permute-start.3 = (bf16[512,512]{1,0:T(8,128)(2,1)}, bf16[512,512]{1,0:T(8,128)(2,1)S(1)}, u32[]{:S(2)}, u32[]{:S(2)}) collective-permute-start(bf16[512,512]{1,0:T(8,128)(2,1)} %refs_6_.3), channel_id=1, source_target_pairs={{0,4},{1,5},{2,6},{3,7},{4,0},{5,1},{6,2},{7,3},{8,12},{9,13},{10,... | collective-permute-start | bytes 1572872 | tf_op jit(solution)/shard_map/ppermute | solution.py:20
  6.3 1.5 %collective-permute-start.2 = (bf16[512,512]{1,0:T(8,128)(2,1)}, bf16[512,512]{1,0:T(8,128)(2,1)S(1)}, u32[]{:S(2)}, u32[]{:S(2)}) collective-permute-start(bf16[512,512]{1,0:T(8,128)(2,1)} %refs_6_.3), channel_id=1, source_target_pairs={{0,2},{1,3},{2,0},{3,1},{4,6},{5,7},{6,4},{7,5},{8,10},{9,11},{10,... | collective-permute-start | bytes 1572872 | tf_op jit(solution)/shard_map/ppermute | solution.py:20
  11.2 1.5 %collective-permute-start.7 = (bf16[512,1024]{1,0:T(8,128)(2,1)}, bf16[512,1024]{1,0:T(8,128)(2,1)S(1)}, u32[]{:S(2)}, u32[]{:S(2)}) collective-permute-start(bf16[512,1024]{1,0:T(8,128)(2,1)} %pad_maximum_fusion), channel_id=1, source_target_pairs={{0,16},{16,0},{1,17},{17,1},{2,18},{18,2},{3,19},{19,3},{4,20},{20... | collective-permute-start | bytes 3145736 | tf_op jit(solution)/shard_map/ppermute | solution.py:25
  15.0 6.1 %collective-permute-done.1 = bf16[128,256]{1,0:T(8,128)(2,1)S(1)} collective-permute-done((bf16[128,256]{1,0:T(8,128)(2,1)S(1)}, bf16[128,256]{1,0:T(8,128)(2,1)S(1)}, u32[]{:S(2)}, u32[]{:S(2)}) %collective-permute-start.1) | collective-permute-done | bytes 65568 | tf_op jit(solution)/shard_map/ppermute | solution.py:20
  22.0 6.3 %collective-permute-done.4.refs_5_ = bf16[512,512]{1,0:T(8,128)(2,1)S(1)} collective-permute-done((bf16[512,512]{1,0:T(8,128)(2,1)}, bf16[512,512]{1,0:T(8,128)(2,1)S(1)}, u32[]{:S(2)}, u32[]{:S(2)}) %collective-permute-start.4) | collective-permute-done | bytes 524320 | tf_op jit(solution)/shard_map/ppermute | solution.py:20
  29.3 1.6 %collective-permute-start.5 = (bf16[128,256]{1,0:T(8,128)(2,1)S(1)}, bf16[128,256]{1,0:T(8,128)(2,1)S(1)}, u32[]{:S(2)}, u32[]{:S(2)}) collective-permute-start(bf16[128,256]{1,0:T(8,128)(2,1)S(1)} %convert_element_type.82), channel_id=1, source_target_pairs={{0,4},{1,5},{2,6},{3,7},{4,0},{5,1},{6,2},{7,3},{8,12},{9,13},{10,... | collective-permute-start | bytes 196616 | tf_op jit(solution)/shard_map/ppermute | solution.py:20
  30.8 2.8 %collective-permute-done.5 = bf16[128,256]{1,0:T(8,128)(2,1)S(1)} collective-permute-done((bf16[128,256]{1,0:T(8,128)(2,1)S(1)}, bf16[128,256]{1,0:T(8,128)(2,1)S(1)}, u32[]{:S(2)}, u32[]{:S(2)}) %collective-permute-start.5) | collective-permute-done | bytes 65568 | tf_op jit(solution)/shard_map/ppermute | solution.py:20
  33.6 1.9 %collective-permute-start.6 = (bf16[128,256]{1,0:T(8,128)(2,1)S(1)}, bf16[128,256]{1,0:T(8,128)(2,1)S(1)}, u32[]{:S(2)}, u32[]{:S(2)}) collective-permute-start(bf16[128,256]{1,0:T(8,128)(2,1)S(1)} %fusion.13), channel_id=1, source_target_pairs={{0,8},{1,9},{2,10},{3,11},{4,12},{5,13},{6,14},{7,15},{8,0},{9,1},... | collective-permute-start | bytes 196616 | tf_op jit(solution)/shard_map/ppermute | solution.py:20
  35.5 3.3 %collective-permute-done.6 = bf16[128,256]{1,0:T(8,128)(2,1)S(1)} collective-permute-done((bf16[128,256]{1,0:T(8,128)(2,1)S(1)}, bf16[128,256]{1,0:T(8,128)(2,1)S(1)}, u32[]{:S(2)}, u32[]{:S(2)}) %collective-permute-start.6) | collective-permute-done | bytes 65568 | tf_op jit(solution)/shard_map/ppermute | solution.py:20
  38.9 1.6 %collective-permute-start.15 = (bf16[128,256]{1,0:T(8,128)(2,1)S(1)}, bf16[128,256]{1,0:T(8,128)(2,1)S(1)}, u32[]{:S(2)}, u32[]{:S(2)}) collective-permute-start(bf16[128,256]{1,0:T(8,128)(2,1)S(1)} %convert_add_fusion.4), channel_id=1, source_target_pairs={{0,16},{16,0},{1,17},{17,1},{2,18},{18,2},{3,19},{19,3},{4,20},{20... | collective-permute-start | bytes 196616 | tf_op jit(solution)/shard_map/ppermute | solution.py:25
  40.5 1.5 %collective-permute-start.8 = (bf16[128,256]{1,0:T(8,128)(2,1)S(1)}, bf16[128,256]{1,0:T(8,128)(2,1)}, u32[]{:S(2)}, u32[]{:S(2)}) collective-permute-start(bf16[128,256]{1,0:T(8,128)(2,1)S(1)} %convert_add_fusion.4), channel_id=1, source_target_pairs={{0,2},{1,3},{2,0},{3,1},{4,6},{5,7},{6,4},{7,5},{8,10},{9,11},{10,... | collective-permute-start | bytes 196616 | tf_op jit(solution)/shard_map/ppermute | solution.py:20
  42.0 2.7 %slice.11 = bf16[512,1536]{1,0:T(8,128)(2,1)} slice(bf16[512,2048]{1,0:T(8,128)(2,1)} %refs_10_.1), slice={[0:512], [512:2048]} | slice | bytes 3145728 | tf_op jit(solution)/shard_map/slice | solution.py:228
  47.5 1.5 %collective-permute-start.14 = (bf16[512,512]{1,0:T(8,128)(2,1)S(1)}, bf16[512,512]{1,0:T(8,128)(2,1)S(1)}, u32[]{:S(2)}, u32[]{:S(2)}) collective-permute-start(bf16[512,512]{1,0:T(8,128)(2,1)S(1)} %slice.10.refs_0_.refs_1_.refs_6_), channel_id=1, source_target_pairs={{0,4},{1,5},{2,6},{3,7},{4,0},{5,1},{6,2},{7,3},{8,12},{9,13},{10,... | collective-permute-start | bytes 1572872 | tf_op jit(solution)/shard_map/ppermute | solution.py:20
  50.6 2.0 %copy-done.2 = bf16[4,7,128,512]{3,2,1,0:T(8,128)(2,1)S(1)} copy-done((bf16[4,7,128,512]{3,2,1,0:T(8,128)(2,1)S(1)}, bf16[4,7,128,512]{3,2,1,0:T(8,128)(2,1)}, u32[]{:S(2)}) %copy-start.2) | copy-done | bytes 3670040
  52.6 1.6 %copy-done.5 = bf16[512,2048]{1,0:T(8,128)(2,1)S(1)} copy-done((bf16[512,2048]{1,0:T(8,128)(2,1)S(1)}, bf16[512,2048]{1,0:T(8,128)(2,1)}, u32[]{:S(2)}) %copy-start.5) | copy-done | bytes 2097176
  54.2 11.2 %forward.1 = (bf16[512,2048]{1,0:T(8,128)(2,1)}, bf16[512,2048]{1,0:T(8,128)(2,1)S(1)}, f32[512,256]{1,0:T(8,128)S(1)}, bf16[512,512]{1,0:T(8,128)(2,1)S(1)}, bf...) custom-call(bf16[512,512]{1,0:T(8,128)(2,1)S(1)} %copy-done.1, ...), custom_call_target="tpu_custom_call" | custom-call | flops 1000 | bytes 1000 | tf_op jit(solution)/shard_map/forward/pallas_call | solution.py:262
  67.1 1.6 %collective-permute-start.19 = (bf16[128,256]{1,0:T(8,128)(2,1)S(1)}, bf16[128,256]{1,0:T(8,128)(2,1)S(1)}, u32[]{:S(2)}, u32[]{:S(2)}) collective-permute-start(bf16[128,256]{1,0:T(8,128)(2,1)S(1)} %copy-done.14), channel_id=1, source_target_pairs={{0,2},{1,3},{2,0},{3,1},{4,6},{5,7},{6,4},{7,5},{8,10},{9,11},{10,... | collective-permute-start | bytes 196616 | tf_op jit(solution)/shard_map/ppermute | solution.py:20
  70.4 2.0 %collective-permute-start.22 = (bf16[512,512]{1,0:T(8,128)(2,1)S(1)}, bf16[512,512]{1,0:T(8,128)(2,1)S(1)}, u32[]{:S(2)}, u32[]{:S(2)}) collective-permute-start(bf16[512,512]{1,0:T(8,128)(2,1)S(1)} %get-tuple-element.79), channel_id=1, source_target_pairs={{0,8},{1,9},{2,10},{3,11},{4,12},{5,13},{6,14},{7,15},{8,0},{9,1},... | collective-permute-start | bytes 1572872 | tf_op jit(solution)/shard_map/ppermute | solution.py:20
  72.4 6.3 %own_grad.1 = (f32[4,7,128,512]{3,2,1,0:T(8,128)}, f32[256,2048]{1,0:T(8,128)}) custom-call(bf16[512,512]{1,0:T(8,128)(2,1)S(1)} %copy-done.1, bf16[512,512]{1,0:T(8,128)(2,1)S(1)} %copy-done.1, bf16[512,512]{1,0:T(8,128)(2,1)} %collective-permute-done.10.refs_2_, bf16[512,512]{1,0:T(8,128)(2,1)S(1)} %copy-done.9, bf16[512,512]{1,0:T(8,128)(2,1)S(1)} %copy-done.7, ...), custom_call_target="tpu_custom_call" | custom-call | flops 1000 | bytes 1000 | tf_op jit(solution)/shard_map/own_grad/pallas_call | solution.py:278
  78.7 3.6 %collective-permute-done.16.refs_10_ = bf16[512,1536]{1,0:T(8,128)(2,1)} collective-permute-done((bf16[512,1536]{1,0:T(8,128)(2,1)}, bf16[512,1536]{1,0:T(8,128)(2,1)}, u32[]{:S(2)}, u32[]{:S(2)}) %collective-permute-start.16) | collective-permute-done | bytes 1572896 | tf_op jit(solution)/shard_map/ppermute | solution.py:25
  83.0 3.7 %collective-permute-done.17 = bf16[128,256]{1,0:T(8,128)(2,1)S(1)} collective-permute-done((bf16[128,256]{1,0:T(8,128)(2,1)S(1)}, bf16[128,256]{1,0:T(8,128)(2,1)S(1)}, u32[]{:S(2)}, u32[]{:S(2)}) %collective-permute-start.17) | collective-permute-done | bytes 65568 | tf_op jit(solution)/shard_map/ppermute | solution.py:20
  87.3 5.7 %collective-permute-done.18.refs_5_ = bf16[512,512]{1,0:T(8,128)(2,1)S(1)} collective-permute-done((bf16[512,512]{1,0:T(8,128)(2,1)S(1)}, bf16[512,512]{1,0:T(8,128)(2,1)S(1)}, u32[]{:S(2)}, u32[]{:S(2)}) %collective-permute-start.18) | collective-permute-done | bytes 524320 | tf_op jit(solution)/shard_map/ppermute | solution.py:25
  93.0 5.0 %other_grad.2 = (f32[4,7,128,512]{3,2,1,0:T(8,128)}, f32[256,2048]{1,0:T(8,128)}) custom-call(bf16[512,512]{1,0:T(8,128)(2,1)S(1)} %slice.10.refs_0_.refs_1_.refs_6_, bf16[512,512]{1,0:T(8,128)(2,1)S(1)} %slice.10.refs_0_.refs_1_.refs_6_, bf16[512,512]{1,0:T(8,128)(2,1)S(1)} %collective-permute-done.12.refs_2_, ...), custom_call_target="tpu_custom_call", output_to_operand_aliasing={{0}: (11, {}), {1}: (12, {})} | custom-call | flops 1000 | bytes 1000 | tf_op jit(solution)/shard_map/other_grad/pallas_call | solution.py:294
  98.1 9.6 %other_grad.3 = (f32[4,7,128,512]{3,2,1,0:T(8,128)}, f32[256,2048]{1,0:T(8,128)}) custom-call(bf16[512,512]{1,0:T(8,128)(2,1)S(1)} %slice.10.refs_0_.refs_1_.refs_6_, bf16[512,512]{1,0:T(8,128)(2,1)S(1)} %slice.10.refs_0_.refs_1_.refs_6_, bf16[512,512]{1,0:T(8,128)(2,1)S(1)} %collective-permute-done.12.refs_2_, ...), custom_call_target="tpu_custom_call", output_to_operand_aliasing={{0}: (11, {}), {1}: (12, {})} | custom-call | flops 1000 | bytes 1000 | tf_op jit(solution)/shard_map/other_grad/pallas_call | solution.py:294
  107.7 1.5 %collective-permute-start.23 = (bf16[128,256]{1,0:T(8,128)(2,1)S(1)}, bf16[128,256]{1,0:T(8,128)(2,1)S(1)}, u32[]{:S(2)}, u32[]{:S(2)}) collective-permute-start(bf16[128,256]{1,0:T(8,128)(2,1)S(1)} %convert_element_type.91), channel_id=1, source_target_pairs={{0,4},{1,5},{2,6},{3,7},{4,0},{5,1},{6,2},{7,3},{8,12},{9,13},{10,... | collective-permute-start | bytes 196616 | tf_op jit(solution)/shard_map/ppermute | solution.py:20
  109.2 2.8 %collective-permute-done.23 = bf16[128,256]{1,0:T(8,128)(2,1)S(1)} collective-permute-done((bf16[128,256]{1,0:T(8,128)(2,1)S(1)}, bf16[128,256]{1,0:T(8,128)(2,1)S(1)}, u32[]{:S(2)}, u32[]{:S(2)}) %collective-permute-start.23) | collective-permute-done | bytes 65568 | tf_op jit(solution)/shard_map/ppermute | solution.py:20
  112.1 2.0 %collective-permute-start.24 = (bf16[128,256]{1,0:T(8,128)(2,1)S(1)}, bf16[128,256]{1,0:T(8,128)(2,1)S(1)}, u32[]{:S(2)}, u32[]{:S(2)}) collective-permute-start(bf16[128,256]{1,0:T(8,128)(2,1)S(1)} %fusion.14), channel_id=1, source_target_pairs={{0,8},{1,9},{2,10},{3,11},{4,12},{5,13},{6,14},{7,15},{8,0},{9,1},... | collective-permute-start | bytes 196616 | tf_op jit(solution)/shard_map/ppermute | solution.py:20
  114.1 3.2 %collective-permute-done.24 = bf16[128,256]{1,0:T(8,128)(2,1)S(1)} collective-permute-done((bf16[128,256]{1,0:T(8,128)(2,1)S(1)}, bf16[128,256]{1,0:T(8,128)(2,1)S(1)}, u32[]{:S(2)}, u32[]{:S(2)}) %collective-permute-start.24) | collective-permute-done | bytes 65568 | tf_op jit(solution)/shard_map/ppermute | solution.py:20
  118.4 3.3 %collective-permute-done.29 = bf16[128,256]{1,0:T(8,128)(2,1)S(1)} collective-permute-done((bf16[128,256]{1,0:T(8,128)(2,1)S(1)}, bf16[128,256]{1,0:T(8,128)(2,1)S(1)}, u32[]{:S(2)}, u32[]{:S(2)}) %collective-permute-start.29) | collective-permute-done | bytes 65568 | tf_op jit(solution)/shard_map/ppermute | solution.py:25
  123.0 2.9 %collective-permute-done.30 = bf16[128,256]{1,0:T(8,128)(2,1)S(1)} collective-permute-done((bf16[128,256]{1,0:T(8,128)(2,1)S(1)}, bf16[128,256]{1,0:T(8,128)(2,1)S(1)}, u32[]{:S(2)}, u32[]{:S(2)}) %collective-permute-start.30) | collective-permute-done | bytes 65568 | tf_op jit(solution)/shard_map/ppermute | solution.py:20
  126.1 1.5 %fusion.6 = bf16[512,512]{1,0:T(8,128)(2,1)} fusion(bf16[512,256]{1,0:T(8,128)(2,1)S(1)} %copy-done, bf16[512,512]{1,0:T(8,128)(2,1)S(1)} %get-tuple-element.90, bf16[512,512]{1,0:T(8,128)(2,1)S(1)} %collective-permute-done.22, bf16[512,512]{1,0:T(8,128)(2,1)S(1)} %collective-permute-done.21, bf16[512,512]{1,0:T(8,128)(2,1)S(1)} %collective-permute-done.25, ...), kind=kOutput, calls=%fused_computation.7 | convolution fusion | flops 138674176 | bytes 4718592 | tf_op jit(solution)/shard_map/dot_general | solution.py:79
  (104 shorter events, 20.8 us)
Async XLA Ops:
  0.7 27.6 %collective-permute-start.4 = (bf16[512,512]{1,0:T(8,128)(2,1)}, bf16[512,512]{1,0:T(8,128)(2,1)S(1)}, u32[]{:S(2)}, u32[]{:S(2)}) collective-permute-start(bf16[512,512]{1,0:T(8,128)(2,1)} %refs_6_.3), channel_id=1, source_target_pairs={{0,8},{1,9},{2,10},{3,11},{4,12},{5,13},{6,14},{7,15},{8,0},{9,1},... | collective-permute-start | bytes 1572872 | tf_op jit(solution)/shard_map/ppermute | solution.py:20
  4.8 23.7 %collective-permute-start.3 = (bf16[512,512]{1,0:T(8,128)(2,1)}, bf16[512,512]{1,0:T(8,128)(2,1)S(1)}, u32[]{:S(2)}, u32[]{:S(2)}) collective-permute-start(bf16[512,512]{1,0:T(8,128)(2,1)} %refs_6_.3), channel_id=1, source_target_pairs={{0,4},{1,5},{2,6},{3,7},{4,0},{5,1},{6,2},{7,3},{8,12},{9,13},{10,... | collective-permute-start | bytes 1572872 | tf_op jit(solution)/shard_map/ppermute | solution.py:20
  6.3 22.1 %collective-permute-start.2 = (bf16[512,512]{1,0:T(8,128)(2,1)}, bf16[512,512]{1,0:T(8,128)(2,1)S(1)}, u32[]{:S(2)}, u32[]{:S(2)}) collective-permute-start(bf16[512,512]{1,0:T(8,128)(2,1)} %refs_6_.3), channel_id=1, source_target_pairs={{0,2},{1,3},{2,0},{3,1},{4,6},{5,7},{6,4},{7,5},{8,10},{9,11},{10,... | collective-permute-start | bytes 1572872 | tf_op jit(solution)/shard_map/ppermute | solution.py:20
  9.3 3.4 %collective-permute-start = (bf16[256,256]{1,0:T(8,128)(2,1)S(1)}, bf16[256,256]{1,0:T(8,128)(2,1)}, u32[]{:S(2)}, u32[]{:S(2)}) collective-permute-start(bf16[256,256]{1,0:T(8,128)(2,1)S(1)} %dynamic-slice_convert_fusion.1), channel_id=1, source_target_pairs={{0,1},{1,0},{2,3},{3,2},{4,5},{5,4},{6,7},{7,6},{8,9},{9,8},{10,11... | collective-permute-start | bytes 393224 | tf_op jit(solution)/shard_map/ppermute | solution.py:20
  11.2 27.7 %collective-permute-start.7 = (bf16[512,1024]{1,0:T(8,128)(2,1)}, bf16[512,1024]{1,0:T(8,128)(2,1)S(1)}, u32[]{:S(2)}, u32[]{:S(2)}) collective-permute-start(bf16[512,1024]{1,0:T(8,128)(2,1)} %pad_maximum_fusion), channel_id=1, source_target_pairs={{0,16},{16,0},{1,17},{17,1},{2,18},{18,2},{3,19},{19,3},{4,20},{20... | collective-permute-start | bytes 3145736 | tf_op jit(solution)/shard_map/ppermute | solution.py:25
  14.4 6.6 %collective-permute-start.1 = (bf16[128,256]{1,0:T(8,128)(2,1)S(1)}, bf16[128,256]{1,0:T(8,128)(2,1)S(1)}, u32[]{:S(2)}, u32[]{:S(2)}) collective-permute-start(bf16[128,256]{1,0:T(8,128)(2,1)S(1)} %dynamic-slice_convert_fusion.3), channel_id=1, source_target_pairs={{0,2},{1,3},{2,0},{3,1},{4,6},{5,7},{6,4},{7,5},{8,10},{9,11},{10,... | collective-permute-start | bytes 196616 | tf_op jit(solution)/shard_map/ppermute | solution.py:20
  29.3 4.3 %collective-permute-start.5 = (bf16[128,256]{1,0:T(8,128)(2,1)S(1)}, bf16[128,256]{1,0:T(8,128)(2,1)S(1)}, u32[]{:S(2)}, u32[]{:S(2)}) collective-permute-start(bf16[128,256]{1,0:T(8,128)(2,1)S(1)} %convert_element_type.82), channel_id=1, source_target_pairs={{0,4},{1,5},{2,6},{3,7},{4,0},{5,1},{6,2},{7,3},{8,12},{9,13},{10,... | collective-permute-start | bytes 196616 | tf_op jit(solution)/shard_map/ppermute | solution.py:20
  33.6 5.2 %collective-permute-start.6 = (bf16[128,256]{1,0:T(8,128)(2,1)S(1)}, bf16[128,256]{1,0:T(8,128)(2,1)S(1)}, u32[]{:S(2)}, u32[]{:S(2)}) collective-permute-start(bf16[128,256]{1,0:T(8,128)(2,1)S(1)} %fusion.13), channel_id=1, source_target_pairs={{0,8},{1,9},{2,10},{3,11},{4,12},{5,13},{6,14},{7,15},{8,0},{9,1},... | collective-permute-start | bytes 196616 | tf_op jit(solution)/shard_map/ppermute | solution.py:20
  38.9 5.8 %collective-permute-start.15 = (bf16[128,256]{1,0:T(8,128)(2,1)S(1)}, bf16[128,256]{1,0:T(8,128)(2,1)S(1)}, u32[]{:S(2)}, u32[]{:S(2)}) collective-permute-start(bf16[128,256]{1,0:T(8,128)(2,1)S(1)} %convert_add_fusion.4), channel_id=1, source_target_pairs={{0,16},{16,0},{1,17},{17,1},{2,18},{18,2},{3,19},{19,3},{4,20},{20... | collective-permute-start | bytes 196616 | tf_op jit(solution)/shard_map/ppermute | solution.py:25
  40.5 4.9 %collective-permute-start.8 = (bf16[128,256]{1,0:T(8,128)(2,1)S(1)}, bf16[128,256]{1,0:T(8,128)(2,1)}, u32[]{:S(2)}, u32[]{:S(2)}) collective-permute-start(bf16[128,256]{1,0:T(8,128)(2,1)S(1)} %convert_add_fusion.4), channel_id=1, source_target_pairs={{0,2},{1,3},{2,0},{3,1},{4,6},{5,7},{6,4},{7,5},{8,10},{9,11},{10,... | collective-permute-start | bytes 196616 | tf_op jit(solution)/shard_map/ppermute | solution.py:20
  44.7 5.8 %collective-permute-start.10 = (bf16[512,512]{1,0:T(8,128)(2,1)S(1)}, bf16[512,512]{1,0:T(8,128)(2,1)}, u32[]{:S(2)}, u32[]{:S(2)}) collective-permute-start(bf16[512,512]{1,0:T(8,128)(2,1)S(1)} %copy-done.1), channel_id=1, source_target_pairs={{0,1},{1,0},{2,3},{3,2},{4,5},{5,4},{6,7},{7,6},{8,9},{9,8},{10,11... | collective-permute-start | bytes 1572872 | tf_op jit(solution)/shard_map/ppermute | solution.py:20
  44.8 37.6 %collective-permute-start.16 = (bf16[512,1536]{1,0:T(8,128)(2,1)}, bf16[512,1536]{1,0:T(8,128)(2,1)}, u32[]{:S(2)}, u32[]{:S(2)}) collective-permute-start(bf16[512,1536]{1,0:T(8,128)(2,1)} %slice.11), channel_id=1, source_target_pairs={{0,16},{16,0},{1,17},{17,1},{2,18},{18,2},{3,19},{19,3},{4,20},{20... | collective-permute-start | bytes 4718600 | tf_op jit(solution)/shard_map/ppermute | solution.py:25
  46.9 2.6 %collective-permute-start.9 = (bf16[256,256]{1,0:T(8,128)(2,1)}, bf16[256,256]{1,0:T(8,128)(2,1)}, u32[]{:S(2)}, u32[]{:S(2)}) collective-permute-start(bf16[256,256]{1,0:T(8,128)(2,1)} %pad_maximum_fusion.6), channel_id=1, source_target_pairs={{0,1},{1,0},{2,3},{3,2},{4,5},{5,4},{6,7},{7,6},{8,9},{9,8},{10,11... | collective-permute-start | bytes 393224 | tf_op jit(solution)/shard_map/ppermute | solution.py:20
  47.5 19.6 %collective-permute-start.14 = (bf16[512,512]{1,0:T(8,128)(2,1)S(1)}, bf16[512,512]{1,0:T(8,128)(2,1)S(1)}, u32[]{:S(2)}, u32[]{:S(2)}) collective-permute-start(bf16[512,512]{1,0:T(8,128)(2,1)S(1)} %slice.10.refs_0_.refs_1_.refs_6_), channel_id=1, source_target_pairs={{0,4},{1,5},{2,6},{3,7},{4,0},{5,1},{6,2},{7,3},{8,12},{9,13},{10,... | collective-permute-start | bytes 1572872 | tf_op jit(solution)/shard_map/ppermute | solution.py:20
  49.0 18.1 %collective-permute-start.13 = (bf16[512,512]{1,0:T(8,128)(2,1)S(1)}, bf16[512,512]{1,0:T(8,128)(2,1)S(1)}, u32[]{:S(2)}, u32[]{:S(2)}) collective-permute-start(bf16[512,512]{1,0:T(8,128)(2,1)S(1)} %slice.10.refs_0_.refs_1_.refs_6_), channel_id=1, source_target_pairs={{0,2},{1,3},{2,0},{3,1},{4,6},{5,7},{6,4},{7,5},{8,10},{9,11},{10,... | collective-permute-start | bytes 1572872 | tf_op jit(solution)/shard_map/ppermute | solution.py:20
  49.5 17.5 %collective-permute-start.12 = (bf16[512,512]{1,0:T(8,128)(2,1)S(1)}, bf16[512,512]{1,0:T(8,128)(2,1)S(1)}, u32[]{:S(2)}, u32[]{:S(2)}) collective-permute-start(bf16[512,512]{1,0:T(8,128)(2,1)S(1)} %slice.10.refs_0_.refs_1_.refs_6_), channel_id=1, source_target_pairs={{0,1},{1,0},{2,3},{3,2},{4,5},{5,4},{6,7},{7,6},{8,9},{9,8},{10,11... | collective-permute-start | bytes 1572872 | tf_op jit(solution)/shard_map/ppermute | solution.py:20
  65.5 1.5 %collective-permute-start.11 = (bf16[256,256]{1,0:T(8,128)(2,1)S(1)}, bf16[256,256]{1,0:T(8,128)(2,1)S(1)}, u32[]{:S(2)}, u32[]{:S(2)}) collective-permute-start(bf16[256,256]{1,0:T(8,128)(2,1)S(1)} %dynamic-slice_convert_fusion), channel_id=1, source_target_pairs={{0,1},{1,0},{2,3},{3,2},{4,5},{5,4},{6,7},{7,6},{8,9},{9,8},{10,11... | collective-permute-start | bytes 393224 | tf_op jit(solution)/shard_map/ppermute | solution.py:20
  67.1 11.6 %collective-permute-start.19 = (bf16[128,256]{1,0:T(8,128)(2,1)S(1)}, bf16[128,256]{1,0:T(8,128)(2,1)S(1)}, u32[]{:S(2)}, u32[]{:S(2)}) collective-permute-start(bf16[128,256]{1,0:T(8,128)(2,1)S(1)} %copy-done.14), channel_id=1, source_target_pairs={{0,2},{1,3},{2,0},{3,1},{4,6},{5,7},{6,4},{7,5},{8,10},{9,11},{10,... | collective-permute-start | bytes 196616 | tf_op jit(solution)/shard_map/ppermute | solution.py:20
  68.6 24.4 %collective-permute-start.18 = (bf16[512,512]{1,0:T(8,128)(2,1)S(1)}, bf16[512,512]{1,0:T(8,128)(2,1)S(1)}, u32[]{:S(2)}, u32[]{:S(2)}) collective-permute-start(bf16[512,512]{1,0:T(8,128)(2,1)S(1)} %collective-permute-done.4.refs_5_), channel_id=1, source_target_pairs={{0,16},{16,0},{1,17},{17,1},{2,18},{18,2},{3,19},{19,3},{4,20},{20... | collective-permute-start | bytes 1572872 | tf_op jit(solution)/shard_map/ppermute | solution.py:25
  69.8 37.9 %collective-permute-start.21 = (bf16[512,512]{1,0:T(8,128)(2,1)S(1)}, bf16[512,512]{1,0:T(8,128)(2,1)S(1)}, u32[]{:S(2)}, u32[]{:S(2)}) collective-permute-start(bf16[512,512]{1,0:T(8,128)(2,1)S(1)} %get-tuple-element.78), channel_id=1, source_target_pairs={{0,4},{1,5},{2,6},{3,7},{4,0},{5,1},{6,2},{7,3},{8,12},{9,13},{10,... | collective-permute-start | bytes 1572872 | tf_op jit(solution)/shard_map/ppermute | solution.py:20
  70.4 37.3 %collective-permute-start.22 = (bf16[512,512]{1,0:T(8,128)(2,1)S(1)}, bf16[512,512]{1,0:T(8,128)(2,1)S(1)}, u32[]{:S(2)}, u32[]{:S(2)}) collective-permute-start(bf16[512,512]{1,0:T(8,128)(2,1)S(1)} %get-tuple-element.79), channel_id=1, source_target_pairs={{0,8},{1,9},{2,10},{3,11},{4,12},{5,13},{6,14},{7,15},{8,0},{9,1},... | collective-permute-start | bytes 1572872 | tf_op jit(solution)/shard_map/ppermute | solution.py:20
  82.3 4.3 %collective-permute-start.17 = (bf16[128,256]{1,0:T(8,128)(2,1)S(1)}, bf16[128,256]{1,0:T(8,128)(2,1)S(1)}, u32[]{:S(2)}, u32[]{:S(2)}) collective-permute-start(bf16[128,256]{1,0:T(8,128)(2,1)S(1)} %dynamic-slice_convert_fusion.2), channel_id=1, source_target_pairs={{0,2},{1,3},{2,0},{3,1},{4,6},{5,7},{6,4},{7,5},{8,10},{9,11},{10,... | collective-permute-start | bytes 196616 | tf_op jit(solution)/shard_map/ppermute | solution.py:20
  82.9 4.3 %collective-permute-start.20 = (bf16[256,256]{1,0:T(8,128)(2,1)S(1)}, bf16[256,256]{1,0:T(8,128)(2,1)S(1)}, u32[]{:S(2)}, u32[]{:S(2)}) collective-permute-start(bf16[256,256]{1,0:T(8,128)(2,1)S(1)} %pad_maximum_fusion.7), channel_id=1, source_target_pairs={{0,1},{1,0},{2,3},{3,2},{4,5},{5,4},{6,7},{7,6},{8,9},{9,8},{10,11... | collective-permute-start | bytes 393224 | tf_op jit(solution)/shard_map/ppermute | solution.py:20
  86.7 30.6 %collective-permute-start.25 = (bf16[512,512]{1,0:T(8,128)(2,1)S(1)}, bf16[512,512]{1,0:T(8,128)(2,1)S(1)}, u32[]{:S(2)}, u32[]{:S(2)}) collective-permute-start(bf16[512,512]{1,0:T(8,128)(2,1)S(1)} %get-tuple-element.82), channel_id=1, source_target_pairs={{0,2},{1,3},{2,0},{3,1},{4,6},{5,7},{6,4},{7,5},{8,10},{9,11},{10,... | collective-permute-start | bytes 1572872 | tf_op jit(solution)/shard_map/ppermute | solution.py:20
  107.7 4.3 %collective-permute-start.23 = (bf16[128,256]{1,0:T(8,128)(2,1)S(1)}, bf16[128,256]{1,0:T(8,128)(2,1)S(1)}, u32[]{:S(2)}, u32[]{:S(2)}) collective-permute-start(bf16[128,256]{1,0:T(8,128)(2,1)S(1)} %convert_element_type.91), channel_id=1, source_target_pairs={{0,4},{1,5},{2,6},{3,7},{4,0},{5,1},{6,2},{7,3},{8,12},{9,13},{10,... | collective-permute-start | bytes 196616 | tf_op jit(solution)/shard_map/ppermute | solution.py:20
  112.1 5.2 %collective-permute-start.24 = (bf16[128,256]{1,0:T(8,128)(2,1)S(1)}, bf16[128,256]{1,0:T(8,128)(2,1)S(1)}, u32[]{:S(2)}, u32[]{:S(2)}) collective-permute-start(bf16[128,256]{1,0:T(8,128)(2,1)S(1)} %fusion.14), channel_id=1, source_target_pairs={{0,8},{1,9},{2,10},{3,11},{4,12},{5,13},{6,14},{7,15},{8,0},{9,1},... | collective-permute-start | bytes 196616 | tf_op jit(solution)/shard_map/ppermute | solution.py:20
  117.3 4.3 %collective-permute-start.29 = (bf16[128,256]{1,0:T(8,128)(2,1)S(1)}, bf16[128,256]{1,0:T(8,128)(2,1)S(1)}, u32[]{:S(2)}, u32[]{:S(2)}) collective-permute-start(bf16[128,256]{1,0:T(8,128)(2,1)S(1)} %add_convert_fusion), channel_id=1, source_target_pairs={{0,16},{16,0},{1,17},{17,1},{2,18},{18,2},{3,19},{19,3},{4,20},{20... | collective-permute-start | bytes 196616 | tf_op jit(solution)/shard_map/ppermute | solution.py:25
  117.9 5.0 %collective-permute-start.26 = (bf16[128,256]{1,0:T(8,128)(2,1)S(1)}, bf16[128,256]{1,0:T(8,128)(2,1)S(1)}, u32[]{:S(2)}, u32[]{:S(2)}) collective-permute-start(bf16[128,256]{1,0:T(8,128)(2,1)S(1)} %add_convert_fusion), channel_id=1, source_target_pairs={{0,2},{1,3},{2,0},{3,1},{4,6},{5,7},{6,4},{7,5},{8,10},{9,11},{10,... | collective-permute-start | bytes 196616 | tf_op jit(solution)/shard_map/ppermute | solution.py:20
  118.4 7.7 %collective-permute-start.28 = (bf16[512,512]{1,0:T(8,128)(2,1)S(1)}, bf16[512,512]{1,0:T(8,128)(2,1)S(1)}, u32[]{:S(2)}, u32[]{:S(2)}) collective-permute-start(bf16[512,512]{1,0:T(8,128)(2,1)S(1)} %get-tuple-element.86), channel_id=1, source_target_pairs={{0,1},{1,0},{2,3},{3,2},{4,5},{5,4},{6,7},{7,6},{8,9},{9,8},{10,11... | collective-permute-start | bytes 1572872 | tf_op jit(solution)/shard_map/ppermute | solution.py:20
  121.7 4.3 %collective-permute-start.30 = (bf16[128,256]{1,0:T(8,128)(2,1)S(1)}, bf16[128,256]{1,0:T(8,128)(2,1)S(1)}, u32[]{:S(2)}, u32[]{:S(2)}) collective-permute-start(bf16[128,256]{1,0:T(8,128)(2,1)S(1)} %collective-permute-done.29), channel_id=1, source_target_pairs={{0,2},{1,3},{2,0},{3,1},{4,6},{5,7},{6,4},{7,5},{8,10},{9,11},{10,... | collective-permute-start | bytes 196616 | tf_op jit(solution)/shard_map/ppermute | solution.py:20
  122.9 3.1 %collective-permute-start.27 = (bf16[256,256]{1,0:T(8,128)(2,1)S(1)}, bf16[256,256]{1,0:T(8,128)(2,1)S(1)}, u32[]{:S(2)}, u32[]{:S(2)}) collective-permute-start(bf16[256,256]{1,0:T(8,128)(2,1)S(1)} %pad_maximum_fusion.8), channel_id=1, source_target_pairs={{0,1},{1,0},{2,3},{3,2},{4,5},{5,4},{6,7},{7,6},{8,9},{9,8},{10,11... | collective-permute-start | bytes 393224 | tf_op jit(solution)/shard_map/ppermute | solution.py:20
  126.0 1.6 %collective-permute-start.31 = (bf16[256,256]{1,0:T(8,128)(2,1)S(1)}, bf16[256,256]{1,0:T(8,128)(2,1)S(1)}, u32[]{:S(2)}, u32[]{:S(2)}) collective-permute-start(bf16[256,256]{1,0:T(8,128)(2,1)S(1)} %pad_maximum_fusion.9), channel_id=1, source_target_pairs={{0,1},{1,0},{2,3},{3,2},{4,5},{5,4},{6,7},{7,6},{8,9},{9,8},{10,11... | collective-permute-start | bytes 393224 | tf_op jit(solution)/shard_map/ppermute | solution.py:20
  (16 other events, 98.2 us)

commit v3 on v2

v3 whole, which is shorter than its diff:
```python
import functools

import jax
import jax.numpy as jnp
import numpy as np
from jax import lax
from jax.experimental import pallas as pl
from jax.experimental.pallas import tpu as pltpu
from jax.sharding import PartitionSpec as P

BF = jnp.bfloat16
F32 = jnp.float32
VMEM_LIMIT = 32 * 1024 * 1024
GELU_C = float(np.sqrt(2.0 / np.pi))
GELU_A = 0.044715


def crossed(block, axis, mask):
    count = lax.axis_size(axis)
    return lax.ppermute(block, axis, [(i, i ^ mask) for i in range(count)])


def rolled(block, axis, shift):
    count = lax.axis_size(axis)
    return lax.ppermute(block, axis, [(i, (i + shift) % count) for i in range(count)])


def scatter_half(part, bit, axis):
    rows = part.shape[0] // 2
    mine = (lax.axis_index(axis) >> bit) & 1
    keep = lax.dynamic_slice_in_dim(part, mine * rows, rows, 0)
    send = lax.dynamic_slice_in_dim(part, (1 - mine) * rows, rows, 0)
    return keep + crossed(send.astype(BF), axis, 1 << bit).astype(F32)


def tie(value, *others):
    return lax.optimization_barrier((value, *others))


def no_hooks(step, value):
    return value


def near_bits(axis):
    return min(lax.axis_size(axis).bit_length() - 1, 2)


def scatter_near(part, axis, hooks, direct):
    near = near_bits(axis)
    if not direct:
        for bit in range(near):
            part = hooks(f"scatter{bit}", scatter_half(part, bit, axis))
        return part
    count = 1 << near
    rows = part.shape[0] // count
    mine = lax.axis_index(axis) & (count - 1)
    total = lax.dynamic_slice_in_dim(part, mine * rows, rows, 0)
    for mask in range(1, count):
        send = lax.dynamic_slice_in_dim(part, (mine ^ mask) * rows, rows, 0)
        total = total + crossed(send.astype(BF), axis, mask).astype(F32)
    return hooks("scatter", total)


def sum_far(part, axis, hooks):
    near = near_bits(axis)
    sent = part.astype(BF)
    for mask in range(1, lax.axis_size(axis) >> near):
        part = part + crossed(sent, axis, mask << near).astype(F32)
    return hooks("far", part).astype(BF)


def gather_near(part, axis, direct):
    near = near_bits(axis)
    mine = lax.axis_index(axis)
    held = [part] + [crossed(part, axis, mask) for mask in range(1, 1 << near)]
    for bit in range(near):
        swap = (mine >> bit) & 1
        held = [jnp.where(swap == 0, h, held[i ^ (1 << bit)]) for i, h in enumerate(held)]
    if not direct and near == 2:
        held = [held[i] for i in (0, 2, 1, 3)]
    return jnp.concatenate(held, 0)


def gelu_parts(pre):
    square = pre * pre
    tanh = jnp.tanh(GELU_C * (pre + GELU_A * (square * pre)))
    half = 0.5 * (1.0 + tanh)
    slope = half + (0.5 * GELU_C) * pre * (1.0 - tanh * tanh) * (1.0 + (3.0 * GELU_A) * square)
    return pre * half, slope


def nt(a, b):
    return lax.dot_general(a, b, (((1,), (1,)), ((), ())), preferred_element_type=F32)


def tn(a, b):
    return lax.dot_general(a, b, (((0,), (0,)), ((), ())), preferred_element_type=F32)


def gathered(refs, pieces):
    refs = iter(refs)
    columns = []
    for count in pieces:
        rows = [next(refs)[...] for _ in range(count)]
        columns.append(rows[0] if count == 1 else jnp.concatenate(rows, axis=0))
    return columns[0] if len(columns) == 1 else jnp.concatenate(columns, axis=1)


def forward_kernel(pieces, *refs):
    sections, count = len(pieces), sum(pieces)
    x = refs[:count]
    bfly, low, lr_v, cot, act, d_pre, d_low = refs[count : count + 7]
    terms = refs[count + 7 :]
    width = bfly.shape[2]
    tiles = bfly[0].reshape(sections * width, bfly.shape[3])
    block = gathered(x, pieces)
    pre = jnp.dot(block, tiles, preferred_element_type=F32) + jnp.dot(
        low[...], lr_v[...], preferred_element_type=F32
    )
    value, slope = gelu_parts(pre)
    act[...] = value.astype(BF)
    grad = (cot[...].astype(F32) * slope).astype(BF)
    d_pre[...] = grad
    part = nt(grad, lr_v[...])

    @pl.when(pl.program_id(0) == 0)
    def _():
        d_low[...] = part

    @pl.when(pl.program_id(0) > 0)
    def _():
        d_low[...] += part

    back = nt(grad, tiles).astype(BF)
    for section in range(sections):
        terms[section][...] = back[:, section * width : (section + 1) * width]


def weight_grad_kernel(sections, own, other, starts, scale, *refs):
    refs = list(refs)

    def take(count):
        taken, refs[:] = refs[:count], refs[count:]
        return taken

    def side(x):
        return jnp.concatenate([ref[...] for ref in x], axis=1)

    parts = []
    if own:
        block = side(take(sections))
        low, grad = (ref[...] for ref in take(2))
        parts.append((tn(block, grad), tn(low, grad)))
    if other:
        block = side(take(sections))
        bfly, low, lr_v = take(3)
        cots = take(len(starts))
        cot = cots[0][...]
        for start, piece in zip(starts[1:], cots[1:]):
            cot = jnp.where(pl.program_id(0) >= start, piece[...], cot)
        tiles = bfly[0].reshape(sections * bfly.shape[2], bfly.shape[3])
        pre = jnp.dot(block, tiles, preferred_element_type=F32) + jnp.dot(
            low[...], lr_v[...], preferred_element_type=F32
        )
        _, slope = gelu_parts(pre)
        grad = (cot.astype(F32) * slope).astype(BF)
        parts.append((tn(block, grad), tn(low[...], grad)))
    if not own:
        d_bfly_in, d_v_in = take(2)
        parts.append((d_bfly_in[0].reshape(parts[0][0].shape), d_v_in[...]))
    d_bfly, d_v = refs
    total, total_v = parts[0]
    for part, part_v in parts[1:]:
        total, total_v = total + part, total_v + part_v
    d_bfly[0] = (total * scale).reshape(d_bfly.shape[1:])
    d_v[...] = total_v * scale


def finish_kernel(sections, others, scale, *refs):
    terms, (d_low, lr_u, x), rest = refs[:sections], refs[sections : sections + 3], refs[sections + 3 :]
    d_inputs, d_u = rest[2 * others :]
    total = nt(d_low[...], lr_u[...])
    for term in terms:
        total = total + term[...].astype(F32)
    d_inputs[...] = total.astype(BF)
    grad = tn(x[...], d_low[...])
    for other in range(others):
        grad = grad + tn(rest[2 * other][...], rest[2 * other + 1][...])
    d_u[...] = grad * scale


def column(rows, width, flip, base=0, at=0):
    return pl.BlockSpec((rows, width), lambda g: (at, (g + base) ^ flip))


def row(rows, width, base=0, at=0):
    return pl.BlockSpec((rows, width), lambda g: (at, g + base))


def clipped(rows, width, start, count):
    return pl.BlockSpec((rows, width), lambda g: (0, jnp.clip(g - start, 0, count - 1)))


def in_hbm(array):
    return pltpu.with_memory_space_constraint(array, pltpu.HBM)


def resident(*shape):
    return pl.BlockSpec(shape, lambda g: (0,) * len(shape))


def call(kernel, grid, in_specs, out_specs, out_shape, cost, aliases=None, name=None):
    return pl.pallas_call(
        kernel,
        grid=(grid,),
        in_specs=in_specs,
        out_specs=out_specs,
        out_shape=out_shape,
        input_output_aliases=aliases or {},
        cost_estimate=pl.CostEstimate(flops=cost[0], bytes_accessed=cost[1], transcendentals=0),
        compiler_params=pltpu.CompilerParams(vmem_limit_bytes=VMEM_LIMIT),
        name=name,
    )


def local(inputs, bfly, lr_u, lr_v, cotangent):
    tokens = inputs.shape[0]
    per_dev, sections, width, group = bfly.shape
    levels = sections - 1
    rank = lr_v.shape[0]
    local_bits = per_dev.bit_length() - 1
    data_groups = lax.axis_size("dp")
    scale = float(1.0 / np.sqrt(np.float32(tokens * data_groups)))
    remote = list(range(local_bits, levels))
    others = range(1, data_groups)

    flips = [(1 << s) if s < local_bits else 0 for s in range(sections)]

    def tile_spec(base=0):
        return pl.BlockSpec((1, sections, width, group), lambda g: (g + base, 0, 0, 0))

    low_spec = resident(tokens, rank)
    wide = jax.ShapeDtypeStruct((tokens, per_dev * group), BF)
    narrow = jax.ShapeDtypeStruct((tokens, per_dev * width), BF)
    tile_shape = jax.ShapeDtypeStruct(bfly.shape, F32)
    v_shape = jax.ShapeDtypeStruct(lr_v.shape, F32)

    def to_partner(block, section):
        return crossed(block, "feat", 1 << (section - local_bits))

    env = {}

    def pin(value, *names):
        names = [n for n in names if n in env]
        if names:
            value, *rest = tie(value, *[env[n] for n in names])
            env.update(zip(names, rest))
        return value

    def each(prefix, *tails):
        return [f"{prefix}{d}{t}" for d in others for t in tails or ("",)]

    far = remote[-1:]
    near = remote[:-1]
    lead = 1
    parts = [(0, lead), (lead, per_dev)] if per_dev > lead else [(0, lead)]

    low_part = jnp.dot(inputs, lr_u, preferred_element_type=F32)
    for s in reversed(near[1:] + far):
        env[f"x{s}"] = to_partner(inputs, s)
    joined = jnp.concatenate([cotangent[:, : lead * group], inputs], axis=1)
    for d in others:
        env[f"in{d}"] = rolled(joined, "dp", d)

    def cut_rest():
        pieces = [cotangent[:, lead * group :]] if per_dev > lead else []
        pieces += [env[f"x{s}"] for s in far]
        env["cut"] = jnp.concatenate(pieces, axis=1) if len(pieces) > 1 else pieces[0]

    def send_rest(value):
        piece = tie(env["cut"], value)[0]
        for d in others:
            env[f"rest{d}"] = rolled(piece, "dp", d)

    def low_hooks(step, value):
        if step == "scatter1":
            value = pin(value, *[f"x{s}" for s in near[1:] + far])
            cut_rest()
        if step == "far":
            value = pin(value, *each("in"), "cut")
        return value

    low = sum_far(scatter_near(low_part, "feat", low_hooks, False), "feat", low_hooks)
    for s in near[:1]:
        env[f"x{s}"] = to_partner(tie(inputs, low)[0], s)
    for d in others:
        env[f"low{d}"] = rolled(low, "dp", d)
    low = gather_near(low, "feat", False)
    for d in others:
        env[f"cot{d}0"] = env[f"in{d}"]
        env[f"in{d}"] = env[f"in{d}"][:, lead * group :]
        for s in near[1:]:
            env[f"xo{d}{s}"] = to_partner(tie(env[f"in{d}"], low)[0], s)
    send_rest(env["low1"] if others else low)
    low = pin(low, *[f"x{s}" for s in remote])

    def x_blocks(base_block, prefix):
        arrays = [env.get(f"{prefix}{s}", base_block) for s in range(sections)]
        return arrays, [column(tokens, width, flip) for flip in flips]

    arrays, specs = x_blocks(inputs, "x")
    term_specs = [column(tokens, width, flip) for flip in flips]
    out = call(
        functools.partial(forward_kernel, [1] * sections),
        per_dev,
        specs + [tile_spec(), low_spec, row(rank, group), row(tokens, group)],
        [row(tokens, group), row(tokens, group), resident(tokens, rank)] + term_specs,
        [wide, wide, jax.ShapeDtypeStruct((tokens, rank), F32)]
        + [pltpu.HBM(narrow.shape, BF)] * sections,
        (1000, 1000),
        name="forward",
    )(*arrays, in_hbm(bfly), low, lr_v, in_hbm(cotangent))
    activated, d_pre, d_low_part = out[:3]
    terms = list(out[3:])
    for d in others:
        env[f"low{d}"] = gather_near(tie(env[f"low{d}"], d_low_part)[0], "feat", False)

    def send_terms(value, which):
        for s in reversed(which):
            env[f"t{s}"] = to_partner(tie(terms[s], value)[0], s)

    def d_low_hooks(step, value):
        if step == "scatter":
            for d in others:
                for s in near[:1]:
                    env[f"xo{d}{s}"] = to_partner(tie(env[f"in{d}"], value)[0], s)
        if step == "far":
            send_terms(value, near[1:] + far)
        return value

    d_low_part = pin(d_low_part, *each("xo", *near[1:]))
    d_low = sum_far(scatter_near(d_low_part, "feat", d_low_hooks, True), "feat", d_low_hooks)
    d_low = gather_near(d_low, "feat", True)
    for d in others:
        env[f"d_low{d}"] = rolled(d_low, "dp", d)

    grads = []
    for d in [0, *others] if data_groups == 1 or data_groups > 2 else [1]:
        own, other = d == 0 or data_groups == 2, d > 0
        last = scale if d == data_groups - 1 else 1.0
        operands, blocks = [], []
        if own:
            operands += arrays + [low, d_pre]
            blocks += specs + [low_spec, row(tokens, group)]
        if other:
            x_others, x_specs = x_blocks(env[f"in{d}"], f"xo{d}")
            for s in far:
                x_others[s] = env[f"rest{d}"]
                x_specs[s] = column(tokens, width, 0, (per_dev - lead) * group // width)
            cots = [in_hbm(a) for a in (env[f"cot{d}0"], env[f"rest{d}"])[: len(parts)]]
            operands += x_others + [in_hbm(bfly), env[f"low{d}"], lr_v] + cots
            blocks += x_specs + [tile_spec(), low_spec, row(rank, group)]
            blocks += [clipped(tokens, group, p[0], p[1] - p[0]) for p in parts]
        count = len(operands)
        grads = call(
            functools.partial(
                weight_grad_kernel, sections, own, other, [p[0] for p in parts], last
            ),
            per_dev,
            blocks + ([tile_spec(), row(rank, group)] if grads else []),
            [tile_spec(), row(rank, group)],
            [tile_shape, v_shape],
            (1000, 1000),
            aliases={count: 0, count + 1: 1} if grads else None,
            name="weight_grad",
        )(*operands, *grads)
    d_bfly, d_v = grads

    send_terms(d_low, [s for s in remote if f"t{s}" not in env])
    d_low, d_v = tie(d_low, d_v)
    last_arrays = [env.get(f"t{s}", terms[s]) for s in range(sections)] + [d_low, lr_u, inputs]
    for d in others:
        last_arrays += [env[f"in{d}"], env[f"d_low{d}"]]
    d_inputs, d_u = call(
        functools.partial(finish_kernel, sections, data_groups - 1, scale),
        1,
        [resident(*a.shape) for a in last_arrays],
        [resident(*narrow.shape), resident(*lr_u.shape)],
        [narrow, jax.ShapeDtypeStruct(lr_u.shape, F32)],
        (1000, 1000),
        name="finish",
    )(*last_arrays)
    return activated, d_inputs, d_bfly, d_u, d_v


def solution(mesh):
    return jax.shard_map(
        local,
        mesh=mesh,
        in_specs=(
            P("dp", "feat"),
            P("feat", None, None, None),
            P("feat", None),
            P(None, "feat"),
            P("dp", "feat"),
        ),
        out_specs=(
            P("dp", "feat"),
            P("dp", "feat"),
            P("feat", None, None, None),
            P("feat", None),
            P(None, "feat"),
        ),
        check_vma=False,
    )
```

time: 130 us -> 117 us (0.900)
  waiting for transfers between devices: 45.6 us -> 37.1 us
  Pallas kernels: 32.2 us -> 28.6 us
  starting transfers between devices: 31.3 us -> 34.2 us
  matrix products: 3.52 us -> 1.4 us
  local copies, waits for them, and re-layouts: 9.67 us -> 7.72 us
    ppermute x5 -> x4, waiting for transfers between devices: 12.6 us -> 0.4 us  [rolled(): lax.ppermute(block, axis, [(i, (i + shift) % count) for i in range(count)])]
    pallas_call x3 -> x2, Pallas kernels: 21 us -> 16.5 us  [the longest x1 14.9 us: local(): call(functools.partial(weight_grad_kernel, sections, own, other, [p[0] fo...]
    ppermute x27 -> x31, starting transfers between devices: 25.9 us -> 29.6 us  [crossed(): return lax.ppermute(block, axis, [(i, i ^ mask) for i in range(count)])]
    unnamed x31 -> x26, local copies, waits for them, and re-layouts: 6.88 us -> 3.25 us
    ppermute x27 -> x31, waiting for transfers between devices: 33 us -> 36.7 us  [crossed(): return lax.ppermute(block, axis, [(i, i ^ mask) for i in range(count)])]
    concatenate x6 -> x4, other arithmetic: 0.74 us -> 3.09 us  [the longest x1 3.03 us: cut_rest(): jnp.concatenate(pieces, axis=1)]
    dot_general x3 -> x0, matrix products: 2.16 us -> none  [the longest x1 1.49 us: nt(): lax.dot_general(a, b, (((1,), (1,)), ((), ())), preferred_element_type=F32)]
    add x4 -> x2, other arithmetic: 2 us -> 0.04 us  [scatter_half(): return keep + crossed(send.astype(BF), axis, 1 << bit).astype(F32)]
  transfers between devices with their start and end apart: 32 -> 35, of which waited for: 14 -> 13; matrix products, arithmetic and copies ran while one was open for 9% -> 10% of each run, Pallas kernels for 25% -> 23%
where the time goes in v3:
time: 117 us; the launch traced here: 116 us
  waiting for transfers between devices  37.1 us (32%)
  starting transfers between devices  34.2 us (29%)
  Pallas kernels  28.6 us (24%)
  local copies, waits for them, and re-layouts  7.72 us (7%)
  other arithmetic  6.23 us (5%)
  matrix products  1.4 us (1%)
    ppermute x31, waiting for transfers between devices, crossed(): return lax.ppermute(block, axis, [(i, i ^ mask) for i in range(count)])  36.7 us
    ppermute x31, starting transfers between devices, crossed(): return lax.ppermute(block, axis, [(i, i ^ mask) for i in range(count)])  29.6 us
    pallas_call x1, Pallas kernels, local(): call(functools.partial(weight_grad_kernel, sections, own, other, [p[0] fo...  14.9 us
    pallas_call x1, Pallas kernels, local(): call(functools.partial(forward_kernel, [1] * sections), per_dev, specs +...  12 us
    ppermute x4, starting transfers between devices, rolled(): lax.ppermute(block, axis, [(i, (i + shift) % count) for i in range(count)])  4.61 us
    unnamed x26, local copies, waits for them, and re-layouts  3.25 us
    concatenate x1, other arithmetic, cut_rest(): jnp.concatenate(pieces, axis=1)  3.03 us
    slice x1, local copies, waits for them, and re-layouts, cut_rest(): pieces = [cotangent[:, lead * group:]] if per_dev > lead else []  2.65 us
  transfers between devices with their start and end apart: 35, of which 13 were waited for; matrix products, arithmetic and copies ran while one was open for 10% of the time, Pallas kernels for 23%

profile of v3, /device:TPU:0, one launch (start us, length us, event | category | flops | bytes accessed | tf_op | source)
XLA Modules:
  0.0 116.1 jit_solution(10187652495446213619)
XLA Ops:
  0.7 3.0 %collective-permute-start.2 = (bf16[512,512]{1,0:T(8,128)(2,1)}, bf16[512,512]{1,0:T(8,128)(2,1)S(1)}, u32[]{:S(2)}, u32[]{:S(2)}) collective-permute-start(bf16[512,512]{1,0:T(8,128)(2,1)} %refs_9_.3), channel_id=1, source_target_pairs={{0,2},{1,3},{2,0},{3,1},{4,6},{5,7},{6,4},{7,5},{8,10},{9,11},{10,... | collective-permute-start | bytes 1572872 | tf_op jit(solution)/shard_map/ppermute | solution.py:20
  3.7 1.6 %collective-permute-start.3 = (bf16[512,512]{1,0:T(8,128)(2,1)}, bf16[512,512]{1,0:T(8,128)(2,1)S(1)}, u32[]{:S(2)}, u32[]{:S(2)}) collective-permute-start(bf16[512,512]{1,0:T(8,128)(2,1)} %refs_9_.3), channel_id=1, source_target_pairs={{0,4},{1,5},{2,6},{3,7},{4,0},{5,1},{6,2},{7,3},{8,12},{9,13},{10,... | collective-permute-start | bytes 1572872 | tf_op jit(solution)/shard_map/ppermute | solution.py:20
  5.3 2.6 %collective-permute-start.4 = (bf16[512,512]{1,0:T(8,128)(2,1)}, bf16[512,512]{1,0:T(8,128)(2,1)S(1)}, u32[]{:S(2)}, u32[]{:S(2)}) collective-permute-start(bf16[512,512]{1,0:T(8,128)(2,1)} %refs_9_.3), channel_id=1, source_target_pairs={{0,8},{1,9},{2,10},{3,11},{4,12},{5,13},{6,14},{7,15},{8,0},{9,1},... | collective-permute-start | bytes 1572872 | tf_op jit(solution)/shard_map/ppermute | solution.py:20
  7.9 1.4 %fusion.1 = f32[512,256]{1,0:T(8,128)S(1)} fusion(bf16[512,512]{1,0:T(8,128)(2,1)} %refs_9_.3, bf16[512,256]{1,0:T(8,128)(2,1)} %refs_8_.1), kind=kOutput, calls=%fused_computation.40 | convolution fusion | flops 134217728 | bytes 1310720 | tf_op jit(solution)/shard_map/dot_general | solution.py:268
  9.4 1.1 pad_maximum_fusion.1
  10.5 1.5 %collective-permute-start.8 = (bf16[512,1024]{1,0:T(8,128)(2,1)}, bf16[512,1024]{1,0:T(8,128)(2,1)}, u32[]{:S(2)}, u32[]{:S(2)}) collective-permute-start(bf16[512,1024]{1,0:T(8,128)(2,1)} %pad_maximum_fusion.1), channel_id=1, source_target_pairs={{0,16},{16,0},{1,17},{17,1},{2,18},{18,2},{3,19},{19,3},{4,20},{20... | collective-permute-start | bytes 3145736 | tf_op jit(solution)/shard_map/ppermute | solution.py:25
  12.6 2.7 %slice.10 = bf16[512,1536]{1,0:T(8,128)(2,1)} slice(bf16[512,2048]{1,0:T(8,128)(2,1)} %refs_10_.1), slice={[0:512], [512:2048]} | slice | bytes 3145728 | tf_op jit(solution)/shard_map/slice | solution.py:276
  15.3 1.9 %collective-permute-done.1 = bf16[128,256]{1,0:T(8,128)(2,1)S(1)} collective-permute-done((bf16[128,256]{1,0:T(8,128)(2,1)S(1)}, bf16[128,256]{1,0:T(8,128)(2,1)S(1)}, u32[]{:S(2)}, u32[]{:S(2)}) %collective-permute-start.1) | collective-permute-done | bytes 65568 | tf_op jit(solution)/shard_map/ppermute | solution.py:20
  17.3 11.1 %collective-permute-done.3.refs_4_ = bf16[512,512]{1,0:T(8,128)(2,1)S(1)} collective-permute-done((bf16[512,512]{1,0:T(8,128)(2,1)}, bf16[512,512]{1,0:T(8,128)(2,1)S(1)}, u32[]{:S(2)}, u32[]{:S(2)}) %collective-permute-start.3) | collective-permute-done | bytes 524320 | tf_op jit(solution)/shard_map/ppermute | solution.py:20
  28.4 2.4 %collective-permute-done.4.refs_5_ = bf16[512,512]{1,0:T(8,128)(2,1)S(1)} collective-permute-done((bf16[512,512]{1,0:T(8,128)(2,1)}, bf16[512,512]{1,0:T(8,128)(2,1)S(1)}, u32[]{:S(2)}, u32[]{:S(2)}) %collective-permute-start.4) | collective-permute-done | bytes 524320 | tf_op jit(solution)/shard_map/ppermute | solution.py:20
  31.3 2.7 %collective-permute-start.6 = (bf16[128,256]{1,0:T(8,128)(2,1)S(1)}, bf16[128,256]{1,0:T(8,128)(2,1)S(1)}, u32[]{:S(2)}, u32[]{:S(2)}) collective-permute-start(bf16[128,256]{1,0:T(8,128)(2,1)S(1)} %convert_element_type.64), channel_id=1, source_target_pairs={{0,8},{1,9},{2,10},{3,11},{4,12},{5,13},{6,14},{7,15},{8,0},{9,1},... | collective-permute-start | bytes 196616 | tf_op jit(solution)/shard_map/ppermute | solution.py:20
  33.9 1.3 %collective-permute-start.7 = (bf16[128,256]{1,0:T(8,128)(2,1)S(1)}, bf16[128,256]{1,0:T(8,128)(2,1)S(1)}, u32[]{:S(2)}, u32[]{:S(2)}) collective-permute-start(bf16[128,256]{1,0:T(8,128)(2,1)S(1)} %convert_element_type.64), channel_id=1, source_target_pairs={{0,12},{1,13},{2,14},{3,15},{4,8},{5,9},{6,10},{7,11},{8,4},{9,5},... | collective-permute-start | bytes 196616 | tf_op jit(solution)/shard_map/ppermute | solution.py:20
  35.2 3.0 %pad_maximum_fusion = bf16[512,2048]{1,0:T(8,128)(2,1)} fusion(bf16[512,512]{1,0:T(8,128)(2,1)S(1)} %collective-permute-done.4.refs_5_, bf16[512,1536]{1,0:T(8,128)(2,1)} %slice.10), kind=kLoop, calls=%fused_computation | loop fusion | flops 4194304 | bytes 4194304 | tf_op jit(solution)/shard_map/concatenate | solution.py:278
  38.3 1.7 %collective-permute-done.7 = bf16[128,256]{1,0:T(8,128)(2,1)S(1)} collective-permute-done((bf16[128,256]{1,0:T(8,128)(2,1)S(1)}, bf16[128,256]{1,0:T(8,128)(2,1)S(1)}, u32[]{:S(2)}, u32[]{:S(2)}) %collective-permute-start.7) | collective-permute-done | bytes 65568 | tf_op jit(solution)/shard_map/ppermute | solution.py:20
  40.1 1.6 %collective-permute-start.29 = (bf16[128,256]{1,0:T(8,128)(2,1)S(1)}, bf16[128,256]{1,0:T(8,128)(2,1)S(1)}, u32[]{:S(2)}, u32[]{:S(2)}) collective-permute-start(bf16[128,256]{1,0:T(8,128)(2,1)S(1)} %convert_add_fusion.3), channel_id=1, source_target_pairs={{0,16},{16,0},{1,17},{17,1},{2,18},{18,2},{3,19},{19,3},{4,20},{20... | collective-permute-start | bytes 196616 | tf_op jit(solution)/shard_map/ppermute | solution.py:25
  42.1 1.6 %collective-permute-start.9 = (bf16[128,256]{1,0:T(8,128)(2,1)S(1)}, bf16[128,256]{1,0:T(8,128)(2,1)S(1)}, u32[]{:S(2)}, u32[]{:S(2)}) collective-permute-start(bf16[128,256]{1,0:T(8,128)(2,1)S(1)} %convert_add_fusion.3), channel_id=1, source_target_pairs={{0,1},{1,0},{2,3},{3,2},{4,5},{5,4},{6,7},{7,6},{8,9},{9,8},{10,11... | collective-permute-start | bytes 196616 | tf_op jit(solution)/shard_map/ppermute | solution.py:20
  43.8 1.1 slice.11.refs_9_.refs_10_.refs_15_
  46.6 1.3 %collective-permute-start.13 = (bf16[512,512]{1,0:T(8,128)(2,1)S(1)}, bf16[512,512]{1,0:T(8,128)(2,1)}, u32[]{:S(2)}, u32[]{:S(2)}) collective-permute-start(bf16[512,512]{1,0:T(8,128)(2,1)S(1)} %slice.11.refs_9_.refs_10_.refs_15_), channel_id=1, source_target_pairs={{0,2},{1,3},{2,0},{3,1},{4,6},{5,7},{6,4},{7,5},{8,10},{9,11},{10,... | collective-permute-start | bytes 1572872 | tf_op jit(solution)/shard_map/ppermute | solution.py:20
  48.0 1.0 copy-done.5
  49.0 12.0 %forward.1 = (bf16[512,2048]{1,0:T(8,128)(2,1)}, bf16[512,2048]{1,0:T(8,128)(2,1)S(1)}, f32[512,256]{1,0:T(8,128)S(1)}, bf16[512,512]{1,0:T(8,128)(2,1)}, bf16[5...) custom-call(bf16[512,512]{1,0:T(8,128)(2,1)S(1)} %copy-done, ...), custom_call_target="tpu_custom_call" | custom-call | flops 1000 | bytes 1000 | tf_op jit(solution)/shard_map/forward/pallas_call | solution.py:313
  61.0 1.3 %copy-done.2 = bf16[512,2048]{1,0:T(8,128)(2,1)} copy-done((bf16[512,2048]{1,0:T(8,128)(2,1)}, bf16[512,2048]{1,0:T(8,128)(2,1)S(1)}, u32[]{:S(2)}) %copy-start.2) | copy-done | bytes 2097176
  65.7 3.2 %collective-permute-done.16 = bf16[128,256]{1,0:T(8,128)(2,1)S(1)} collective-permute-done((bf16[128,256]{1,0:T(8,128)(2,1)}, bf16[128,256]{1,0:T(8,128)(2,1)S(1)}, u32[]{:S(2)}, u32[]{:S(2)}) %collective-permute-start.16) | collective-permute-done | bytes 65568 | tf_op jit(solution)/shard_map/ppermute | solution.py:20
  70.7 2.1 %collective-permute-start.18 = (bf16[128,256]{1,0:T(8,128)(2,1)S(1)}, bf16[128,256]{1,0:T(8,128)(2,1)S(1)}, u32[]{:S(2)}, u32[]{:S(2)}) collective-permute-start(bf16[128,256]{1,0:T(8,128)(2,1)S(1)} %get-tuple-element.85), channel_id=1, source_target_pairs={{0,4},{1,5},{2,6},{3,7},{4,0},{5,1},{6,2},{7,3},{8,12},{9,13},{10,... | collective-permute-start | bytes 196616 | tf_op jit(solution)/shard_map/ppermute | solution.py:20
  72.8 2.4 %collective-permute-start.20 = (bf16[128,256]{1,0:T(8,128)(2,1)S(1)}, bf16[128,256]{1,0:T(8,128)(2,1)S(1)}, u32[]{:S(2)}, u32[]{:S(2)}) collective-permute-start(bf16[128,256]{1,0:T(8,128)(2,1)S(1)} %get-tuple-element.85), channel_id=1, source_target_pairs={{0,12},{1,13},{2,14},{3,15},{4,8},{5,9},{6,10},{7,11},{8,4},{9,5},... | collective-permute-start | bytes 196616 | tf_op jit(solution)/shard_map/ppermute | solution.py:20
  75.5 5.3 %collective-permute-done.19 = bf16[128,256]{1,0:T(8,128)(2,1)S(1)} collective-permute-done((bf16[128,256]{1,0:T(8,128)(2,1)S(1)}, bf16[128,256]{1,0:T(8,128)(2,1)S(1)}, u32[]{:S(2)}, u32[]{:S(2)}) %collective-permute-start.19) | collective-permute-done | bytes 65568 | tf_op jit(solution)/shard_map/ppermute | solution.py:20
  83.2 2.7 %collective-permute-done.22 = bf16[128,256]{1,0:T(8,128)(2,1)S(1)} collective-permute-done((bf16[128,256]{1,0:T(8,128)(2,1)S(1)}, bf16[128,256]{1,0:T(8,128)(2,1)S(1)}, u32[]{:S(2)}, u32[]{:S(2)}) %collective-permute-start.22) | collective-permute-done | bytes 65568 | tf_op jit(solution)/shard_map/ppermute | solution.py:20
  87.6 1.8 %collective-permute-start.27 = (bf16[512,512]{1,0:T(8,128)(2,1)}, bf16[512,512]{1,0:T(8,128)(2,1)S(1)}, u32[]{:S(2)}, u32[]{:S(2)}) collective-permute-start(bf16[512,512]{1,0:T(8,128)(2,1)} %get-tuple-element.70), channel_id=1, source_target_pairs={{0,8},{1,9},{2,10},{3,11},{4,12},{5,13},{6,14},{7,15},{8,0},{9,1},... | collective-permute-start | bytes 1572872 | tf_op jit(solution)/shard_map/ppermute | solution.py:20
  89.4 1.7 %collective-permute-done.32 = bf16[128,256]{1,0:T(8,128)(2,1)S(1)} collective-permute-done((bf16[128,256]{1,0:T(8,128)(2,1)}, bf16[128,256]{1,0:T(8,128)(2,1)S(1)}, u32[]{:S(2)}, u32[]{:S(2)}) %collective-permute-start.32) | collective-permute-done | bytes 65568 | tf_op jit(solution)/shard_map/ppermute | solution.py:20
  91.1 1.7 %collective-permute-start.26 = (bf16[512,512]{1,0:T(8,128)(2,1)}, bf16[512,512]{1,0:T(8,128)(2,1)S(1)}, u32[]{:S(2)}, u32[]{:S(2)}) collective-permute-start(bf16[512,512]{1,0:T(8,128)(2,1)} %get-tuple-element.68), channel_id=1, source_target_pairs={{0,4},{1,5},{2,6},{3,7},{4,0},{5,1},{6,2},{7,3},{8,12},{9,13},{10,... | collective-permute-start | bytes 1572872 | tf_op jit(solution)/shard_map/ppermute | solution.py:20
  94.8 14.9 %weight_grad.1 = (f32[4,7,128,512]{3,2,1,0:T(8,128)}, f32[256,2048]{1,0:T(8,128)}) custom-call(bf16[512,512]{1,0:T(8,128)(2,1)S(1)} %copy-done, bf16[512,512]{1,0:T(8,128)(2,1)S(1)} %copy-done, bf16[512,512]{1,0:T(8,128)(2,1)} %collective-permute-done.12.refs_2_, bf16[512,512]{1,0:T(8,128)(2,1)S(1)} %collective-permute-done.2.refs_3_, ...), custom_call_target="tpu_custom_call" | custom-call | flops 1000 | bytes 1000 | tf_op jit(solution)/shard_map/weight_grad/pallas_call | solution.py:365
  109.7 4.7 %collective-permute-done.27.refs_5_ = bf16[512,512]{1,0:T(8,128)(2,1)S(1)} collective-permute-done((bf16[512,512]{1,0:T(8,128)(2,1)}, bf16[512,512]{1,0:T(8,128)(2,1)S(1)}, u32[]{:S(2)}, u32[]{:S(2)}) %collective-permute-start.27) | collective-permute-done | bytes 524320 | tf_op jit(solution)/shard_map/ppermute | solution.py:20
  114.4 1.7 %finish.1 = (bf16[512,512]{1,0:T(8,128)(2,1)}, f32[512,256]{1,0:T(8,128)}) custom-call(bf16[512,512]{1,0:T(8,128)(2,1)S(1)} %copy-done.8, bf16[512,512]{1,0:T(8,128)(2,1)S(1)} %copy-done.9, bf16[512,512]{1,0:T(8,128)(2,1)S(1)} %collective-permute-done.24.refs_2_, bf16[512,512]{1,0:T(8,128)(2,1)S(1)} %collective-permute-done.25.refs_3_, ...), custom_call_target="tpu_custom_call" | custom-call | flops 1000 | bytes 1000 | tf_op jit(solution)/shard_map/finish/pallas_call | solution.py:384
  (89 shorter events, 14.8 us)
Async XLA Ops:
  0.7 16.6 %collective-permute-start.2 = (bf16[512,512]{1,0:T(8,128)(2,1)}, bf16[512,512]{1,0:T(8,128)(2,1)S(1)}, u32[]{:S(2)}, u32[]{:S(2)}) collective-permute-start(bf16[512,512]{1,0:T(8,128)(2,1)} %refs_9_.3), channel_id=1, source_target_pairs={{0,2},{1,3},{2,0},{3,1},{4,6},{5,7},{6,4},{7,5},{8,10},{9,11},{10,... | collective-permute-start | bytes 1572872 | tf_op jit(solution)/shard_map/ppermute | solution.py:20
  3.7 24.7 %collective-permute-start.3 = (bf16[512,512]{1,0:T(8,128)(2,1)}, bf16[512,512]{1,0:T(8,128)(2,1)S(1)}, u32[]{:S(2)}, u32[]{:S(2)}) collective-permute-start(bf16[512,512]{1,0:T(8,128)(2,1)} %refs_9_.3), channel_id=1, source_target_pairs={{0,4},{1,5},{2,6},{3,7},{4,0},{5,1},{6,2},{7,3},{8,12},{9,13},{10,... | collective-permute-start | bytes 1572872 | tf_op jit(solution)/shard_map/ppermute | solution.py:20
  5.3 25.5 %collective-permute-start.4 = (bf16[512,512]{1,0:T(8,128)(2,1)}, bf16[512,512]{1,0:T(8,128)(2,1)S(1)}, u32[]{:S(2)}, u32[]{:S(2)}) collective-permute-start(bf16[512,512]{1,0:T(8,128)(2,1)} %refs_9_.3), channel_id=1, source_target_pairs={{0,8},{1,9},{2,10},{3,11},{4,12},{5,13},{6,14},{7,15},{8,0},{9,1},... | collective-permute-start | bytes 1572872 | tf_op jit(solution)/shard_map/ppermute | solution.py:20
  10.5 29.5 %collective-permute-start.8 = (bf16[512,1024]{1,0:T(8,128)(2,1)}, bf16[512,1024]{1,0:T(8,128)(2,1)}, u32[]{:S(2)}, u32[]{:S(2)}) collective-permute-start(bf16[512,1024]{1,0:T(8,128)(2,1)} %pad_maximum_fusion.1), channel_id=1, source_target_pairs={{0,16},{16,0},{1,17},{17,1},{2,18},{18,2},{3,19},{19,3},{4,20},{20... | collective-permute-start | bytes 3145736 | tf_op jit(solution)/shard_map/ppermute | solution.py:25
  12.1 5.2 %collective-permute-start.1 = (bf16[128,256]{1,0:T(8,128)(2,1)S(1)}, bf16[128,256]{1,0:T(8,128)(2,1)S(1)}, u32[]{:S(2)}, u32[]{:S(2)}) collective-permute-start(bf16[128,256]{1,0:T(8,128)(2,1)S(1)} %dynamic-slice_convert_fusion.4), channel_id=1, source_target_pairs={{0,2},{1,3},{2,0},{3,1},{4,6},{5,7},{6,4},{7,5},{8,10},{9,11},{10,... | collective-permute-start | bytes 196616 | tf_op jit(solution)/shard_map/ppermute | solution.py:20
  30.8 7.5 %collective-permute-start.5 = (bf16[128,256]{1,0:T(8,128)(2,1)S(1)}, bf16[128,256]{1,0:T(8,128)(2,1)S(1)}, u32[]{:S(2)}, u32[]{:S(2)}) collective-permute-start(bf16[128,256]{1,0:T(8,128)(2,1)S(1)} %convert_element_type.64), channel_id=1, source_target_pairs={{0,4},{1,5},{2,6},{3,7},{4,0},{5,1},{6,2},{7,3},{8,12},{9,13},{10,... | collective-permute-start | bytes 196616 | tf_op jit(solution)/shard_map/ppermute | solution.py:20
  31.3 7.0 %collective-permute-start.6 = (bf16[128,256]{1,0:T(8,128)(2,1)S(1)}, bf16[128,256]{1,0:T(8,128)(2,1)S(1)}, u32[]{:S(2)}, u32[]{:S(2)}) collective-permute-start(bf16[128,256]{1,0:T(8,128)(2,1)S(1)} %convert_element_type.64), channel_id=1, source_target_pairs={{0,8},{1,9},{2,10},{3,11},{4,12},{5,13},{6,14},{7,15},{8,0},{9,1},... | collective-permute-start | bytes 196616 | tf_op jit(solution)/shard_map/ppermute | solution.py:20
  33.9 6.1 %collective-permute-start.7 = (bf16[128,256]{1,0:T(8,128)(2,1)S(1)}, bf16[128,256]{1,0:T(8,128)(2,1)S(1)}, u32[]{:S(2)}, u32[]{:S(2)}) collective-permute-start(bf16[128,256]{1,0:T(8,128)(2,1)S(1)} %convert_element_type.64), channel_id=1, source_target_pairs={{0,12},{1,13},{2,14},{3,15},{4,8},{5,9},{6,10},{7,11},{8,4},{9,5},... | collective-permute-start | bytes 196616 | tf_op jit(solution)/shard_map/ppermute | solution.py:20
  40.1 4.8 %collective-permute-start.29 = (bf16[128,256]{1,0:T(8,128)(2,1)S(1)}, bf16[128,256]{1,0:T(8,128)(2,1)S(1)}, u32[]{:S(2)}, u32[]{:S(2)}) collective-permute-start(bf16[128,256]{1,0:T(8,128)(2,1)S(1)} %convert_add_fusion.3), channel_id=1, source_target_pairs={{0,16},{16,0},{1,17},{17,1},{2,18},{18,2},{3,19},{19,3},{4,20},{20... | collective-permute-start | bytes 196616 | tf_op jit(solution)/shard_map/ppermute | solution.py:25
  41.6 4.9 %collective-permute-start.10 = (bf16[128,256]{1,0:T(8,128)(2,1)S(1)}, bf16[128,256]{1,0:T(8,128)(2,1)S(1)}, u32[]{:S(2)}, u32[]{:S(2)}) collective-permute-start(bf16[128,256]{1,0:T(8,128)(2,1)S(1)} %convert_add_fusion.3), channel_id=1, source_target_pairs={{0,2},{1,3},{2,0},{3,1},{4,6},{5,7},{6,4},{7,5},{8,10},{9,11},{10,... | collective-permute-start | bytes 196616 | tf_op jit(solution)/shard_map/ppermute | solution.py:20
  42.1 4.4 %collective-permute-start.11 = (bf16[128,256]{1,0:T(8,128)(2,1)S(1)}, bf16[128,256]{1,0:T(8,128)(2,1)S(1)}, u32[]{:S(2)}, u32[]{:S(2)}) collective-permute-start(bf16[128,256]{1,0:T(8,128)(2,1)S(1)} %convert_add_fusion.3), channel_id=1, source_target_pairs={{0,3},{1,2},{2,1},{3,0},{4,7},{5,6},{6,5},{7,4},{8,11},{9,10},{10,... | collective-permute-start | bytes 196616 | tf_op jit(solution)/shard_map/ppermute | solution.py:20
  42.1 4.4 %collective-permute-start.9 = (bf16[128,256]{1,0:T(8,128)(2,1)S(1)}, bf16[128,256]{1,0:T(8,128)(2,1)S(1)}, u32[]{:S(2)}, u32[]{:S(2)}) collective-permute-start(bf16[128,256]{1,0:T(8,128)(2,1)S(1)} %convert_add_fusion.3), channel_id=1, source_target_pairs={{0,1},{1,0},{2,3},{3,2},{4,5},{5,4},{6,7},{7,6},{8,9},{9,8},{10,11... | collective-permute-start | bytes 196616 | tf_op jit(solution)/shard_map/ppermute | solution.py:20
  43.8 4.2 %collective-permute-start.12 = (bf16[512,512]{1,0:T(8,128)(2,1)S(1)}, bf16[512,512]{1,0:T(8,128)(2,1)}, u32[]{:S(2)}, u32[]{:S(2)}) collective-permute-start(bf16[512,512]{1,0:T(8,128)(2,1)S(1)} %copy-done), channel_id=1, source_target_pairs={{0,1},{1,0},{2,3},{3,2},{4,5},{5,4},{6,7},{7,6},{8,9},{9,8},{10,11... | collective-permute-start | bytes 1572872 | tf_op jit(solution)/shard_map/ppermute | solution.py:20
  44.9 48.4 %collective-permute-start.30 = (bf16[512,2048]{1,0:T(8,128)(2,1)}, bf16[512,2048]{1,0:T(8,128)(2,1)}, u32[]{:S(2)}, u32[]{:S(2)}) collective-permute-start(bf16[512,2048]{1,0:T(8,128)(2,1)} %pad_maximum_fusion), channel_id=1, source_target_pairs={{0,16},{16,0},{1,17},{17,1},{2,18},{18,2},{3,19},{19,3},{4,20},{20... | collective-permute-start | bytes 6291464 | tf_op jit(solution)/shard_map/ppermute | solution.py:25
  46.6 15.7 %collective-permute-start.13 = (bf16[512,512]{1,0:T(8,128)(2,1)S(1)}, bf16[512,512]{1,0:T(8,128)(2,1)}, u32[]{:S(2)}, u32[]{:S(2)}) collective-permute-start(bf16[512,512]{1,0:T(8,128)(2,1)S(1)} %slice.11.refs_9_.refs_10_.refs_15_), channel_id=1, source_target_pairs={{0,2},{1,3},{2,0},{3,1},{4,6},{5,7},{6,4},{7,5},{8,10},{9,11},{10,... | collective-permute-start | bytes 1572872 | tf_op jit(solution)/shard_map/ppermute | solution.py:20
  47.9 14.4 %collective-permute-start.14 = (bf16[512,512]{1,0:T(8,128)(2,1)S(1)}, bf16[512,512]{1,0:T(8,128)(2,1)}, u32[]{:S(2)}, u32[]{:S(2)}) collective-permute-start(bf16[512,512]{1,0:T(8,128)(2,1)S(1)} %slice.11.refs_9_.refs_10_.refs_15_), channel_id=1, source_target_pairs={{0,4},{1,5},{2,6},{3,7},{4,0},{5,1},{6,2},{7,3},{8,12},{9,13},{10,... | collective-permute-start | bytes 1572872 | tf_op jit(solution)/shard_map/ppermute | solution.py:20
  63.9 5.1 %collective-permute-start.16 = (bf16[128,256]{1,0:T(8,128)(2,1)}, bf16[128,256]{1,0:T(8,128)(2,1)S(1)}, u32[]{:S(2)}, u32[]{:S(2)}) collective-permute-start(bf16[128,256]{1,0:T(8,128)(2,1)} %get-tuple-element.89), channel_id=1, source_target_pairs={{0,2},{1,3},{2,0},{3,1},{4,6},{5,7},{6,4},{7,5},{8,10},{9,11},{10,... | collective-permute-start | bytes 196616 | tf_op jit(solution)/shard_map/ppermute | solution.py:20
  64.9 4.8 %collective-permute-start.17 = (bf16[128,256]{1,0:T(8,128)(2,1)}, bf16[128,256]{1,0:T(8,128)(2,1)}, u32[]{:S(2)}, u32[]{:S(2)}) collective-permute-start(bf16[128,256]{1,0:T(8,128)(2,1)} %get-tuple-element.88), channel_id=1, source_target_pairs={{0,3},{1,2},{2,1},{3,0},{4,7},{5,6},{6,5},{7,4},{8,11},{9,10},{10,... | collective-permute-start | bytes 196616 | tf_op jit(solution)/shard_map/ppermute | solution.py:20
  70.7 4.8 %collective-permute-start.18 = (bf16[128,256]{1,0:T(8,128)(2,1)S(1)}, bf16[128,256]{1,0:T(8,128)(2,1)S(1)}, u32[]{:S(2)}, u32[]{:S(2)}) collective-permute-start(bf16[128,256]{1,0:T(8,128)(2,1)S(1)} %get-tuple-element.85), channel_id=1, source_target_pairs={{0,4},{1,5},{2,6},{3,7},{4,0},{5,1},{6,2},{7,3},{8,12},{9,13},{10,... | collective-permute-start | bytes 196616 | tf_op jit(solution)/shard_map/ppermute | solution.py:20
  72.8 8.1 %collective-permute-start.19 = (bf16[128,256]{1,0:T(8,128)(2,1)S(1)}, bf16[128,256]{1,0:T(8,128)(2,1)S(1)}, u32[]{:S(2)}, u32[]{:S(2)}) collective-permute-start(bf16[128,256]{1,0:T(8,128)(2,1)S(1)} %get-tuple-element.85), channel_id=1, source_target_pairs={{0,8},{1,9},{2,10},{3,11},{4,12},{5,13},{6,14},{7,15},{8,0},{9,1},... | collective-permute-start | bytes 196616 | tf_op jit(solution)/shard_map/ppermute | solution.py:20
  72.8 8.1 %collective-permute-start.20 = (bf16[128,256]{1,0:T(8,128)(2,1)S(1)}, bf16[128,256]{1,0:T(8,128)(2,1)S(1)}, u32[]{:S(2)}, u32[]{:S(2)}) collective-permute-start(bf16[128,256]{1,0:T(8,128)(2,1)S(1)} %get-tuple-element.85), channel_id=1, source_target_pairs={{0,12},{1,13},{2,14},{3,15},{4,8},{5,9},{6,10},{7,11},{8,4},{9,5},... | collective-permute-start | bytes 196616 | tf_op jit(solution)/shard_map/ppermute | solution.py:20
  75.2 17.6 %collective-permute-start.28 = (bf16[512,512]{1,0:T(8,128)(2,1)S(1)}, bf16[512,512]{1,0:T(8,128)(2,1)S(1)}, u32[]{:S(2)}, u32[]{:S(2)}) collective-permute-start(bf16[512,512]{1,0:T(8,128)(2,1)S(1)} %slice.11.refs_9_.refs_10_.refs_15_), channel_id=1, source_target_pairs={{0,1},{1,0},{2,3},{3,2},{4,5},{5,4},{6,7},{7,6},{8,9},{9,8},{10,11... | collective-permute-start | bytes 1572872 | tf_op jit(solution)/shard_map/ppermute | solution.py:20
  81.0 5.0 %collective-permute-start.22 = (bf16[128,256]{1,0:T(8,128)(2,1)S(1)}, bf16[128,256]{1,0:T(8,128)(2,1)S(1)}, u32[]{:S(2)}, u32[]{:S(2)}) collective-permute-start(bf16[128,256]{1,0:T(8,128)(2,1)S(1)} %convert_add_fusion.1), channel_id=1, source_target_pairs={{0,2},{1,3},{2,0},{3,1},{4,6},{5,7},{6,4},{7,5},{8,10},{9,11},{10,... | collective-permute-start | bytes 196616 | tf_op jit(solution)/shard_map/ppermute | solution.py:20
  81.8 4.7 %collective-permute-start.23 = (bf16[128,256]{1,0:T(8,128)(2,1)S(1)}, bf16[128,256]{1,0:T(8,128)(2,1)S(1)}, u32[]{:S(2)}, u32[]{:S(2)}) collective-permute-start(bf16[128,256]{1,0:T(8,128)(2,1)S(1)} %convert_add_fusion.1), channel_id=1, source_target_pairs={{0,3},{1,2},{2,1},{3,0},{4,7},{5,6},{6,5},{7,4},{8,11},{9,10},{10,... | collective-permute-start | bytes 196616 | tf_op jit(solution)/shard_map/ppermute | solution.py:20
  82.8 4.7 %collective-permute-start.31 = (bf16[128,256]{1,0:T(8,128)(2,1)}, bf16[128,256]{1,0:T(8,128)(2,1)S(1)}, u32[]{:S(2)}, u32[]{:S(2)}) collective-permute-start(bf16[128,256]{1,0:T(8,128)(2,1)} %copy-done.12), channel_id=1, source_target_pairs={{0,1},{1,0},{2,3},{3,2},{4,5},{5,4},{6,7},{7,6},{8,9},{9,8},{10,11... | collective-permute-start | bytes 196616 | tf_op jit(solution)/shard_map/ppermute | solution.py:20
  85.9 5.2 %collective-permute-start.32 = (bf16[128,256]{1,0:T(8,128)(2,1)}, bf16[128,256]{1,0:T(8,128)(2,1)S(1)}, u32[]{:S(2)}, u32[]{:S(2)}) collective-permute-start(bf16[128,256]{1,0:T(8,128)(2,1)} %copy-done.12), channel_id=1, source_target_pairs={{0,2},{1,3},{2,0},{3,1},{4,6},{5,7},{6,4},{7,5},{8,10},{9,11},{10,... | collective-permute-start | bytes 196616 | tf_op jit(solution)/shard_map/ppermute | solution.py:20
  86.5 6.3 %collective-permute-start.33 = (bf16[128,256]{1,0:T(8,128)(2,1)}, bf16[128,256]{1,0:T(8,128)(2,1)S(1)}, u32[]{:S(2)}, u32[]{:S(2)}) collective-permute-start(bf16[128,256]{1,0:T(8,128)(2,1)} %copy-done.12), channel_id=1, source_target_pairs={{0,3},{1,2},{2,1},{3,0},{4,7},{5,6},{6,5},{7,4},{8,11},{9,10},{10,... | collective-permute-start | bytes 196616 | tf_op jit(solution)/shard_map/ppermute | solution.py:20
  87.6 26.8 %collective-permute-start.27 = (bf16[512,512]{1,0:T(8,128)(2,1)}, bf16[512,512]{1,0:T(8,128)(2,1)S(1)}, u32[]{:S(2)}, u32[]{:S(2)}) collective-permute-start(bf16[512,512]{1,0:T(8,128)(2,1)} %get-tuple-element.70), channel_id=1, source_target_pairs={{0,8},{1,9},{2,10},{3,11},{4,12},{5,13},{6,14},{7,15},{8,0},{9,1},... | collective-permute-start | bytes 1572872 | tf_op jit(solution)/shard_map/ppermute | solution.py:20
  91.1 23.3 %collective-permute-start.26 = (bf16[512,512]{1,0:T(8,128)(2,1)}, bf16[512,512]{1,0:T(8,128)(2,1)S(1)}, u32[]{:S(2)}, u32[]{:S(2)}) collective-permute-start(bf16[512,512]{1,0:T(8,128)(2,1)} %get-tuple-element.68), channel_id=1, source_target_pairs={{0,4},{1,5},{2,6},{3,7},{4,0},{5,1},{6,2},{7,3},{8,12},{9,13},{10,... | collective-permute-start | bytes 1572872 | tf_op jit(solution)/shard_map/ppermute | solution.py:20
  92.8 21.6 %collective-permute-start.25 = (bf16[512,512]{1,0:T(8,128)(2,1)}, bf16[512,512]{1,0:T(8,128)(2,1)S(1)}, u32[]{:S(2)}, u32[]{:S(2)}) collective-permute-start(bf16[512,512]{1,0:T(8,128)(2,1)} %get-tuple-element.66), channel_id=1, source_target_pairs={{0,2},{1,3},{2,0},{3,1},{4,6},{5,7},{6,4},{7,5},{8,10},{9,11},{10,... | collective-permute-start | bytes 1572872 | tf_op jit(solution)/shard_map/ppermute | solution.py:20
  92.8 21.6 %collective-permute-start.24 = (bf16[512,512]{1,0:T(8,128)(2,1)}, bf16[512,512]{1,0:T(8,128)(2,1)S(1)}, u32[]{:S(2)}, u32[]{:S(2)}) collective-permute-start(bf16[512,512]{1,0:T(8,128)(2,1)} %get-tuple-element.64), channel_id=1, source_target_pairs={{0,1},{1,0},{2,3},{3,2},{4,5},{5,4},{6,7},{7,6},{8,9},{9,8},{10,11... | collective-permute-start | bytes 1572872 | tf_op jit(solution)/shard_map/ppermute | solution.py:20
  93.3 16.4 %collective-permute-start.34 = (bf16[512,256]{1,0:T(8,128)(2,1)S(1)}, bf16[512,256]{1,0:T(8,128)(2,1)S(1)}, u32[]{:S(2)}, u32[]{:S(2)}) collective-permute-start(bf16[512,256]{1,0:T(8,128)(2,1)S(1)} %pad_maximum_fusion.3.refs_7_), channel_id=1, source_target_pairs={{0,16},{16,0},{1,17},{17,1},{2,18},{18,2},{3,19},{19,3},{4,20},{20... | collective-permute-start | bytes 786440 | tf_op jit(solution)/shard_map/ppermute | solution.py:25
  (17 other events, 185.1 us)

commit v4 on v3

--- a/solution.py
+++ b/solution.py
@@ -146,11 +146,12 @@
     def side(x):
         return jnp.concatenate([ref[...] for ref in x], axis=1)
 
-    parts = []
+    blocks, lows, grads = [], [], []
     if own:
-        block = side(take(sections))
-        low, grad = (ref[...] for ref in take(2))
-        parts.append((tn(block, grad), tn(low, grad)))
+        blocks.append(side(take(sections)))
+        low, grad = take(2)
+        lows.append(low[...])
+        grads.append(grad[...])
     if other:
         block = side(take(sections))
         bfly, low, lr_v = take(3)
@@ -163,15 +164,18 @@
             low[...], lr_v[...], preferred_element_type=F32
         )
         _, slope = gelu_parts(pre)
-        grad = (cot.astype(F32) * slope).astype(BF)
-        parts.append((tn(block, grad), tn(low[...], grad)))
+        blocks.append(block)
+        lows.append(low[...])
+        grads.append((cot.astype(F32) * slope).astype(BF))
+    block, low, grad = (
+        a[0] if len(a) == 1 else jnp.concatenate(a, axis=0) for a in (blocks, lows, grads)
+    )
+    total, total_v = tn(block, grad), tn(low, grad)
     if not own:
         d_bfly_in, d_v_in = take(2)
-        parts.append((d_bfly_in[0].reshape(parts[0][0].shape), d_v_in[...]))
+        total = total + d_bfly_in[0].reshape(total.shape)
+        total_v = total_v + d_v_in[...]
     d_bfly, d_v = refs
-    total, total_v = parts[0]
-    for part, part_v in parts[1:]:
-        total, total_v = total + part, total_v + part_v
     d_bfly[0] = (total * scale).reshape(d_bfly.shape[1:])
     d_v[...] = total_v * scale
 
@@ -266,8 +270,10 @@
     parts = [(0, lead), (lead, per_dev)] if per_dev > lead else [(0, lead)]
 
     low_part = jnp.dot(inputs, lr_u, preferred_element_type=F32)
-    for s in reversed(near[1:] + far):
+    for s in reversed(near[2:] + far):
         env[f"x{s}"] = to_partner(inputs, s)
+    for s in near[1:2]:
+        env[f"x{s}"] = to_partner(tie(inputs, low_part)[0], s)
     joined = jnp.concatenate([cotangent[:, : lead * group], inputs], axis=1)
     for d in others:
         env[f"in{d}"] = rolled(joined, "dp", d)
@@ -315,11 +321,12 @@
         per_dev,
         specs + [tile_spec(), low_spec, row(rank, group), row(tokens, group)],
         [row(tokens, group), row(tokens, group), resident(tokens, rank)] + term_specs,
-        [wide, wide, jax.ShapeDtypeStruct((tokens, rank), F32)]
+        [pltpu.HBM(wide.shape, BF)] * 2
+        + [pltpu.HBM((tokens, rank), F32)]
         + [pltpu.HBM(narrow.shape, BF)] * sections,
         (1000, 1000),
         name="forward",
-    )(*arrays, in_hbm(bfly), low, lr_v, in_hbm(cotangent))
+    )(*[a if s in near[:1] else in_hbm(a) for s, a in enumerate(arrays)], in_hbm(bfly), low, lr_v, in_hbm(cotangent))
     activated, d_pre, d_low_part = out[:3]
     terms = list(out[3:])
     for d in others:
@@ -340,7 +347,7 @@
 
     d_low_part = pin(d_low_part, *each("xo", *near[1:]))
     d_low = sum_far(scatter_near(d_low_part, "feat", d_low_hooks, True), "feat", d_low_hooks)
-    d_low = gather_near(d_low, "feat", True)
+    d_low = gather_near(pin(d_low, *each("low")), "feat", True)
     for d in others:
         env[f"d_low{d}"] = rolled(d_low, "dp", d)
 
@@ -373,7 +380,7 @@
             (1000, 1000),
             aliases={count: 0, count + 1: 1} if grads else None,
             name="weight_grad",
-        )(*operands, *grads)
+        )(*map(in_hbm, operands), *grads)
     d_bfly, d_v = grads
 
     send_terms(d_low, [s for s in remote if f"t{s}" not in env])

time: 117 us -> 110 us (0.940)
  local copies, waits for them, and re-layouts: 7.72 us -> 2.27 us
  starting transfers between devices: 34.2 us -> 36.6 us
  Pallas kernels: 28.6 us -> 27.1 us
    ppermute x31, waiting for transfers between devices: 36.7 us -> 29.3 us  [crossed(): return lax.ppermute(block, axis, [(i, i ^ mask) for i in range(count)])]
    ppermute x4, waiting for transfers between devices: 0.4 us -> 6.7 us  [rolled(): lax.ppermute(block, axis, [(i, (i + shift) % count) for i in range(count)])]
    unnamed x26 -> x38, local copies, waits for them, and re-layouts: 3.25 us -> 0.09 us
    slice x1 -> x2, local copies, waits for them, and re-layouts: 2.65 us -> 0.01 us  [cut_rest(): pieces = [cotangent[:, lead * group:]] if per_dev > lead else []]
    pallas_call x1, Pallas kernels: 14.9 us -> 13.3 us  [local(): call(functools.partial(weight_grad_kernel, sections, own, other, [p[0] fo...]
    concatenate x1, other arithmetic: 3.03 us -> 1.63 us  [cut_rest(): jnp.concatenate(pieces, axis=1)]
    ppermute x4, starting transfers between devices: 4.61 us -> 5.97 us  [rolled(): lax.ppermute(block, axis, [(i, (i + shift) % count) for i in range(count)])]
  transfers between devices with their start and end apart: 35 -> 35, of which waited for: 13 -> 11; matrix products, arithmetic and copies ran while one was open for 10% -> 8% of each run, Pallas kernels for 23% -> 23%
where the time goes in v4:
time: 110 us
  starting transfers between devices  36.6 us (33%)
  waiting for transfers between devices  36 us (33%)
  Pallas kernels  27.1 us (25%)
  other arithmetic  5.73 us (5%)
  local copies, waits for them, and re-layouts  2.27 us (2%)
  matrix products  1.4 us (1%)
    ppermute x31, starting transfers between devices, crossed(): return lax.ppermute(block, axis, [(i, i ^ mask) for i in range(count)])  30.7 us
    ppermute x31, waiting for transfers between devices, crossed(): return lax.ppermute(block, axis, [(i, i ^ mask) for i in range(count)])  29.3 us
    pallas_call x1, Pallas kernels, local(): call(functools.partial(weight_grad_kernel, sections, own, other, [p[0] fo...  13.3 us
    pallas_call x1, Pallas kernels, local(): call(functools.partial(forward_kernel, [1] * sections), per_dev, specs +...  12.1 us
    ppermute x4, waiting for transfers between devices, rolled(): lax.ppermute(block, axis, [(i, (i + shift) % count) for i in range(count)])  6.7 us
    ppermute x4, starting transfers between devices, rolled(): lax.ppermute(block, axis, [(i, (i + shift) % count) for i in range(count)])  5.97 us
  transfers between devices with their start and end apart: 35, of which 11 were waited for; matrix products, arithmetic and copies ran while one was open for 8% of the time, Pallas kernels for 23%

profile of v4, /device:TPU:0, one launch (start us, length us, event | category | flops | bytes accessed | tf_op | source)
XLA Modules:
  0.0 110.2 jit_solution(10985920688968926029)
XLA Ops:
  0.7 3.1 %collective-permute-start.3 = (bf16[512,512]{1,0:T(8,128)(2,1)}, bf16[512,512]{1,0:T(8,128)(2,1)}, u32[]{:S(2)}, u32[]{:S(2)}) collective-permute-start(bf16[512,512]{1,0:T(8,128)(2,1)} %refs_9_.3), channel_id=1, source_target_pairs={{0,4},{1,5},{2,6},{3,7},{4,0},{5,1},{6,2},{7,3},{8,12},{9,13},{10,... | collective-permute-start | bytes 1572872 | tf_op jit(solution)/shard_map/ppermute | solution.py:20
  3.7 2.6 %collective-permute-start.4 = (bf16[512,512]{1,0:T(8,128)(2,1)}, bf16[512,512]{1,0:T(8,128)(2,1)S(1)}, u32[]{:S(2)}, u32[]{:S(2)}) collective-permute-start(bf16[512,512]{1,0:T(8,128)(2,1)} %refs_9_.3), channel_id=1, source_target_pairs={{0,8},{1,9},{2,10},{3,11},{4,12},{5,13},{6,14},{7,15},{8,0},{9,1},... | collective-permute-start | bytes 1572872 | tf_op jit(solution)/shard_map/ppermute | solution.py:20
  6.3 1.4 %fusion.1 = f32[512,256]{1,0:T(8,128)S(1)} fusion(bf16[512,512]{1,0:T(8,128)(2,1)} %refs_9_.3, bf16[512,256]{1,0:T(8,128)(2,1)} %refs_8_.1), kind=kOutput, calls=%fused_computation.40 | convolution fusion | flops 134217728 | bytes 1310720 | tf_op jit(solution)/shard_map/dot_general | solution.py:272
  7.9 1.6 %collective-permute-start.2 = (bf16[512,512]{1,0:T(8,128)(2,1)}, bf16[512,512]{1,0:T(8,128)(2,1)}, u32[]{:S(2)}, u32[]{:S(2)}) collective-permute-start(bf16[512,512]{1,0:T(8,128)(2,1)} %refs_9_.3), channel_id=1, source_target_pairs={{0,2},{1,3},{2,0},{3,1},{4,6},{5,7},{6,4},{7,5},{8,10},{9,11},{10,... | collective-permute-start | bytes 1572872 | tf_op jit(solution)/shard_map/ppermute | solution.py:20
  9.5 1.1 %pad_maximum_fusion.1 = bf16[512,1024]{1,0:T(8,128)(2,1)} fusion(bf16[512,512]{1,0:T(8,128)(2,1)S(1)} %copy-done, bf16[512,512]{1,0:T(8,128)(2,1)S(1)} %slice-done), kind=kLoop, calls=%fused_computation.1 | loop fusion | flops 2097152 | bytes 2097152 | tf_op jit(solution)/shard_map/concatenate | solution.py:277
  10.6 1.5 %collective-permute-start.8 = (bf16[512,1024]{1,0:T(8,128)(2,1)}, bf16[512,1024]{1,0:T(8,128)(2,1)}, u32[]{:S(2)}, u32[]{:S(2)}) collective-permute-start(bf16[512,1024]{1,0:T(8,128)(2,1)} %pad_maximum_fusion.1), channel_id=1, source_target_pairs={{0,16},{16,0},{1,17},{17,1},{2,18},{18,2},{3,19},{19,3},{4,20},{20... | collective-permute-start | bytes 3145736 | tf_op jit(solution)/shard_map/ppermute | solution.py:25
  13.8 10.0 %collective-permute-done.1 = bf16[128,256]{1,0:T(8,128)(2,1)S(1)} collective-permute-done((bf16[128,256]{1,0:T(8,128)(2,1)S(1)}, bf16[128,256]{1,0:T(8,128)(2,1)S(1)}, u32[]{:S(2)}, u32[]{:S(2)}) %collective-permute-start.1) | collective-permute-done | bytes 65568 | tf_op jit(solution)/shard_map/ppermute | solution.py:20
  23.8 3.2 %collective-permute-done.3.refs_4_ = bf16[512,512]{1,0:T(8,128)(2,1)} collective-permute-done((bf16[512,512]{1,0:T(8,128)(2,1)}, bf16[512,512]{1,0:T(8,128)(2,1)}, u32[]{:S(2)}, u32[]{:S(2)}) %collective-permute-start.3) | collective-permute-done | bytes 524320 | tf_op jit(solution)/shard_map/ppermute | solution.py:20
  27.1 2.4 %collective-permute-done.4.refs_5_ = bf16[512,512]{1,0:T(8,128)(2,1)S(1)} collective-permute-done((bf16[512,512]{1,0:T(8,128)(2,1)}, bf16[512,512]{1,0:T(8,128)(2,1)S(1)}, u32[]{:S(2)}, u32[]{:S(2)}) %collective-permute-start.4) | collective-permute-done | bytes 524320 | tf_op jit(solution)/shard_map/ppermute | solution.py:20
  30.0 2.6 %collective-permute-start.6 = (bf16[128,256]{1,0:T(8,128)(2,1)S(1)}, bf16[128,256]{1,0:T(8,128)(2,1)S(1)}, u32[]{:S(2)}, u32[]{:S(2)}) collective-permute-start(bf16[128,256]{1,0:T(8,128)(2,1)S(1)} %convert_element_type.64), channel_id=1, source_target_pairs={{0,8},{1,9},{2,10},{3,11},{4,12},{5,13},{6,14},{7,15},{8,0},{9,1},... | collective-permute-start | bytes 196616 | tf_op jit(solution)/shard_map/ppermute | solution.py:20
  32.7 1.3 %collective-permute-start.7 = (bf16[128,256]{1,0:T(8,128)(2,1)S(1)}, bf16[128,256]{1,0:T(8,128)(2,1)S(1)}, u32[]{:S(2)}, u32[]{:S(2)}) collective-permute-start(bf16[128,256]{1,0:T(8,128)(2,1)S(1)} %convert_element_type.64), channel_id=1, source_target_pairs={{0,12},{1,13},{2,14},{3,15},{4,8},{5,9},{6,10},{7,11},{8,4},{9,5},... | collective-permute-start | bytes 196616 | tf_op jit(solution)/shard_map/ppermute | solution.py:20
  34.0 1.6 %pad_maximum_fusion = bf16[512,2048]{1,0:T(8,128)(2,1)} fusion(bf16[512,512]{1,0:T(8,128)(2,1)S(1)} %collective-permute-done.4.refs_5_, bf16[512,1536]{1,0:T(8,128)(2,1)S(1)} %slice-done.1), kind=kLoop, calls=%fused_computation | loop fusion | flops 4194304 | bytes 4194304 | tf_op jit(solution)/shard_map/concatenate | solution.py:284
  35.6 3.1 %collective-permute-done.7 = bf16[128,256]{1,0:T(8,128)(2,1)S(1)} collective-permute-done((bf16[128,256]{1,0:T(8,128)(2,1)S(1)}, bf16[128,256]{1,0:T(8,128)(2,1)S(1)}, u32[]{:S(2)}, u32[]{:S(2)}) %collective-permute-start.7) | collective-permute-done | bytes 65568 | tf_op jit(solution)/shard_map/ppermute | solution.py:20
  38.8 1.6 %collective-permute-start.10 = (bf16[128,256]{1,0:T(8,128)(2,1)S(1)}, bf16[128,256]{1,0:T(8,128)(2,1)S(1)}, u32[]{:S(2)}, u32[]{:S(2)}) collective-permute-start(bf16[128,256]{1,0:T(8,128)(2,1)S(1)} %convert_add_fusion.3), channel_id=1, source_target_pairs={{0,2},{1,3},{2,0},{3,1},{4,6},{5,7},{6,4},{7,5},{8,10},{9,11},{10,... | collective-permute-start | bytes 196616 | tf_op jit(solution)/shard_map/ppermute | solution.py:20
  41.0 1.5 %collective-permute-start.21 = (bf16[128,256]{1,0:T(8,128)(2,1)S(1)}, bf16[128,256]{1,0:T(8,128)(2,1)S(1)}, u32[]{:S(2)}, u32[]{:S(2)}) collective-permute-start(bf16[128,256]{1,0:T(8,128)(2,1)S(1)} %convert_add_fusion.3), channel_id=1, source_target_pairs={{0,16},{16,0},{1,17},{17,1},{2,18},{18,2},{3,19},{19,3},{4,20},{20... | collective-permute-start | bytes 196616 | tf_op jit(solution)/shard_map/ppermute | solution.py:25
  45.4 1.5 %collective-permute-start.33 = (bf16[512,2048]{1,0:T(8,128)(2,1)}, bf16[512,2048]{1,0:T(8,128)(2,1)}, u32[]{:S(2)}, u32[]{:S(2)}) collective-permute-start(bf16[512,2048]{1,0:T(8,128)(2,1)} %pad_maximum_fusion), channel_id=1, source_target_pairs={{0,16},{16,0},{1,17},{17,1},{2,18},{18,2},{3,19},{19,3},{4,20},{20... | collective-permute-start | bytes 6291464 | tf_op jit(solution)/shard_map/ppermute | solution.py:25
  46.9 12.1 %forward.1 = (bf16[512,2048]{1,0:T(8,128)(2,1)}, bf16[512,2048]{1,0:T(8,128)(2,1)}, f32[512,256]{1,0:T(8,128)}, bf16[512,512]{1,0:T(8,128)(2,1)}, bf16[512,512]{...) custom-call(bf16[512,512]{1,0:T(8,128)(2,1)} %refs_9_.3, ...), custom_call_target="tpu_custom_call" | custom-call | flops 1000 | bytes 1000 | tf_op jit(solution)/shard_map/forward/pallas_call | solution.py:319
  59.2 1.4 %collective-permute-start.23 = (bf16[128,256]{1,0:T(8,128)(2,1)S(1)}, bf16[128,256]{1,0:T(8,128)(2,1)S(1)}, u32[]{:S(2)}, u32[]{:S(2)}) collective-permute-start(bf16[128,256]{1,0:T(8,128)(2,1)S(1)} %collective-permute-done.21), channel_id=1, source_target_pairs={{0,2},{1,3},{2,0},{3,1},{4,6},{5,7},{6,4},{7,5},{8,10},{9,11},{10,... | collective-permute-start | bytes 196616 | tf_op jit(solution)/shard_map/ppermute | solution.py:20
  62.6 1.4 %collective-permute-start.16 = (bf16[128,256]{1,0:T(8,128)(2,1)S(1)}, bf16[128,256]{1,0:T(8,128)(2,1)S(1)}, u32[]{:S(2)}, u32[]{:S(2)}) collective-permute-start(bf16[128,256]{1,0:T(8,128)(2,1)S(1)} %get-tuple-element.95), channel_id=1, source_target_pairs={{0,2},{1,3},{2,0},{3,1},{4,6},{5,7},{6,4},{7,5},{8,10},{9,11},{10,... | collective-permute-start | bytes 196616 | tf_op jit(solution)/shard_map/ppermute | solution.py:20
  64.9 1.9 %collective-permute-done.16 = bf16[128,256]{1,0:T(8,128)(2,1)S(1)} collective-permute-done((bf16[128,256]{1,0:T(8,128)(2,1)S(1)}, bf16[128,256]{1,0:T(8,128)(2,1)S(1)}, u32[]{:S(2)}, u32[]{:S(2)}) %collective-permute-start.16) | collective-permute-done | bytes 65568 | tf_op jit(solution)/shard_map/ppermute | solution.py:20
  66.8 1.3 %collective-permute-done.17 = bf16[128,256]{1,0:T(8,128)(2,1)S(1)} collective-permute-done((bf16[128,256]{1,0:T(8,128)(2,1)S(1)}, bf16[128,256]{1,0:T(8,128)(2,1)S(1)}, u32[]{:S(2)}, u32[]{:S(2)}) %collective-permute-start.17) | collective-permute-done | bytes 65568 | tf_op jit(solution)/shard_map/ppermute | solution.py:20
  69.1 2.2 %collective-permute-start.18 = (bf16[128,256]{1,0:T(8,128)(2,1)S(1)}, bf16[128,256]{1,0:T(8,128)(2,1)S(1)}, u32[]{:S(2)}, u32[]{:S(2)}) collective-permute-start(bf16[128,256]{1,0:T(8,128)(2,1)S(1)} %get-tuple-element.91), channel_id=1, source_target_pairs={{0,4},{1,5},{2,6},{3,7},{4,0},{5,1},{6,2},{7,3},{8,12},{9,13},{10,... | collective-permute-start | bytes 196616 | tf_op jit(solution)/shard_map/ppermute | solution.py:20
  71.3 2.4 %collective-permute-start.20 = (bf16[128,256]{1,0:T(8,128)(2,1)S(1)}, bf16[128,256]{1,0:T(8,128)(2,1)S(1)}, u32[]{:S(2)}, u32[]{:S(2)}) collective-permute-start(bf16[128,256]{1,0:T(8,128)(2,1)S(1)} %get-tuple-element.91), channel_id=1, source_target_pairs={{0,12},{1,13},{2,14},{3,15},{4,8},{5,9},{6,10},{7,11},{8,4},{9,5},... | collective-permute-start | bytes 196616 | tf_op jit(solution)/shard_map/ppermute | solution.py:20
  74.5 4.7 %collective-permute-done.19 = bf16[128,256]{1,0:T(8,128)(2,1)S(1)} collective-permute-done((bf16[128,256]{1,0:T(8,128)(2,1)S(1)}, bf16[128,256]{1,0:T(8,128)(2,1)S(1)}, u32[]{:S(2)}, u32[]{:S(2)}) %collective-permute-start.19) | collective-permute-done | bytes 65568 | tf_op jit(solution)/shard_map/ppermute | solution.py:20
  79.3 1.3 %collective-permute-start.26 = (bf16[128,256]{1,0:T(8,128)(2,1)S(1)}, bf16[128,256]{1,0:T(8,128)(2,1)S(1)}, u32[]{:S(2)}, u32[]{:S(2)}) collective-permute-start(bf16[128,256]{1,0:T(8,128)(2,1)S(1)} %convert_add_fusion.1), channel_id=1, source_target_pairs={{0,2},{1,3},{2,0},{3,1},{4,6},{5,7},{6,4},{7,5},{8,10},{9,11},{10,... | collective-permute-start | bytes 196616 | tf_op jit(solution)/shard_map/ppermute | solution.py:20
  81.2 1.7 %collective-permute-start.31 = (bf16[512,512]{1,0:T(8,128)(2,1)S(1)}, bf16[512,512]{1,0:T(8,128)(2,1)S(1)}, u32[]{:S(2)}, u32[]{:S(2)}) collective-permute-start(bf16[512,512]{1,0:T(8,128)(2,1)S(1)} %copy-done.18), channel_id=1, source_target_pairs={{0,8},{1,9},{2,10},{3,11},{4,12},{5,13},{6,14},{7,15},{8,0},{9,1},... | collective-permute-start | bytes 1572872 | tf_op jit(solution)/shard_map/ppermute | solution.py:20
  82.9 1.2 %collective-permute-done.26 = bf16[128,256]{1,0:T(8,128)(2,1)S(1)} collective-permute-done((bf16[128,256]{1,0:T(8,128)(2,1)S(1)}, bf16[128,256]{1,0:T(8,128)(2,1)S(1)}, u32[]{:S(2)}, u32[]{:S(2)}) %collective-permute-start.26) | collective-permute-done | bytes 65568 | tf_op jit(solution)/shard_map/ppermute | solution.py:20
  84.1 1.8 %collective-permute-start.30 = (bf16[512,512]{1,0:T(8,128)(2,1)S(1)}, bf16[512,512]{1,0:T(8,128)(2,1)S(1)}, u32[]{:S(2)}, u32[]{:S(2)}) collective-permute-start(bf16[512,512]{1,0:T(8,128)(2,1)S(1)} %copy-done.17), channel_id=1, source_target_pairs={{0,4},{1,5},{2,6},{3,7},{4,0},{5,1},{6,2},{7,3},{8,12},{9,13},{10,... | collective-permute-start | bytes 1572872 | tf_op jit(solution)/shard_map/ppermute | solution.py:20
  86.8 6.7 %collective-permute-done.33.refs_14_.refs_20_ = bf16[512,2048]{1,0:T(8,128)(2,1)} collective-permute-done((bf16[512,2048]{1,0:T(8,128)(2,1)}, bf16[512,2048]{1,0:T(8,128)(2,1)}, u32[]{:S(2)}, u32[]{:S(2)}) %collective-permute-start.33) | collective-permute-done | bytes 2097184 | tf_op jit(solution)/shard_map/ppermute | solution.py:25
  93.5 1.5 %collective-permute-start.34 = (bf16[512,256]{1,0:T(8,128)(2,1)S(1)}, bf16[512,256]{1,0:T(8,128)(2,1)S(1)}, u32[]{:S(2)}, u32[]{:S(2)}) collective-permute-start(bf16[512,256]{1,0:T(8,128)(2,1)S(1)} %pad_maximum_fusion.4.refs_7_), channel_id=1, source_target_pairs={{0,16},{16,0},{1,17},{17,1},{2,18},{18,2},{3,19},{19,3},{4,20},{20... | collective-permute-start | bytes 786440 | tf_op jit(solution)/shard_map/ppermute | solution.py:25
  95.1 13.3 %weight_grad.1 = (f32[4,7,128,512]{3,2,1,0:T(8,128)}, f32[256,2048]{1,0:T(8,128)}) custom-call(bf16[512,512]{1,0:T(8,128)(2,1)} %refs_9_.3, bf16[512,512]{1,0:T(8,128)(2,1)} %refs_9_.3, bf16[512,512]{1,0:T(8,128)(2,1)} %copy-done.6, bf16[512,512]{1,0:T(8,128)(2,1)} %collective-permute-done.2.refs_3_, bf16[512,512]{1,0:T(8,128)(2,1)} %collective-permute-done.3.refs_4_, ...), custom_call_target="tpu_custom_call" | custom-call | flops 1000 | bytes 1000 | tf_op jit(solution)/shard_map/weight_grad/pallas_call | solution.py:372
  108.5 1.7 %finish.1 = (bf16[512,512]{1,0:T(8,128)(2,1)}, f32[512,256]{1,0:T(8,128)}) custom-call(bf16[512,512]{1,0:T(8,128)(2,1)S(1)} %copy-done.8, bf16[512,512]{1,0:T(8,128)(2,1)S(1)} %copy-done.9, bf16[512,512]{1,0:T(8,128)(2,1)S(1)} %collective-permute-done.28.refs_2_, bf16[512,512]{1,0:T(8,128)(2,1)S(1)} %collective-permute-done.29.refs_3_, ...), custom_call_target="tpu_custom_call" | custom-call | flops 1000 | bytes 1000 | tf_op jit(solution)/shard_map/finish/pallas_call | solution.py:391
  (102 shorter events, 12.1 us)
Async XLA Ops:
  0.7 26.4 %collective-permute-start.3 = (bf16[512,512]{1,0:T(8,128)(2,1)}, bf16[512,512]{1,0:T(8,128)(2,1)}, u32[]{:S(2)}, u32[]{:S(2)}) collective-permute-start(bf16[512,512]{1,0:T(8,128)(2,1)} %refs_9_.3), channel_id=1, source_target_pairs={{0,4},{1,5},{2,6},{3,7},{4,0},{5,1},{6,2},{7,3},{8,12},{9,13},{10,... | collective-permute-start | bytes 1572872 | tf_op jit(solution)/shard_map/ppermute | solution.py:20
  3.7 25.8 %collective-permute-start.4 = (bf16[512,512]{1,0:T(8,128)(2,1)}, bf16[512,512]{1,0:T(8,128)(2,1)S(1)}, u32[]{:S(2)}, u32[]{:S(2)}) collective-permute-start(bf16[512,512]{1,0:T(8,128)(2,1)} %refs_9_.3), channel_id=1, source_target_pairs={{0,8},{1,9},{2,10},{3,11},{4,12},{5,13},{6,14},{7,15},{8,0},{9,1},... | collective-permute-start | bytes 1572872 | tf_op jit(solution)/shard_map/ppermute | solution.py:20
  7.8 4.3 %collective-permute-start = (bf16[256,256]{1,0:T(8,128)(2,1)S(1)}, bf16[256,256]{1,0:T(8,128)(2,1)S(1)}, u32[]{:S(2)}, u32[]{:S(2)}) collective-permute-start(bf16[256,256]{1,0:T(8,128)(2,1)S(1)} %dynamic-slice_convert_fusion), channel_id=1, source_target_pairs={{0,1},{1,0},{2,3},{3,2},{4,5},{5,4},{6,7},{7,6},{8,9},{9,8},{10,11... | collective-permute-start | bytes 393224 | tf_op jit(solution)/shard_map/ppermute | solution.py:20
  7.9 16.0 %collective-permute-start.2 = (bf16[512,512]{1,0:T(8,128)(2,1)}, bf16[512,512]{1,0:T(8,128)(2,1)}, u32[]{:S(2)}, u32[]{:S(2)}) collective-permute-start(bf16[512,512]{1,0:T(8,128)(2,1)} %refs_9_.3), channel_id=1, source_target_pairs={{0,2},{1,3},{2,0},{3,1},{4,6},{5,7},{6,4},{7,5},{8,10},{9,11},{10,... | collective-permute-start | bytes 1572872 | tf_op jit(solution)/shard_map/ppermute | solution.py:20
  10.6 28.2 %collective-permute-start.8 = (bf16[512,1024]{1,0:T(8,128)(2,1)}, bf16[512,1024]{1,0:T(8,128)(2,1)}, u32[]{:S(2)}, u32[]{:S(2)}) collective-permute-start(bf16[512,1024]{1,0:T(8,128)(2,1)} %pad_maximum_fusion.1), channel_id=1, source_target_pairs={{0,16},{16,0},{1,17},{17,1},{2,18},{18,2},{3,19},{19,3},{4,20},{20... | collective-permute-start | bytes 3145736 | tf_op jit(solution)/shard_map/ppermute | solution.py:25
  13.2 10.6 %collective-permute-start.1 = (bf16[128,256]{1,0:T(8,128)(2,1)S(1)}, bf16[128,256]{1,0:T(8,128)(2,1)S(1)}, u32[]{:S(2)}, u32[]{:S(2)}) collective-permute-start(bf16[128,256]{1,0:T(8,128)(2,1)S(1)} %dynamic-slice_convert_fusion.4), channel_id=1, source_target_pairs={{0,2},{1,3},{2,0},{3,1},{4,6},{5,7},{6,4},{7,5},{8,10},{9,11},{10,... | collective-permute-start | bytes 196616 | tf_op jit(solution)/shard_map/ppermute | solution.py:20
  29.6 6.1 %collective-permute-start.5 = (bf16[128,256]{1,0:T(8,128)(2,1)S(1)}, bf16[128,256]{1,0:T(8,128)(2,1)S(1)}, u32[]{:S(2)}, u32[]{:S(2)}) collective-permute-start(bf16[128,256]{1,0:T(8,128)(2,1)S(1)} %convert_element_type.64), channel_id=1, source_target_pairs={{0,4},{1,5},{2,6},{3,7},{4,0},{5,1},{6,2},{7,3},{8,12},{9,13},{10,... | collective-permute-start | bytes 196616 | tf_op jit(solution)/shard_map/ppermute | solution.py:20
  30.0 5.6 %collective-permute-start.6 = (bf16[128,256]{1,0:T(8,128)(2,1)S(1)}, bf16[128,256]{1,0:T(8,128)(2,1)S(1)}, u32[]{:S(2)}, u32[]{:S(2)}) collective-permute-start(bf16[128,256]{1,0:T(8,128)(2,1)S(1)} %convert_element_type.64), channel_id=1, source_target_pairs={{0,8},{1,9},{2,10},{3,11},{4,12},{5,13},{6,14},{7,15},{8,0},{9,1},... | collective-permute-start | bytes 196616 | tf_op jit(solution)/shard_map/ppermute | solution.py:20
  32.7 6.1 %collective-permute-start.7 = (bf16[128,256]{1,0:T(8,128)(2,1)S(1)}, bf16[128,256]{1,0:T(8,128)(2,1)S(1)}, u32[]{:S(2)}, u32[]{:S(2)}) collective-permute-start(bf16[128,256]{1,0:T(8,128)(2,1)S(1)} %convert_element_type.64), channel_id=1, source_target_pairs={{0,12},{1,13},{2,14},{3,15},{4,8},{5,9},{6,10},{7,11},{8,4},{9,5},... | collective-permute-start | bytes 196616 | tf_op jit(solution)/shard_map/ppermute | solution.py:20
  38.8 4.9 %collective-permute-start.10 = (bf16[128,256]{1,0:T(8,128)(2,1)S(1)}, bf16[128,256]{1,0:T(8,128)(2,1)S(1)}, u32[]{:S(2)}, u32[]{:S(2)}) collective-permute-start(bf16[128,256]{1,0:T(8,128)(2,1)S(1)} %convert_add_fusion.3), channel_id=1, source_target_pairs={{0,2},{1,3},{2,0},{3,1},{4,6},{5,7},{6,4},{7,5},{8,10},{9,11},{10,... | collective-permute-start | bytes 196616 | tf_op jit(solution)/shard_map/ppermute | solution.py:20
  40.4 4.2 %collective-permute-start.11 = (bf16[128,256]{1,0:T(8,128)(2,1)S(1)}, bf16[128,256]{1,0:T(8,128)(2,1)S(1)}, u32[]{:S(2)}, u32[]{:S(2)}) collective-permute-start(bf16[128,256]{1,0:T(8,128)(2,1)S(1)} %convert_add_fusion.3), channel_id=1, source_target_pairs={{0,3},{1,2},{2,1},{3,0},{4,7},{5,6},{6,5},{7,4},{8,11},{9,10},{10,... | collective-permute-start | bytes 196616 | tf_op jit(solution)/shard_map/ppermute | solution.py:20
  40.4 4.2 %collective-permute-start.9 = (bf16[128,256]{1,0:T(8,128)(2,1)S(1)}, bf16[128,256]{1,0:T(8,128)(2,1)S(1)}, u32[]{:S(2)}, u32[]{:S(2)}) collective-permute-start(bf16[128,256]{1,0:T(8,128)(2,1)S(1)} %convert_add_fusion.3), channel_id=1, source_target_pairs={{0,1},{1,0},{2,3},{3,2},{4,5},{5,4},{6,7},{7,6},{8,9},{9,8},{10,11... | collective-permute-start | bytes 196616 | tf_op jit(solution)/shard_map/ppermute | solution.py:20
  41.0 4.4 %collective-permute-start.21 = (bf16[128,256]{1,0:T(8,128)(2,1)S(1)}, bf16[128,256]{1,0:T(8,128)(2,1)S(1)}, u32[]{:S(2)}, u32[]{:S(2)}) collective-permute-start(bf16[128,256]{1,0:T(8,128)(2,1)S(1)} %convert_add_fusion.3), channel_id=1, source_target_pairs={{0,16},{16,0},{1,17},{17,1},{2,18},{18,2},{3,19},{19,3},{4,20},{20... | collective-permute-start | bytes 196616 | tf_op jit(solution)/shard_map/ppermute | solution.py:25
  44.6 16.0 %collective-permute-start.13 = (bf16[512,512]{1,0:T(8,128)(2,1)S(1)}, bf16[512,512]{1,0:T(8,128)(2,1)S(1)}, u32[]{:S(2)}, u32[]{:S(2)}) collective-permute-start(bf16[512,512]{1,0:T(8,128)(2,1)S(1)} %slice.11.refs_9_.refs_10_.refs_15_), channel_id=1, source_target_pairs={{0,2},{1,3},{2,0},{3,1},{4,6},{5,7},{6,4},{7,5},{8,10},{9,11},{10,... | collective-permute-start | bytes 1572872 | tf_op jit(solution)/shard_map/ppermute | solution.py:20
  45.4 15.7 %collective-permute-start.14 = (bf16[512,512]{1,0:T(8,128)(2,1)S(1)}, bf16[512,512]{1,0:T(8,128)(2,1)}, u32[]{:S(2)}, u32[]{:S(2)}) collective-permute-start(bf16[512,512]{1,0:T(8,128)(2,1)S(1)} %slice.11.refs_9_.refs_10_.refs_15_), channel_id=1, source_target_pairs={{0,4},{1,5},{2,6},{3,7},{4,0},{5,1},{6,2},{7,3},{8,12},{9,13},{10,... | collective-permute-start | bytes 1572872 | tf_op jit(solution)/shard_map/ppermute | solution.py:20
  45.4 48.1 %collective-permute-start.33 = (bf16[512,2048]{1,0:T(8,128)(2,1)}, bf16[512,2048]{1,0:T(8,128)(2,1)}, u32[]{:S(2)}, u32[]{:S(2)}) collective-permute-start(bf16[512,2048]{1,0:T(8,128)(2,1)} %pad_maximum_fusion), channel_id=1, source_target_pairs={{0,16},{16,0},{1,17},{17,1},{2,18},{18,2},{3,19},{19,3},{4,20},{20... | collective-permute-start | bytes 6291464 | tf_op jit(solution)/shard_map/ppermute | solution.py:25
  59.2 3.4 %collective-permute-start.22 = (bf16[128,256]{1,0:T(8,128)(2,1)S(1)}, bf16[128,256]{1,0:T(8,128)(2,1)S(1)}, u32[]{:S(2)}, u32[]{:S(2)}) collective-permute-start(bf16[128,256]{1,0:T(8,128)(2,1)S(1)} %collective-permute-done.21), channel_id=1, source_target_pairs={{0,1},{1,0},{2,3},{3,2},{4,5},{5,4},{6,7},{7,6},{8,9},{9,8},{10,11... | collective-permute-start | bytes 196616 | tf_op jit(solution)/shard_map/ppermute | solution.py:20
  59.2 4.7 %collective-permute-start.23 = (bf16[128,256]{1,0:T(8,128)(2,1)S(1)}, bf16[128,256]{1,0:T(8,128)(2,1)S(1)}, u32[]{:S(2)}, u32[]{:S(2)}) collective-permute-start(bf16[128,256]{1,0:T(8,128)(2,1)S(1)} %collective-permute-done.21), channel_id=1, source_target_pairs={{0,2},{1,3},{2,0},{3,1},{4,6},{5,7},{6,4},{7,5},{8,10},{9,11},{10,... | collective-permute-start | bytes 196616 | tf_op jit(solution)/shard_map/ppermute | solution.py:20
  60.7 4.2 %collective-permute-start.24 = (bf16[128,256]{1,0:T(8,128)(2,1)S(1)}, bf16[128,256]{1,0:T(8,128)(2,1)S(1)}, u32[]{:S(2)}, u32[]{:S(2)}) collective-permute-start(bf16[128,256]{1,0:T(8,128)(2,1)S(1)} %collective-permute-done.21), channel_id=1, source_target_pairs={{0,3},{1,2},{2,1},{3,0},{4,7},{5,6},{6,5},{7,4},{8,11},{9,10},{10,... | collective-permute-start | bytes 196616 | tf_op jit(solution)/shard_map/ppermute | solution.py:20
  62.6 4.3 %collective-permute-start.16 = (bf16[128,256]{1,0:T(8,128)(2,1)S(1)}, bf16[128,256]{1,0:T(8,128)(2,1)S(1)}, u32[]{:S(2)}, u32[]{:S(2)}) collective-permute-start(bf16[128,256]{1,0:T(8,128)(2,1)S(1)} %get-tuple-element.95), channel_id=1, source_target_pairs={{0,2},{1,3},{2,0},{3,1},{4,6},{5,7},{6,4},{7,5},{8,10},{9,11},{10,... | collective-permute-start | bytes 196616 | tf_op jit(solution)/shard_map/ppermute | solution.py:20
  63.9 4.2 %collective-permute-start.17 = (bf16[128,256]{1,0:T(8,128)(2,1)S(1)}, bf16[128,256]{1,0:T(8,128)(2,1)S(1)}, u32[]{:S(2)}, u32[]{:S(2)}) collective-permute-start(bf16[128,256]{1,0:T(8,128)(2,1)S(1)} %get-tuple-element.94), channel_id=1, source_target_pairs={{0,3},{1,2},{2,1},{3,0},{4,7},{5,6},{6,5},{7,4},{8,11},{9,10},{10,... | collective-permute-start | bytes 196616 | tf_op jit(solution)/shard_map/ppermute | solution.py:20
  69.1 5.4 %collective-permute-start.18 = (bf16[128,256]{1,0:T(8,128)(2,1)S(1)}, bf16[128,256]{1,0:T(8,128)(2,1)S(1)}, u32[]{:S(2)}, u32[]{:S(2)}) collective-permute-start(bf16[128,256]{1,0:T(8,128)(2,1)S(1)} %get-tuple-element.91), channel_id=1, source_target_pairs={{0,4},{1,5},{2,6},{3,7},{4,0},{5,1},{6,2},{7,3},{8,12},{9,13},{10,... | collective-permute-start | bytes 196616 | tf_op jit(solution)/shard_map/ppermute | solution.py:20
  71.3 7.9 %collective-permute-start.19 = (bf16[128,256]{1,0:T(8,128)(2,1)S(1)}, bf16[128,256]{1,0:T(8,128)(2,1)S(1)}, u32[]{:S(2)}, u32[]{:S(2)}) collective-permute-start(bf16[128,256]{1,0:T(8,128)(2,1)S(1)} %get-tuple-element.91), channel_id=1, source_target_pairs={{0,8},{1,9},{2,10},{3,11},{4,12},{5,13},{6,14},{7,15},{8,0},{9,1},... | collective-permute-start | bytes 196616 | tf_op jit(solution)/shard_map/ppermute | solution.py:20
  71.3 7.9 %collective-permute-start.20 = (bf16[128,256]{1,0:T(8,128)(2,1)S(1)}, bf16[128,256]{1,0:T(8,128)(2,1)S(1)}, u32[]{:S(2)}, u32[]{:S(2)}) collective-permute-start(bf16[128,256]{1,0:T(8,128)(2,1)S(1)} %get-tuple-element.91), channel_id=1, source_target_pairs={{0,12},{1,13},{2,14},{3,15},{4,8},{5,9},{6,10},{7,11},{8,4},{9,5},... | collective-permute-start | bytes 196616 | tf_op jit(solution)/shard_map/ppermute | solution.py:20
  74.5 12.3 %collective-permute-start.32 = (bf16[512,512]{1,0:T(8,128)(2,1)S(1)}, bf16[512,512]{1,0:T(8,128)(2,1)S(1)}, u32[]{:S(2)}, u32[]{:S(2)}) collective-permute-start(bf16[512,512]{1,0:T(8,128)(2,1)S(1)} %slice.11.refs_9_.refs_10_.refs_15_), channel_id=1, source_target_pairs={{0,1},{1,0},{2,3},{3,2},{4,5},{5,4},{6,7},{7,6},{8,9},{9,8},{10,11... | collective-permute-start | bytes 1572872 | tf_op jit(solution)/shard_map/ppermute | solution.py:20
  79.3 4.8 %collective-permute-start.26 = (bf16[128,256]{1,0:T(8,128)(2,1)S(1)}, bf16[128,256]{1,0:T(8,128)(2,1)S(1)}, u32[]{:S(2)}, u32[]{:S(2)}) collective-permute-start(bf16[128,256]{1,0:T(8,128)(2,1)S(1)} %convert_add_fusion.1), channel_id=1, source_target_pairs={{0,2},{1,3},{2,0},{3,1},{4,6},{5,7},{6,4},{7,5},{8,10},{9,11},{10,... | collective-permute-start | bytes 196616 | tf_op jit(solution)/shard_map/ppermute | solution.py:20
  80.6 5.3 %collective-permute-start.27 = (bf16[128,256]{1,0:T(8,128)(2,1)S(1)}, bf16[128,256]{1,0:T(8,128)(2,1)S(1)}, u32[]{:S(2)}, u32[]{:S(2)}) collective-permute-start(bf16[128,256]{1,0:T(8,128)(2,1)S(1)} %convert_add_fusion.1), channel_id=1, source_target_pairs={{0,3},{1,2},{2,1},{3,0},{4,7},{5,6},{6,5},{7,4},{8,11},{9,10},{10,... | collective-permute-start | bytes 196616 | tf_op jit(solution)/shard_map/ppermute | solution.py:20
  81.2 27.2 %collective-permute-start.31 = (bf16[512,512]{1,0:T(8,128)(2,1)S(1)}, bf16[512,512]{1,0:T(8,128)(2,1)S(1)}, u32[]{:S(2)}, u32[]{:S(2)}) collective-permute-start(bf16[512,512]{1,0:T(8,128)(2,1)S(1)} %copy-done.18), channel_id=1, source_target_pairs={{0,8},{1,9},{2,10},{3,11},{4,12},{5,13},{6,14},{7,15},{8,0},{9,1},... | collective-permute-start | bytes 1572872 | tf_op jit(solution)/shard_map/ppermute | solution.py:20
  84.1 24.3 %collective-permute-start.30 = (bf16[512,512]{1,0:T(8,128)(2,1)S(1)}, bf16[512,512]{1,0:T(8,128)(2,1)S(1)}, u32[]{:S(2)}, u32[]{:S(2)}) collective-permute-start(bf16[512,512]{1,0:T(8,128)(2,1)S(1)} %copy-done.17), channel_id=1, source_target_pairs={{0,4},{1,5},{2,6},{3,7},{4,0},{5,1},{6,2},{7,3},{8,12},{9,13},{10,... | collective-permute-start | bytes 1572872 | tf_op jit(solution)/shard_map/ppermute | solution.py:20
  85.9 22.5 %collective-permute-start.29 = (bf16[512,512]{1,0:T(8,128)(2,1)S(1)}, bf16[512,512]{1,0:T(8,128)(2,1)S(1)}, u32[]{:S(2)}, u32[]{:S(2)}) collective-permute-start(bf16[512,512]{1,0:T(8,128)(2,1)S(1)} %copy-done.16), channel_id=1, source_target_pairs={{0,2},{1,3},{2,0},{3,1},{4,6},{5,7},{6,4},{7,5},{8,10},{9,11},{10,... | collective-permute-start | bytes 1572872 | tf_op jit(solution)/shard_map/ppermute | solution.py:20
  86.8 21.7 %collective-permute-start.28 = (bf16[512,512]{1,0:T(8,128)(2,1)S(1)}, bf16[512,512]{1,0:T(8,128)(2,1)S(1)}, u32[]{:S(2)}, u32[]{:S(2)}) collective-permute-start(bf16[512,512]{1,0:T(8,128)(2,1)S(1)} %copy-done.15), channel_id=1, source_target_pairs={{0,1},{1,0},{2,3},{3,2},{4,5},{5,4},{6,7},{7,6},{8,9},{9,8},{10,11... | collective-permute-start | bytes 1572872 | tf_op jit(solution)/shard_map/ppermute | solution.py:20
  93.5 14.9 %collective-permute-start.34 = (bf16[512,256]{1,0:T(8,128)(2,1)S(1)}, bf16[512,256]{1,0:T(8,128)(2,1)S(1)}, u32[]{:S(2)}, u32[]{:S(2)}) collective-permute-start(bf16[512,256]{1,0:T(8,128)(2,1)S(1)} %pad_maximum_fusion.4.refs_7_), channel_id=1, source_target_pairs={{0,16},{16,0},{1,17},{17,1},{2,18},{18,2},{3,19},{19,3},{4,20},{20... | collective-permute-start | bytes 786440 | tf_op jit(solution)/shard_map/ppermute | solution.py:25
  (24 other events, 351.5 us)

commit v5 on v4

--- a/solution.py
+++ b/solution.py
@@ -64,7 +64,7 @@
 def sum_far(part, axis, hooks):
     near = near_bits(axis)
     sent = part.astype(BF)
-    for mask in range(1, lax.axis_size(axis) >> near):
+    for mask in reversed(range(1, lax.axis_size(axis) >> near)):
         part = part + crossed(sent, axis, mask << near).astype(F32)
     return hooks("far", part).astype(BF)
 
@@ -308,7 +308,7 @@
         for s in near[1:]:
             env[f"xo{d}{s}"] = to_partner(tie(env[f"in{d}"], low)[0], s)
     send_rest(env["low1"] if others else low)
-    low = pin(low, *[f"x{s}" for s in remote])
+    low = pin(low, *[f"x{s}" for s in remote], *each("low"))
 
     def x_blocks(base_block, prefix):
         arrays = [env.get(f"{prefix}{s}", base_block) for s in range(sections)]
@@ -380,7 +380,7 @@
             (1000, 1000),
             aliases={count: 0, count + 1: 1} if grads else None,
             name="weight_grad",
-        )(*map(in_hbm, operands), *grads)
+        )(*operands, *grads)
     d_bfly, d_v = grads
 
     send_terms(d_low, [s for s in remote if f"t{s}" not in env])

time: 110 us -> 109 us (level)
  local copies, waits for them, and re-layouts: 2.27 us -> 4.9 us
  waiting for transfers between devices: 36 us -> 33.6 us
    ppermute x31, waiting for transfers between devices: 29.3 us -> 25.8 us  [crossed(): return lax.ppermute(block, axis, [(i, i ^ mask) for i in range(count)])]
    slice x2 -> x1, local copies, waits for them, and re-layouts: 0.01 us -> 2.65 us  [cut_rest(): pieces = [cotangent[:, lead * group:]] if per_dev > lead else []]
    concatenate x1, other arithmetic: 1.63 us -> 3.03 us  [cut_rest(): jnp.concatenate(pieces, axis=1)]
    ppermute x4, waiting for transfers between devices: 6.7 us -> 7.82 us  [rolled(): lax.ppermute(block, axis, [(i, (i + shift) % count) for i in range(count)])]
  transfers between devices with their start and end apart: 35 -> 35, of which waited for: 11 -> 13; matrix products, arithmetic and copies ran while one was open for 8% -> 11% of each run, Pallas kernels for 23% -> 23%
where the time goes in v5:
time: 109 us
  starting transfers between devices  36.1 us (33%)
  waiting for transfers between devices  33.6 us (31%)
  Pallas kernels  26.6 us (24%)
  other arithmetic  5.36 us (5%)
  local copies, waits for them, and re-layouts  4.9 us (4%)
  matrix products  1.4 us (1%)
    ppermute x31, starting transfers between devices, crossed(): return lax.ppermute(block, axis, [(i, i ^ mask) for i in range(count)])  30.1 us
    ppermute x31, waiting for transfers between devices, crossed(): return lax.ppermute(block, axis, [(i, i ^ mask) for i in range(count)])  25.8 us
    pallas_call x1, Pallas kernels, local(): call(functools.partial(weight_grad_kernel, sections, own, other, [p[0] fo...  12.9 us
    pallas_call x1, Pallas kernels, local(): call(functools.partial(forward_kernel, [1] * sections), per_dev, specs +...  12.1 us
    ppermute x4, waiting for transfers between devices, rolled(): lax.ppermute(block, axis, [(i, (i + shift) % count) for i in range(count)])  7.82 us
    ppermute x4, starting transfers between devices, rolled(): lax.ppermute(block, axis, [(i, (i + shift) % count) for i in range(count)])  5.98 us
    concatenate x1, other arithmetic, cut_rest(): jnp.concatenate(pieces, axis=1)  3.03 us
    slice x1, local copies, waits for them, and re-layouts, cut_rest(): pieces = [cotangent[:, lead * group:]] if per_dev > lead else []  2.65 us
  transfers between devices with their start and end apart: 35, of which 13 were waited for; matrix products, arithmetic and copies ran while one was open for 11% of the time, Pallas kernels for 23%

profile of v5, /device:TPU:0, one launch (start us, length us, event | category | flops | bytes accessed | tf_op | source)
XLA Modules:
  0.0 109.0 jit_solution(2765362074138921087)
XLA Ops:
  0.7 3.1 %collective-permute-start.3 = (bf16[512,512]{1,0:T(8,128)(2,1)}, bf16[512,512]{1,0:T(8,128)(2,1)S(1)}, u32[]{:S(2)}, u32[]{:S(2)}) collective-permute-start(bf16[512,512]{1,0:T(8,128)(2,1)} %refs_9_.3), channel_id=1, source_target_pairs={{0,4},{1,5},{2,6},{3,7},{4,0},{5,1},{6,2},{7,3},{8,12},{9,13},{10,... | collective-permute-start | bytes 1572872 | tf_op jit(solution)/shard_map/ppermute | solution.py:20
  3.7 2.6 %collective-permute-start.4 = (bf16[512,512]{1,0:T(8,128)(2,1)}, bf16[512,512]{1,0:T(8,128)(2,1)S(1)}, u32[]{:S(2)}, u32[]{:S(2)}) collective-permute-start(bf16[512,512]{1,0:T(8,128)(2,1)} %refs_9_.3), channel_id=1, source_target_pairs={{0,8},{1,9},{2,10},{3,11},{4,12},{5,13},{6,14},{7,15},{8,0},{9,1},... | collective-permute-start | bytes 1572872 | tf_op jit(solution)/shard_map/ppermute | solution.py:20
  6.3 1.4 %fusion.1 = f32[512,256]{1,0:T(8,128)S(1)} fusion(bf16[512,512]{1,0:T(8,128)(2,1)} %refs_9_.3, bf16[512,256]{1,0:T(8,128)(2,1)} %refs_8_.1), kind=kOutput, calls=%fused_computation.40 | convolution fusion | flops 134217728 | bytes 1310720 | tf_op jit(solution)/shard_map/dot_general | solution.py:272
  7.8 1.6 %collective-permute-start.2 = (bf16[512,512]{1,0:T(8,128)(2,1)}, bf16[512,512]{1,0:T(8,128)(2,1)S(1)}, u32[]{:S(2)}, u32[]{:S(2)}) collective-permute-start(bf16[512,512]{1,0:T(8,128)(2,1)} %refs_9_.3), channel_id=1, source_target_pairs={{0,2},{1,3},{2,0},{3,1},{4,6},{5,7},{6,4},{7,5},{8,10},{9,11},{10,... | collective-permute-start | bytes 1572872 | tf_op jit(solution)/shard_map/ppermute | solution.py:20
  9.4 1.1 %pad_maximum_fusion.1 = bf16[512,1024]{1,0:T(8,128)(2,1)} fusion(bf16[512,512]{1,0:T(8,128)(2,1)S(1)} %copy-done, bf16[512,512]{1,0:T(8,128)(2,1)S(1)} %slice-done), kind=kLoop, calls=%fused_computation.1 | loop fusion | flops 2097152 | bytes 2097152 | tf_op jit(solution)/shard_map/concatenate | solution.py:277
  10.6 1.5 %collective-permute-start.8 = (bf16[512,1024]{1,0:T(8,128)(2,1)}, bf16[512,1024]{1,0:T(8,128)(2,1)}, u32[]{:S(2)}, u32[]{:S(2)}) collective-permute-start(bf16[512,1024]{1,0:T(8,128)(2,1)} %pad_maximum_fusion.1), channel_id=1, source_target_pairs={{0,16},{16,0},{1,17},{17,1},{2,18},{18,2},{3,19},{19,3},{4,20},{20... | collective-permute-start | bytes 3145736 | tf_op jit(solution)/shard_map/ppermute | solution.py:25
  12.7 2.7 %slice.10 = bf16[512,1536]{1,0:T(8,128)(2,1)} slice(bf16[512,2048]{1,0:T(8,128)(2,1)} %refs_10_.1), slice={[0:512], [512:2048]} | slice | bytes 3145728 | tf_op jit(solution)/shard_map/slice | solution.py:282
  15.3 8.5 %collective-permute-done.1 = bf16[128,256]{1,0:T(8,128)(2,1)S(1)} collective-permute-done((bf16[128,256]{1,0:T(8,128)(2,1)S(1)}, bf16[128,256]{1,0:T(8,128)(2,1)S(1)}, u32[]{:S(2)}, u32[]{:S(2)}) %collective-permute-start.1) | collective-permute-done | bytes 65568 | tf_op jit(solution)/shard_map/ppermute | solution.py:20
  23.8 3.1 %collective-permute-done.3.refs_4_ = bf16[512,512]{1,0:T(8,128)(2,1)S(1)} collective-permute-done((bf16[512,512]{1,0:T(8,128)(2,1)}, bf16[512,512]{1,0:T(8,128)(2,1)S(1)}, u32[]{:S(2)}, u32[]{:S(2)}) %collective-permute-start.3) | collective-permute-done | bytes 524320 | tf_op jit(solution)/shard_map/ppermute | solution.py:20
  27.0 2.5 %collective-permute-done.4.refs_5_ = bf16[512,512]{1,0:T(8,128)(2,1)S(1)} collective-permute-done((bf16[512,512]{1,0:T(8,128)(2,1)}, bf16[512,512]{1,0:T(8,128)(2,1)S(1)}, u32[]{:S(2)}, u32[]{:S(2)}) %collective-permute-start.4) | collective-permute-done | bytes 524320 | tf_op jit(solution)/shard_map/ppermute | solution.py:20
  29.5 2.5 %collective-permute-start.5 = (bf16[128,256]{1,0:T(8,128)(2,1)S(1)}, bf16[128,256]{1,0:T(8,128)(2,1)S(1)}, u32[]{:S(2)}, u32[]{:S(2)}) collective-permute-start(bf16[128,256]{1,0:T(8,128)(2,1)S(1)} %convert_element_type.64), channel_id=1, source_target_pairs={{0,12},{1,13},{2,14},{3,15},{4,8},{5,9},{6,10},{7,11},{8,4},{9,5},... | collective-permute-start | bytes 196616 | tf_op jit(solution)/shard_map/ppermute | solution.py:20
  32.1 1.9 %collective-permute-start.7 = (bf16[128,256]{1,0:T(8,128)(2,1)S(1)}, bf16[128,256]{1,0:T(8,128)(2,1)S(1)}, u32[]{:S(2)}, u32[]{:S(2)}) collective-permute-start(bf16[128,256]{1,0:T(8,128)(2,1)S(1)} %convert_element_type.64), channel_id=1, source_target_pairs={{0,4},{1,5},{2,6},{3,7},{4,0},{5,1},{6,2},{7,3},{8,12},{9,13},{10,... | collective-permute-start | bytes 196616 | tf_op jit(solution)/shard_map/ppermute | solution.py:20
  34.0 3.0 %pad_maximum_fusion = bf16[512,2048]{1,0:T(8,128)(2,1)} fusion(bf16[512,512]{1,0:T(8,128)(2,1)S(1)} %collective-permute-done.4.refs_5_, bf16[512,1536]{1,0:T(8,128)(2,1)} %slice.10), kind=kLoop, calls=%fused_computation | loop fusion | flops 4194304 | bytes 4194304 | tf_op jit(solution)/shard_map/concatenate | solution.py:284
  37.3 1.6 %collective-permute-start.10 = (bf16[128,256]{1,0:T(8,128)(2,1)S(1)}, bf16[128,256]{1,0:T(8,128)(2,1)S(1)}, u32[]{:S(2)}, u32[]{:S(2)}) collective-permute-start(bf16[128,256]{1,0:T(8,128)(2,1)S(1)} %convert_add_fusion.3), channel_id=1, source_target_pairs={{0,2},{1,3},{2,0},{3,1},{4,6},{5,7},{6,4},{7,5},{8,10},{9,11},{10,... | collective-permute-start | bytes 196616 | tf_op jit(solution)/shard_map/ppermute | solution.py:20
  39.5 1.5 %collective-permute-start.13 = (bf16[128,256]{1,0:T(8,128)(2,1)S(1)}, bf16[128,256]{1,0:T(8,128)(2,1)S(1)}, u32[]{:S(2)}, u32[]{:S(2)}) collective-permute-start(bf16[128,256]{1,0:T(8,128)(2,1)S(1)} %convert_add_fusion.3), channel_id=1, source_target_pairs={{0,16},{16,0},{1,17},{17,1},{2,18},{18,2},{3,19},{19,3},{4,20},{20... | collective-permute-start | bytes 196616 | tf_op jit(solution)/shard_map/ppermute | solution.py:25
  41.0 1.1 slice.11.refs_9_.refs_10_.refs_15_
  44.9 1.5 %collective-permute-start.33 = (bf16[512,2048]{1,0:T(8,128)(2,1)}, bf16[512,2048]{1,0:T(8,128)(2,1)}, u32[]{:S(2)}, u32[]{:S(2)}) collective-permute-start(bf16[512,2048]{1,0:T(8,128)(2,1)} %pad_maximum_fusion), channel_id=1, source_target_pairs={{0,16},{16,0},{1,17},{17,1},{2,18},{18,2},{3,19},{19,3},{4,20},{20... | collective-permute-start | bytes 6291464 | tf_op jit(solution)/shard_map/ppermute | solution.py:25
  46.4 12.1 %forward.1 = (bf16[512,2048]{1,0:T(8,128)(2,1)}, bf16[512,2048]{1,0:T(8,128)(2,1)}, f32[512,256]{1,0:T(8,128)}, bf16[512,512]{1,0:T(8,128)(2,1)}, bf16[512,512]{...) custom-call(bf16[512,512]{1,0:T(8,128)(2,1)} %refs_9_.3, ...), custom_call_target="tpu_custom_call" | custom-call | flops 1000 | bytes 1000 | tf_op jit(solution)/shard_map/forward/pallas_call | solution.py:319
  58.6 1.3 %collective-permute-start.23 = (bf16[128,256]{1,0:T(8,128)(2,1)S(1)}, bf16[128,256]{1,0:T(8,128)(2,1)S(1)}, u32[]{:S(2)}, u32[]{:S(2)}) collective-permute-start(bf16[128,256]{1,0:T(8,128)(2,1)S(1)} %collective-permute-done.13), channel_id=1, source_target_pairs={{0,2},{1,3},{2,0},{3,1},{4,6},{5,7},{6,4},{7,5},{8,10},{9,11},{10,... | collective-permute-start | bytes 196616 | tf_op jit(solution)/shard_map/ppermute | solution.py:20
  62.0 1.3 %collective-permute-start.17 = (bf16[128,256]{1,0:T(8,128)(2,1)S(1)}, bf16[128,256]{1,0:T(8,128)(2,1)S(1)}, u32[]{:S(2)}, u32[]{:S(2)}) collective-permute-start(bf16[128,256]{1,0:T(8,128)(2,1)S(1)} %get-tuple-element.97), channel_id=1, source_target_pairs={{0,2},{1,3},{2,0},{3,1},{4,6},{5,7},{6,4},{7,5},{8,10},{9,11},{10,... | collective-permute-start | bytes 196616 | tf_op jit(solution)/shard_map/ppermute | solution.py:20
  64.4 1.9 %collective-permute-done.17 = bf16[128,256]{1,0:T(8,128)(2,1)S(1)} collective-permute-done((bf16[128,256]{1,0:T(8,128)(2,1)S(1)}, bf16[128,256]{1,0:T(8,128)(2,1)S(1)}, u32[]{:S(2)}, u32[]{:S(2)}) %collective-permute-start.17) | collective-permute-done | bytes 65568 | tf_op jit(solution)/shard_map/ppermute | solution.py:20
  66.2 1.5 %collective-permute-done.18 = bf16[128,256]{1,0:T(8,128)(2,1)S(1)} collective-permute-done((bf16[128,256]{1,0:T(8,128)(2,1)S(1)}, bf16[128,256]{1,0:T(8,128)(2,1)S(1)}, u32[]{:S(2)}, u32[]{:S(2)}) %collective-permute-start.18) | collective-permute-done | bytes 65568 | tf_op jit(solution)/shard_map/ppermute | solution.py:20
  68.6 2.5 %collective-permute-start.19 = (bf16[128,256]{1,0:T(8,128)(2,1)S(1)}, bf16[128,256]{1,0:T(8,128)(2,1)S(1)}, u32[]{:S(2)}, u32[]{:S(2)}) collective-permute-start(bf16[128,256]{1,0:T(8,128)(2,1)S(1)} %get-tuple-element.93), channel_id=1, source_target_pairs={{0,12},{1,13},{2,14},{3,15},{4,8},{5,9},{6,10},{7,11},{8,4},{9,5},... | collective-permute-start | bytes 196616 | tf_op jit(solution)/shard_map/ppermute | solution.py:20
  71.2 1.9 %collective-permute-start.21 = (bf16[128,256]{1,0:T(8,128)(2,1)S(1)}, bf16[128,256]{1,0:T(8,128)(2,1)S(1)}, u32[]{:S(2)}, u32[]{:S(2)}) collective-permute-start(bf16[128,256]{1,0:T(8,128)(2,1)S(1)} %get-tuple-element.93), channel_id=1, source_target_pairs={{0,4},{1,5},{2,6},{3,7},{4,0},{5,1},{6,2},{7,3},{8,12},{9,13},{10,... | collective-permute-start | bytes 196616 | tf_op jit(solution)/shard_map/ppermute | solution.py:20
  73.2 2.3 %collective-permute-done.19 = bf16[128,256]{1,0:T(8,128)(2,1)S(1)} collective-permute-done((bf16[128,256]{1,0:T(8,128)(2,1)S(1)}, bf16[128,256]{1,0:T(8,128)(2,1)S(1)}, u32[]{:S(2)}, u32[]{:S(2)}) %collective-permute-start.19) | collective-permute-done | bytes 65568 | tf_op jit(solution)/shard_map/ppermute | solution.py:20
  75.5 2.1 %collective-permute-done.20 = bf16[128,256]{1,0:T(8,128)(2,1)S(1)} collective-permute-done((bf16[128,256]{1,0:T(8,128)(2,1)S(1)}, bf16[128,256]{1,0:T(8,128)(2,1)S(1)}, u32[]{:S(2)}, u32[]{:S(2)}) %collective-permute-start.20) | collective-permute-done | bytes 65568 | tf_op jit(solution)/shard_map/ppermute | solution.py:20
  77.8 1.2 %collective-permute-start.26 = (bf16[128,256]{1,0:T(8,128)(2,1)S(1)}, bf16[128,256]{1,0:T(8,128)(2,1)S(1)}, u32[]{:S(2)}, u32[]{:S(2)}) collective-permute-start(bf16[128,256]{1,0:T(8,128)(2,1)S(1)} %convert_add_fusion.1), channel_id=1, source_target_pairs={{0,2},{1,3},{2,0},{3,1},{4,6},{5,7},{6,4},{7,5},{8,10},{9,11},{10,... | collective-permute-start | bytes 196616 | tf_op jit(solution)/shard_map/ppermute | solution.py:20
  80.4 2.1 %collective-permute-done.26 = bf16[128,256]{1,0:T(8,128)(2,1)S(1)} collective-permute-done((bf16[128,256]{1,0:T(8,128)(2,1)S(1)}, bf16[128,256]{1,0:T(8,128)(2,1)S(1)}, u32[]{:S(2)}, u32[]{:S(2)}) %collective-permute-start.26) | collective-permute-done | bytes 65568 | tf_op jit(solution)/shard_map/ppermute | solution.py:20
  84.9 7.8 %collective-permute-done.33.refs_14_.refs_20_ = bf16[512,2048]{1,0:T(8,128)(2,1)} collective-permute-done((bf16[512,2048]{1,0:T(8,128)(2,1)}, bf16[512,2048]{1,0:T(8,128)(2,1)}, u32[]{:S(2)}, u32[]{:S(2)}) %collective-permute-start.33) | collective-permute-done | bytes 2097184 | tf_op jit(solution)/shard_map/ppermute | solution.py:25
  92.7 1.5 %collective-permute-start.34 = (bf16[512,256]{1,0:T(8,128)(2,1)S(1)}, bf16[512,256]{1,0:T(8,128)(2,1)S(1)}, u32[]{:S(2)}, u32[]{:S(2)}) collective-permute-start(bf16[512,256]{1,0:T(8,128)(2,1)S(1)} %pad_maximum_fusion.4.refs_7_), channel_id=1, source_target_pairs={{0,16},{16,0},{1,17},{17,1},{2,18},{18,2},{3,19},{19,3},{4,20},{20... | collective-permute-start | bytes 786440 | tf_op jit(solution)/shard_map/ppermute | solution.py:25
  94.3 12.9 %weight_grad.1 = (f32[4,7,128,512]{3,2,1,0:T(8,128)}, f32[256,2048]{1,0:T(8,128)}) custom-call(bf16[512,512]{1,0:T(8,128)(2,1)S(1)} %copy-done.1, bf16[512,512]{1,0:T(8,128)(2,1)S(1)} %copy-done.1, bf16[512,512]{1,0:T(8,128)(2,1)S(1)} %collective-permute-done.12.refs_2_, bf16[512,512]{1,0:T(8,128)(2,1)S(1)} %copy-done.9, bf16[512,512]{1,0:T(8,128)(2,1)S(1)} %copy-done.7, ...), custom_call_target="tpu_custom_call" | custom-call | flops 1000 | bytes 1000 | tf_op jit(solution)/shard_map/weight_grad/pallas_call | solution.py:372
  107.3 1.7 %finish.1 = (bf16[512,512]{1,0:T(8,128)(2,1)}, f32[512,256]{1,0:T(8,128)}) custom-call(bf16[512,512]{1,0:T(8,128)(2,1)S(1)} %copy-done.11, bf16[512,512]{1,0:T(8,128)(2,1)S(1)} %copy-done.12, bf16[512,512]{1,0:T(8,128)(2,1)S(1)} %collective-permute-done.28.refs_2_, bf16[512,512]{1,0:T(8,128)(2,1)S(1)} %collective-permute-done.29.refs_3_, ...), custom_call_target="tpu_custom_call" | custom-call | flops 1000 | bytes 1000 | tf_op jit(solution)/shard_map/finish/pallas_call | solution.py:391
  (91 shorter events, 12.6 us)
Async XLA Ops:
  0.7 26.3 %collective-permute-start.3 = (bf16[512,512]{1,0:T(8,128)(2,1)}, bf16[512,512]{1,0:T(8,128)(2,1)S(1)}, u32[]{:S(2)}, u32[]{:S(2)}) collective-permute-start(bf16[512,512]{1,0:T(8,128)(2,1)} %refs_9_.3), channel_id=1, source_target_pairs={{0,4},{1,5},{2,6},{3,7},{4,0},{5,1},{6,2},{7,3},{8,12},{9,13},{10,... | collective-permute-start | bytes 1572872 | tf_op jit(solution)/shard_map/ppermute | solution.py:20
  3.7 25.8 %collective-permute-start.4 = (bf16[512,512]{1,0:T(8,128)(2,1)}, bf16[512,512]{1,0:T(8,128)(2,1)S(1)}, u32[]{:S(2)}, u32[]{:S(2)}) collective-permute-start(bf16[512,512]{1,0:T(8,128)(2,1)} %refs_9_.3), channel_id=1, source_target_pairs={{0,8},{1,9},{2,10},{3,11},{4,12},{5,13},{6,14},{7,15},{8,0},{9,1},... | collective-permute-start | bytes 1572872 | tf_op jit(solution)/shard_map/ppermute | solution.py:20
  7.8 4.3 %collective-permute-start = (bf16[256,256]{1,0:T(8,128)(2,1)S(1)}, bf16[256,256]{1,0:T(8,128)(2,1)S(1)}, u32[]{:S(2)}, u32[]{:S(2)}) collective-permute-start(bf16[256,256]{1,0:T(8,128)(2,1)S(1)} %dynamic-slice_convert_fusion), channel_id=1, source_target_pairs={{0,1},{1,0},{2,3},{3,2},{4,5},{5,4},{6,7},{7,6},{8,9},{9,8},{10,11... | collective-permute-start | bytes 393224 | tf_op jit(solution)/shard_map/ppermute | solution.py:20
  7.8 16.0 %collective-permute-start.2 = (bf16[512,512]{1,0:T(8,128)(2,1)}, bf16[512,512]{1,0:T(8,128)(2,1)S(1)}, u32[]{:S(2)}, u32[]{:S(2)}) collective-permute-start(bf16[512,512]{1,0:T(8,128)(2,1)} %refs_9_.3), channel_id=1, source_target_pairs={{0,2},{1,3},{2,0},{3,1},{4,6},{5,7},{6,4},{7,5},{8,10},{9,11},{10,... | collective-permute-start | bytes 1572872 | tf_op jit(solution)/shard_map/ppermute | solution.py:20
  10.6 26.7 %collective-permute-start.8 = (bf16[512,1024]{1,0:T(8,128)(2,1)}, bf16[512,1024]{1,0:T(8,128)(2,1)}, u32[]{:S(2)}, u32[]{:S(2)}) collective-permute-start(bf16[512,1024]{1,0:T(8,128)(2,1)} %pad_maximum_fusion.1), channel_id=1, source_target_pairs={{0,16},{16,0},{1,17},{17,1},{2,18},{18,2},{3,19},{19,3},{4,20},{20... | collective-permute-start | bytes 3145736 | tf_op jit(solution)/shard_map/ppermute | solution.py:25
  12.1 11.7 %collective-permute-start.1 = (bf16[128,256]{1,0:T(8,128)(2,1)S(1)}, bf16[128,256]{1,0:T(8,128)(2,1)S(1)}, u32[]{:S(2)}, u32[]{:S(2)}) collective-permute-start(bf16[128,256]{1,0:T(8,128)(2,1)S(1)} %dynamic-slice_convert_fusion.4), channel_id=1, source_target_pairs={{0,2},{1,3},{2,0},{3,1},{4,6},{5,7},{6,4},{7,5},{8,10},{9,11},{10,... | collective-permute-start | bytes 196616 | tf_op jit(solution)/shard_map/ppermute | solution.py:20
  29.5 7.5 %collective-permute-start.5 = (bf16[128,256]{1,0:T(8,128)(2,1)S(1)}, bf16[128,256]{1,0:T(8,128)(2,1)S(1)}, u32[]{:S(2)}, u32[]{:S(2)}) collective-permute-start(bf16[128,256]{1,0:T(8,128)(2,1)S(1)} %convert_element_type.64), channel_id=1, source_target_pairs={{0,12},{1,13},{2,14},{3,15},{4,8},{5,9},{6,10},{7,11},{8,4},{9,5},... | collective-permute-start | bytes 196616 | tf_op jit(solution)/shard_map/ppermute | solution.py:20
  32.1 5.2 %collective-permute-start.6 = (bf16[128,256]{1,0:T(8,128)(2,1)S(1)}, bf16[128,256]{1,0:T(8,128)(2,1)S(1)}, u32[]{:S(2)}, u32[]{:S(2)}) collective-permute-start(bf16[128,256]{1,0:T(8,128)(2,1)S(1)} %convert_element_type.64), channel_id=1, source_target_pairs={{0,8},{1,9},{2,10},{3,11},{4,12},{5,13},{6,14},{7,15},{8,0},{9,1},... | collective-permute-start | bytes 196616 | tf_op jit(solution)/shard_map/ppermute | solution.py:20
  32.1 5.2 %collective-permute-start.7 = (bf16[128,256]{1,0:T(8,128)(2,1)S(1)}, bf16[128,256]{1,0:T(8,128)(2,1)S(1)}, u32[]{:S(2)}, u32[]{:S(2)}) collective-permute-start(bf16[128,256]{1,0:T(8,128)(2,1)S(1)} %convert_element_type.64), channel_id=1, source_target_pairs={{0,4},{1,5},{2,6},{3,7},{4,0},{5,1},{6,2},{7,3},{8,12},{9,13},{10,... | collective-permute-start | bytes 196616 | tf_op jit(solution)/shard_map/ppermute | solution.py:20
  37.3 4.9 %collective-permute-start.10 = (bf16[128,256]{1,0:T(8,128)(2,1)S(1)}, bf16[128,256]{1,0:T(8,128)(2,1)S(1)}, u32[]{:S(2)}, u32[]{:S(2)}) collective-permute-start(bf16[128,256]{1,0:T(8,128)(2,1)S(1)} %convert_add_fusion.3), channel_id=1, source_target_pairs={{0,2},{1,3},{2,0},{3,1},{4,6},{5,7},{6,4},{7,5},{8,10},{9,11},{10,... | collective-permute-start | bytes 196616 | tf_op jit(solution)/shard_map/ppermute | solution.py:20
  38.9 4.2 %collective-permute-start.11 = (bf16[128,256]{1,0:T(8,128)(2,1)S(1)}, bf16[128,256]{1,0:T(8,128)(2,1)S(1)}, u32[]{:S(2)}, u32[]{:S(2)}) collective-permute-start(bf16[128,256]{1,0:T(8,128)(2,1)S(1)} %convert_add_fusion.3), channel_id=1, source_target_pairs={{0,3},{1,2},{2,1},{3,0},{4,7},{5,6},{6,5},{7,4},{8,11},{9,10},{10,... | collective-permute-start | bytes 196616 | tf_op jit(solution)/shard_map/ppermute | solution.py:20
  38.9 4.2 %collective-permute-start.9 = (bf16[128,256]{1,0:T(8,128)(2,1)S(1)}, bf16[128,256]{1,0:T(8,128)(2,1)S(1)}, u32[]{:S(2)}, u32[]{:S(2)}) collective-permute-start(bf16[128,256]{1,0:T(8,128)(2,1)S(1)} %convert_add_fusion.3), channel_id=1, source_target_pairs={{0,1},{1,0},{2,3},{3,2},{4,5},{5,4},{6,7},{7,6},{8,9},{9,8},{10,11... | collective-permute-start | bytes 196616 | tf_op jit(solution)/shard_map/ppermute | solution.py:20
  39.5 5.4 %collective-permute-start.13 = (bf16[128,256]{1,0:T(8,128)(2,1)S(1)}, bf16[128,256]{1,0:T(8,128)(2,1)S(1)}, u32[]{:S(2)}, u32[]{:S(2)}) collective-permute-start(bf16[128,256]{1,0:T(8,128)(2,1)S(1)} %convert_add_fusion.3), channel_id=1, source_target_pairs={{0,16},{16,0},{1,17},{17,1},{2,18},{18,2},{3,19},{19,3},{4,20},{20... | collective-permute-start | bytes 196616 | tf_op jit(solution)/shard_map/ppermute | solution.py:25
  42.1 4.4 %collective-permute-start.12 = (bf16[512,512]{1,0:T(8,128)(2,1)S(1)}, bf16[512,512]{1,0:T(8,128)(2,1)S(1)}, u32[]{:S(2)}, u32[]{:S(2)}) collective-permute-start(bf16[512,512]{1,0:T(8,128)(2,1)S(1)} %copy-done), channel_id=1, source_target_pairs={{0,1},{1,0},{2,3},{3,2},{4,5},{5,4},{6,7},{7,6},{8,9},{9,8},{10,11... | collective-permute-start | bytes 1572872 | tf_op jit(solution)/shard_map/ppermute | solution.py:20
  43.1 16.9 %collective-permute-start.14 = (bf16[512,512]{1,0:T(8,128)(2,1)S(1)}, bf16[512,512]{1,0:T(8,128)(2,1)}, u32[]{:S(2)}, u32[]{:S(2)}) collective-permute-start(bf16[512,512]{1,0:T(8,128)(2,1)S(1)} %slice.11.refs_9_.refs_10_.refs_15_), channel_id=1, source_target_pairs={{0,2},{1,3},{2,0},{3,1},{4,6},{5,7},{6,4},{7,5},{8,10},{9,11},{10,... | collective-permute-start | bytes 1572872 | tf_op jit(solution)/shard_map/ppermute | solution.py:20
  43.9 16.6 %collective-permute-start.15 = (bf16[512,512]{1,0:T(8,128)(2,1)S(1)}, bf16[512,512]{1,0:T(8,128)(2,1)}, u32[]{:S(2)}, u32[]{:S(2)}) collective-permute-start(bf16[512,512]{1,0:T(8,128)(2,1)S(1)} %slice.11.refs_9_.refs_10_.refs_15_), channel_id=1, source_target_pairs={{0,4},{1,5},{2,6},{3,7},{4,0},{5,1},{6,2},{7,3},{8,12},{9,13},{10,... | collective-permute-start | bytes 1572872 | tf_op jit(solution)/shard_map/ppermute | solution.py:20
  44.9 47.8 %collective-permute-start.33 = (bf16[512,2048]{1,0:T(8,128)(2,1)}, bf16[512,2048]{1,0:T(8,128)(2,1)}, u32[]{:S(2)}, u32[]{:S(2)}) collective-permute-start(bf16[512,2048]{1,0:T(8,128)(2,1)} %pad_maximum_fusion), channel_id=1, source_target_pairs={{0,16},{16,0},{1,17},{17,1},{2,18},{18,2},{3,19},{19,3},{4,20},{20... | collective-permute-start | bytes 6291464 | tf_op jit(solution)/shard_map/ppermute | solution.py:25
  58.6 4.7 %collective-permute-start.23 = (bf16[128,256]{1,0:T(8,128)(2,1)S(1)}, bf16[128,256]{1,0:T(8,128)(2,1)S(1)}, u32[]{:S(2)}, u32[]{:S(2)}) collective-permute-start(bf16[128,256]{1,0:T(8,128)(2,1)S(1)} %collective-permute-done.13), channel_id=1, source_target_pairs={{0,2},{1,3},{2,0},{3,1},{4,6},{5,7},{6,4},{7,5},{8,10},{9,11},{10,... | collective-permute-start | bytes 196616 | tf_op jit(solution)/shard_map/ppermute | solution.py:20
  60.0 4.3 %collective-permute-start.24 = (bf16[128,256]{1,0:T(8,128)(2,1)S(1)}, bf16[128,256]{1,0:T(8,128)(2,1)S(1)}, u32[]{:S(2)}, u32[]{:S(2)}) collective-permute-start(bf16[128,256]{1,0:T(8,128)(2,1)S(1)} %collective-permute-done.13), channel_id=1, source_target_pairs={{0,3},{1,2},{2,1},{3,0},{4,7},{5,6},{6,5},{7,4},{8,11},{9,10},{10,... | collective-permute-start | bytes 196616 | tf_op jit(solution)/shard_map/ppermute | solution.py:20
  62.0 4.3 %collective-permute-start.17 = (bf16[128,256]{1,0:T(8,128)(2,1)S(1)}, bf16[128,256]{1,0:T(8,128)(2,1)S(1)}, u32[]{:S(2)}, u32[]{:S(2)}) collective-permute-start(bf16[128,256]{1,0:T(8,128)(2,1)S(1)} %get-tuple-element.97), channel_id=1, source_target_pairs={{0,2},{1,3},{2,0},{3,1},{4,6},{5,7},{6,4},{7,5},{8,10},{9,11},{10,... | collective-permute-start | bytes 196616 | tf_op jit(solution)/shard_map/ppermute | solution.py:20
  63.4 4.3 %collective-permute-start.18 = (bf16[128,256]{1,0:T(8,128)(2,1)S(1)}, bf16[128,256]{1,0:T(8,128)(2,1)S(1)}, u32[]{:S(2)}, u32[]{:S(2)}) collective-permute-start(bf16[128,256]{1,0:T(8,128)(2,1)S(1)} %get-tuple-element.96), channel_id=1, source_target_pairs={{0,3},{1,2},{2,1},{3,0},{4,7},{5,6},{6,5},{7,4},{8,11},{9,10},{10,... | collective-permute-start | bytes 196616 | tf_op jit(solution)/shard_map/ppermute | solution.py:20
  68.6 6.9 %collective-permute-start.19 = (bf16[128,256]{1,0:T(8,128)(2,1)S(1)}, bf16[128,256]{1,0:T(8,128)(2,1)S(1)}, u32[]{:S(2)}, u32[]{:S(2)}) collective-permute-start(bf16[128,256]{1,0:T(8,128)(2,1)S(1)} %get-tuple-element.93), channel_id=1, source_target_pairs={{0,12},{1,13},{2,14},{3,15},{4,8},{5,9},{6,10},{7,11},{8,4},{9,5},... | collective-permute-start | bytes 196616 | tf_op jit(solution)/shard_map/ppermute | solution.py:20
  71.2 6.4 %collective-permute-start.20 = (bf16[128,256]{1,0:T(8,128)(2,1)S(1)}, bf16[128,256]{1,0:T(8,128)(2,1)S(1)}, u32[]{:S(2)}, u32[]{:S(2)}) collective-permute-start(bf16[128,256]{1,0:T(8,128)(2,1)S(1)} %get-tuple-element.93), channel_id=1, source_target_pairs={{0,8},{1,9},{2,10},{3,11},{4,12},{5,13},{6,14},{7,15},{8,0},{9,1},... | collective-permute-start | bytes 196616 | tf_op jit(solution)/shard_map/ppermute | solution.py:20
  71.2 6.4 %collective-permute-start.21 = (bf16[128,256]{1,0:T(8,128)(2,1)S(1)}, bf16[128,256]{1,0:T(8,128)(2,1)S(1)}, u32[]{:S(2)}, u32[]{:S(2)}) collective-permute-start(bf16[128,256]{1,0:T(8,128)(2,1)S(1)} %get-tuple-element.93), channel_id=1, source_target_pairs={{0,4},{1,5},{2,6},{3,7},{4,0},{5,1},{6,2},{7,3},{8,12},{9,13},{10,... | collective-permute-start | bytes 196616 | tf_op jit(solution)/shard_map/ppermute | solution.py:20
  73.1 11.4 %collective-permute-start.32 = (bf16[512,512]{1,0:T(8,128)(2,1)S(1)}, bf16[512,512]{1,0:T(8,128)(2,1)S(1)}, u32[]{:S(2)}, u32[]{:S(2)}) collective-permute-start(bf16[512,512]{1,0:T(8,128)(2,1)S(1)} %slice.11.refs_9_.refs_10_.refs_15_), channel_id=1, source_target_pairs={{0,1},{1,0},{2,3},{3,2},{4,5},{5,4},{6,7},{7,6},{8,9},{9,8},{10,11... | collective-permute-start | bytes 1572872 | tf_op jit(solution)/shard_map/ppermute | solution.py:20
  77.8 4.8 %collective-permute-start.26 = (bf16[128,256]{1,0:T(8,128)(2,1)S(1)}, bf16[128,256]{1,0:T(8,128)(2,1)S(1)}, u32[]{:S(2)}, u32[]{:S(2)}) collective-permute-start(bf16[128,256]{1,0:T(8,128)(2,1)S(1)} %convert_add_fusion.1), channel_id=1, source_target_pairs={{0,2},{1,3},{2,0},{3,1},{4,6},{5,7},{6,4},{7,5},{8,10},{9,11},{10,... | collective-permute-start | bytes 196616 | tf_op jit(solution)/shard_map/ppermute | solution.py:20
  79.0 4.4 %collective-permute-start.27 = (bf16[128,256]{1,0:T(8,128)(2,1)S(1)}, bf16[128,256]{1,0:T(8,128)(2,1)S(1)}, u32[]{:S(2)}, u32[]{:S(2)}) collective-permute-start(bf16[128,256]{1,0:T(8,128)(2,1)S(1)} %convert_add_fusion.1), channel_id=1, source_target_pairs={{0,3},{1,2},{2,1},{3,0},{4,7},{5,6},{6,5},{7,4},{8,11},{9,10},{10,... | collective-permute-start | bytes 196616 | tf_op jit(solution)/shard_map/ppermute | solution.py:20
  79.6 27.6 %collective-permute-start.31 = (bf16[512,512]{1,0:T(8,128)(2,1)}, bf16[512,512]{1,0:T(8,128)(2,1)S(1)}, u32[]{:S(2)}, u32[]{:S(2)}) collective-permute-start(bf16[512,512]{1,0:T(8,128)(2,1)} %get-tuple-element.78), channel_id=1, source_target_pairs={{0,8},{1,9},{2,10},{3,11},{4,12},{5,13},{6,14},{7,15},{8,0},{9,1},... | collective-permute-start | bytes 1572872 | tf_op jit(solution)/shard_map/ppermute | solution.py:20
  82.5 24.7 %collective-permute-start.30 = (bf16[512,512]{1,0:T(8,128)(2,1)}, bf16[512,512]{1,0:T(8,128)(2,1)S(1)}, u32[]{:S(2)}, u32[]{:S(2)}) collective-permute-start(bf16[512,512]{1,0:T(8,128)(2,1)} %get-tuple-element.76), channel_id=1, source_target_pairs={{0,4},{1,5},{2,6},{3,7},{4,0},{5,1},{6,2},{7,3},{8,12},{9,13},{10,... | collective-permute-start | bytes 1572872 | tf_op jit(solution)/shard_map/ppermute | solution.py:20
  83.4 23.8 %collective-permute-start.29 = (bf16[512,512]{1,0:T(8,128)(2,1)}, bf16[512,512]{1,0:T(8,128)(2,1)S(1)}, u32[]{:S(2)}, u32[]{:S(2)}) collective-permute-start(bf16[512,512]{1,0:T(8,128)(2,1)} %get-tuple-element.74), channel_id=1, source_target_pairs={{0,2},{1,3},{2,0},{3,1},{4,6},{5,7},{6,4},{7,5},{8,10},{9,11},{10,... | collective-permute-start | bytes 1572872 | tf_op jit(solution)/shard_map/ppermute | solution.py:20
  84.5 22.8 %collective-permute-start.28 = (bf16[512,512]{1,0:T(8,128)(2,1)}, bf16[512,512]{1,0:T(8,128)(2,1)S(1)}, u32[]{:S(2)}, u32[]{:S(2)}) collective-permute-start(bf16[512,512]{1,0:T(8,128)(2,1)} %get-tuple-element.72), channel_id=1, source_target_pairs={{0,1},{1,0},{2,3},{3,2},{4,5},{5,4},{6,7},{7,6},{8,9},{9,8},{10,11... | collective-permute-start | bytes 1572872 | tf_op jit(solution)/shard_map/ppermute | solution.py:20
  92.7 14.4 %collective-permute-start.34 = (bf16[512,256]{1,0:T(8,128)(2,1)S(1)}, bf16[512,256]{1,0:T(8,128)(2,1)S(1)}, u32[]{:S(2)}, u32[]{:S(2)}) collective-permute-start(bf16[512,256]{1,0:T(8,128)(2,1)S(1)} %pad_maximum_fusion.4.refs_7_), channel_id=1, source_target_pairs={{0,16},{16,0},{1,17},{17,1},{2,18},{18,2},{3,19},{19,3},{4,20},{20... | collective-permute-start | bytes 786440 | tf_op jit(solution)/shard_map/ppermute | solution.py:25
  (18 other events, 320.6 us)

commit v6 on v5

--- a/solution.py
+++ b/solution.py
@@ -190,7 +190,15 @@
     grad = tn(x[...], d_low[...])
     for other in range(others):
         grad = grad + tn(rest[2 * other][...], rest[2 * other + 1][...])
-    d_u[...] = grad * scale
+    grad = grad * scale
+
+    @pl.when(pl.program_id(0) == 0)
+    def _():
+        d_u[...] = grad
+
+    @pl.when(pl.program_id(0) > 0)
+    def _():
+        d_u[...] += grad
 
 
 def column(rows, width, flip, base=0, at=0):
@@ -388,11 +396,15 @@
     last_arrays = [env.get(f"t{s}", terms[s]) for s in range(sections)] + [d_low, lr_u, inputs]
     for d in others:
         last_arrays += [env[f"in{d}"], env[f"d_low{d}"]]
+
+    def rows_of(columns):
+        return pl.BlockSpec((tokens // 2, columns), lambda i: (i, 0))
+
     d_inputs, d_u = call(
         functools.partial(finish_kernel, sections, data_groups - 1, scale),
-        1,
-        [resident(*a.shape) for a in last_arrays],
-        [resident(*narrow.shape), resident(*lr_u.shape)],
+        2,
+        [resident(*a.shape) if a is lr_u else rows_of(a.shape[1]) for a in last_arrays],
+        [rows_of(per_dev * width), resident(*lr_u.shape)],
         [narrow, jax.ShapeDtypeStruct(lr_u.shape, F32)],
         (1000, 1000),
         name="finish",

time: 109 us -> 110 us (level)
  no operation moved by 1% of the time
where the time goes in v6:
time: 110 us; the launch traced here: 109 us
  starting transfers between devices  36.1 us (33%)
  waiting for transfers between devices  33.6 us (31%)
  Pallas kernels  27 us (25%)
  other arithmetic  5.36 us (5%)
  local copies, waits for them, and re-layouts  4.9 us (4%)
  matrix products  1.4 us (1%)
    ppermute x31, starting transfers between devices, crossed(): return lax.ppermute(block, axis, [(i, i ^ mask) for i in range(count)])  30.1 us
    ppermute x31, waiting for transfers between devices, crossed(): return lax.ppermute(block, axis, [(i, i ^ mask) for i in range(count)])  25.8 us
    pallas_call x1, Pallas kernels, local(): call(functools.partial(weight_grad_kernel, sections, own, other, [p[0] fo...  12.9 us
    pallas_call x1, Pallas kernels, local(): call(functools.partial(forward_kernel, [1] * sections), per_dev, specs +...  12.1 us
    ppermute x4, waiting for transfers between devices, rolled(): lax.ppermute(block, axis, [(i, (i + shift) % count) for i in range(count)])  7.82 us
    ppermute x4, starting transfers between devices, rolled(): lax.ppermute(block, axis, [(i, (i + shift) % count) for i in range(count)])  5.98 us
    concatenate x1, other arithmetic, cut_rest(): jnp.concatenate(pieces, axis=1)  3.03 us
    slice x1, local copies, waits for them, and re-layouts, cut_rest(): pieces = [cotangent[:, lead * group:]] if per_dev > lead else []  2.65 us
  transfers between devices with their start and end apart: 35, of which 13 were waited for; matrix products, arithmetic and copies ran while one was open for 11% of the time, Pallas kernels for 23%

profile of v6, /device:TPU:0, one launch (start us, length us, event | category | flops | bytes accessed | tf_op | source)
XLA Modules:
  0.0 109.4 jit_solution(2587081028294243236)
XLA Ops:
  0.7 3.1 %collective-permute-start.3 = (bf16[512,512]{1,0:T(8,128)(2,1)}, bf16[512,512]{1,0:T(8,128)(2,1)S(1)}, u32[]{:S(2)}, u32[]{:S(2)}) collective-permute-start(bf16[512,512]{1,0:T(8,128)(2,1)} %refs_9_.3), channel_id=1, source_target_pairs={{0,4},{1,5},{2,6},{3,7},{4,0},{5,1},{6,2},{7,3},{8,12},{9,13},{10,... | collective-permute-start | bytes 1572872 | tf_op jit(solution)/shard_map/ppermute | solution.py:20
  3.7 2.6 %collective-permute-start.4 = (bf16[512,512]{1,0:T(8,128)(2,1)}, bf16[512,512]{1,0:T(8,128)(2,1)S(1)}, u32[]{:S(2)}, u32[]{:S(2)}) collective-permute-start(bf16[512,512]{1,0:T(8,128)(2,1)} %refs_9_.3), channel_id=1, source_target_pairs={{0,8},{1,9},{2,10},{3,11},{4,12},{5,13},{6,14},{7,15},{8,0},{9,1},... | collective-permute-start | bytes 1572872 | tf_op jit(solution)/shard_map/ppermute | solution.py:20
  6.3 1.4 %fusion.1 = f32[512,256]{1,0:T(8,128)S(1)} fusion(bf16[512,512]{1,0:T(8,128)(2,1)} %refs_9_.3, bf16[512,256]{1,0:T(8,128)(2,1)} %refs_8_.1), kind=kOutput, calls=%fused_computation.40 | convolution fusion | flops 134217728 | bytes 1310720 | tf_op jit(solution)/shard_map/dot_general | solution.py:280
  7.8 1.6 %collective-permute-start.2 = (bf16[512,512]{1,0:T(8,128)(2,1)}, bf16[512,512]{1,0:T(8,128)(2,1)S(1)}, u32[]{:S(2)}, u32[]{:S(2)}) collective-permute-start(bf16[512,512]{1,0:T(8,128)(2,1)} %refs_9_.3), channel_id=1, source_target_pairs={{0,2},{1,3},{2,0},{3,1},{4,6},{5,7},{6,4},{7,5},{8,10},{9,11},{10,... | collective-permute-start | bytes 1572872 | tf_op jit(solution)/shard_map/ppermute | solution.py:20
  9.4 1.1 %pad_maximum_fusion.1 = bf16[512,1024]{1,0:T(8,128)(2,1)} fusion(bf16[512,512]{1,0:T(8,128)(2,1)S(1)} %copy-done, bf16[512,512]{1,0:T(8,128)(2,1)S(1)} %slice-done), kind=kLoop, calls=%fused_computation.1 | loop fusion | flops 2097152 | bytes 2097152 | tf_op jit(solution)/shard_map/concatenate | solution.py:285
  10.6 1.5 %collective-permute-start.8 = (bf16[512,1024]{1,0:T(8,128)(2,1)}, bf16[512,1024]{1,0:T(8,128)(2,1)}, u32[]{:S(2)}, u32[]{:S(2)}) collective-permute-start(bf16[512,1024]{1,0:T(8,128)(2,1)} %pad_maximum_fusion.1), channel_id=1, source_target_pairs={{0,16},{16,0},{1,17},{17,1},{2,18},{18,2},{3,19},{19,3},{4,20},{20... | collective-permute-start | bytes 3145736 | tf_op jit(solution)/shard_map/ppermute | solution.py:25
  12.7 2.7 %slice.10 = bf16[512,1536]{1,0:T(8,128)(2,1)} slice(bf16[512,2048]{1,0:T(8,128)(2,1)} %refs_10_.1), slice={[0:512], [512:2048]} | slice | bytes 3145728 | tf_op jit(solution)/shard_map/slice | solution.py:290
  15.3 8.5 %collective-permute-done.1 = bf16[128,256]{1,0:T(8,128)(2,1)S(1)} collective-permute-done((bf16[128,256]{1,0:T(8,128)(2,1)S(1)}, bf16[128,256]{1,0:T(8,128)(2,1)S(1)}, u32[]{:S(2)}, u32[]{:S(2)}) %collective-permute-start.1) | collective-permute-done | bytes 65568 | tf_op jit(solution)/shard_map/ppermute | solution.py:20
  23.8 3.1 %collective-permute-done.3.refs_4_ = bf16[512,512]{1,0:T(8,128)(2,1)S(1)} collective-permute-done((bf16[512,512]{1,0:T(8,128)(2,1)}, bf16[512,512]{1,0:T(8,128)(2,1)S(1)}, u32[]{:S(2)}, u32[]{:S(2)}) %collective-permute-start.3) | collective-permute-done | bytes 524320 | tf_op jit(solution)/shard_map/ppermute | solution.py:20
  27.0 2.5 %collective-permute-done.4.refs_5_ = bf16[512,512]{1,0:T(8,128)(2,1)S(1)} collective-permute-done((bf16[512,512]{1,0:T(8,128)(2,1)}, bf16[512,512]{1,0:T(8,128)(2,1)S(1)}, u32[]{:S(2)}, u32[]{:S(2)}) %collective-permute-start.4) | collective-permute-done | bytes 524320 | tf_op jit(solution)/shard_map/ppermute | solution.py:20
  29.5 2.5 %collective-permute-start.5 = (bf16[128,256]{1,0:T(8,128)(2,1)S(1)}, bf16[128,256]{1,0:T(8,128)(2,1)S(1)}, u32[]{:S(2)}, u32[]{:S(2)}) collective-permute-start(bf16[128,256]{1,0:T(8,128)(2,1)S(1)} %convert_element_type.64), channel_id=1, source_target_pairs={{0,12},{1,13},{2,14},{3,15},{4,8},{5,9},{6,10},{7,11},{8,4},{9,5},... | collective-permute-start | bytes 196616 | tf_op jit(solution)/shard_map/ppermute | solution.py:20
  32.1 1.9 %collective-permute-start.7 = (bf16[128,256]{1,0:T(8,128)(2,1)S(1)}, bf16[128,256]{1,0:T(8,128)(2,1)S(1)}, u32[]{:S(2)}, u32[]{:S(2)}) collective-permute-start(bf16[128,256]{1,0:T(8,128)(2,1)S(1)} %convert_element_type.64), channel_id=1, source_target_pairs={{0,4},{1,5},{2,6},{3,7},{4,0},{5,1},{6,2},{7,3},{8,12},{9,13},{10,... | collective-permute-start | bytes 196616 | tf_op jit(solution)/shard_map/ppermute | solution.py:20
  34.0 3.0 %pad_maximum_fusion = bf16[512,2048]{1,0:T(8,128)(2,1)} fusion(bf16[512,512]{1,0:T(8,128)(2,1)S(1)} %collective-permute-done.4.refs_5_, bf16[512,1536]{1,0:T(8,128)(2,1)} %slice.10), kind=kLoop, calls=%fused_computation | loop fusion | flops 4194304 | bytes 4194304 | tf_op jit(solution)/shard_map/concatenate | solution.py:292
  37.3 1.6 %collective-permute-start.10 = (bf16[128,256]{1,0:T(8,128)(2,1)S(1)}, bf16[128,256]{1,0:T(8,128)(2,1)S(1)}, u32[]{:S(2)}, u32[]{:S(2)}) collective-permute-start(bf16[128,256]{1,0:T(8,128)(2,1)S(1)} %convert_add_fusion.3), channel_id=1, source_target_pairs={{0,2},{1,3},{2,0},{3,1},{4,6},{5,7},{6,4},{7,5},{8,10},{9,11},{10,... | collective-permute-start | bytes 196616 | tf_op jit(solution)/shard_map/ppermute | solution.py:20
  39.5 1.5 %collective-permute-start.13 = (bf16[128,256]{1,0:T(8,128)(2,1)S(1)}, bf16[128,256]{1,0:T(8,128)(2,1)S(1)}, u32[]{:S(2)}, u32[]{:S(2)}) collective-permute-start(bf16[128,256]{1,0:T(8,128)(2,1)S(1)} %convert_add_fusion.3), channel_id=1, source_target_pairs={{0,16},{16,0},{1,17},{17,1},{2,18},{18,2},{3,19},{19,3},{4,20},{20... | collective-permute-start | bytes 196616 | tf_op jit(solution)/shard_map/ppermute | solution.py:25
  41.0 1.1 slice.11.refs_9_.refs_10_.refs_15_
  44.9 1.5 %collective-permute-start.33 = (bf16[512,2048]{1,0:T(8,128)(2,1)}, bf16[512,2048]{1,0:T(8,128)(2,1)}, u32[]{:S(2)}, u32[]{:S(2)}) collective-permute-start(bf16[512,2048]{1,0:T(8,128)(2,1)} %pad_maximum_fusion), channel_id=1, source_target_pairs={{0,16},{16,0},{1,17},{17,1},{2,18},{18,2},{3,19},{19,3},{4,20},{20... | collective-permute-start | bytes 6291464 | tf_op jit(solution)/shard_map/ppermute | solution.py:25
  46.4 12.1 %forward.1 = (bf16[512,2048]{1,0:T(8,128)(2,1)}, bf16[512,2048]{1,0:T(8,128)(2,1)}, f32[512,256]{1,0:T(8,128)}, bf16[512,512]{1,0:T(8,128)(2,1)}, bf16[512,512]{...) custom-call(bf16[512,512]{1,0:T(8,128)(2,1)} %refs_9_.3, ...), custom_call_target="tpu_custom_call" | custom-call | flops 1000 | bytes 1000 | tf_op jit(solution)/shard_map/forward/pallas_call | solution.py:327
  58.6 1.3 %collective-permute-start.23 = (bf16[128,256]{1,0:T(8,128)(2,1)S(1)}, bf16[128,256]{1,0:T(8,128)(2,1)S(1)}, u32[]{:S(2)}, u32[]{:S(2)}) collective-permute-start(bf16[128,256]{1,0:T(8,128)(2,1)S(1)} %collective-permute-done.13), channel_id=1, source_target_pairs={{0,2},{1,3},{2,0},{3,1},{4,6},{5,7},{6,4},{7,5},{8,10},{9,11},{10,... | collective-permute-start | bytes 196616 | tf_op jit(solution)/shard_map/ppermute | solution.py:20
  62.0 1.3 %collective-permute-start.17 = (bf16[128,256]{1,0:T(8,128)(2,1)S(1)}, bf16[128,256]{1,0:T(8,128)(2,1)S(1)}, u32[]{:S(2)}, u32[]{:S(2)}) collective-permute-start(bf16[128,256]{1,0:T(8,128)(2,1)S(1)} %get-tuple-element.97), channel_id=1, source_target_pairs={{0,2},{1,3},{2,0},{3,1},{4,6},{5,7},{6,4},{7,5},{8,10},{9,11},{10,... | collective-permute-start | bytes 196616 | tf_op jit(solution)/shard_map/ppermute | solution.py:20
  64.4 1.9 %collective-permute-done.17 = bf16[128,256]{1,0:T(8,128)(2,1)S(1)} collective-permute-done((bf16[128,256]{1,0:T(8,128)(2,1)S(1)}, bf16[128,256]{1,0:T(8,128)(2,1)S(1)}, u32[]{:S(2)}, u32[]{:S(2)}) %collective-permute-start.17) | collective-permute-done | bytes 65568 | tf_op jit(solution)/shard_map/ppermute | solution.py:20
  66.2 1.5 %collective-permute-done.18 = bf16[128,256]{1,0:T(8,128)(2,1)S(1)} collective-permute-done((bf16[128,256]{1,0:T(8,128)(2,1)S(1)}, bf16[128,256]{1,0:T(8,128)(2,1)S(1)}, u32[]{:S(2)}, u32[]{:S(2)}) %collective-permute-start.18) | collective-permute-done | bytes 65568 | tf_op jit(solution)/shard_map/ppermute | solution.py:20
  68.6 2.5 %collective-permute-start.19 = (bf16[128,256]{1,0:T(8,128)(2,1)S(1)}, bf16[128,256]{1,0:T(8,128)(2,1)S(1)}, u32[]{:S(2)}, u32[]{:S(2)}) collective-permute-start(bf16[128,256]{1,0:T(8,128)(2,1)S(1)} %get-tuple-element.93), channel_id=1, source_target_pairs={{0,12},{1,13},{2,14},{3,15},{4,8},{5,9},{6,10},{7,11},{8,4},{9,5},... | collective-permute-start | bytes 196616 | tf_op jit(solution)/shard_map/ppermute | solution.py:20
  71.2 1.9 %collective-permute-start.21 = (bf16[128,256]{1,0:T(8,128)(2,1)S(1)}, bf16[128,256]{1,0:T(8,128)(2,1)S(1)}, u32[]{:S(2)}, u32[]{:S(2)}) collective-permute-start(bf16[128,256]{1,0:T(8,128)(2,1)S(1)} %get-tuple-element.93), channel_id=1, source_target_pairs={{0,4},{1,5},{2,6},{3,7},{4,0},{5,1},{6,2},{7,3},{8,12},{9,13},{10,... | collective-permute-start | bytes 196616 | tf_op jit(solution)/shard_map/ppermute | solution.py:20
  73.2 2.3 %collective-permute-done.19 = bf16[128,256]{1,0:T(8,128)(2,1)S(1)} collective-permute-done((bf16[128,256]{1,0:T(8,128)(2,1)S(1)}, bf16[128,256]{1,0:T(8,128)(2,1)S(1)}, u32[]{:S(2)}, u32[]{:S(2)}) %collective-permute-start.19) | collective-permute-done | bytes 65568 | tf_op jit(solution)/shard_map/ppermute | solution.py:20
  75.5 2.1 %collective-permute-done.20 = bf16[128,256]{1,0:T(8,128)(2,1)S(1)} collective-permute-done((bf16[128,256]{1,0:T(8,128)(2,1)S(1)}, bf16[128,256]{1,0:T(8,128)(2,1)S(1)}, u32[]{:S(2)}, u32[]{:S(2)}) %collective-permute-start.20) | collective-permute-done | bytes 65568 | tf_op jit(solution)/shard_map/ppermute | solution.py:20
  77.8 1.2 %collective-permute-start.26 = (bf16[128,256]{1,0:T(8,128)(2,1)S(1)}, bf16[128,256]{1,0:T(8,128)(2,1)S(1)}, u32[]{:S(2)}, u32[]{:S(2)}) collective-permute-start(bf16[128,256]{1,0:T(8,128)(2,1)S(1)} %convert_add_fusion.1), channel_id=1, source_target_pairs={{0,2},{1,3},{2,0},{3,1},{4,6},{5,7},{6,4},{7,5},{8,10},{9,11},{10,... | collective-permute-start | bytes 196616 | tf_op jit(solution)/shard_map/ppermute | solution.py:20
  80.4 2.1 %collective-permute-done.26 = bf16[128,256]{1,0:T(8,128)(2,1)S(1)} collective-permute-done((bf16[128,256]{1,0:T(8,128)(2,1)S(1)}, bf16[128,256]{1,0:T(8,128)(2,1)S(1)}, u32[]{:S(2)}, u32[]{:S(2)}) %collective-permute-start.26) | collective-permute-done | bytes 65568 | tf_op jit(solution)/shard_map/ppermute | solution.py:20
  84.9 7.8 %collective-permute-done.33.refs_14_.refs_20_ = bf16[512,2048]{1,0:T(8,128)(2,1)} collective-permute-done((bf16[512,2048]{1,0:T(8,128)(2,1)}, bf16[512,2048]{1,0:T(8,128)(2,1)}, u32[]{:S(2)}, u32[]{:S(2)}) %collective-permute-start.33) | collective-permute-done | bytes 2097184 | tf_op jit(solution)/shard_map/ppermute | solution.py:25
  92.7 1.5 %collective-permute-start.34 = (bf16[512,256]{1,0:T(8,128)(2,1)S(1)}, bf16[512,256]{1,0:T(8,128)(2,1)S(1)}, u32[]{:S(2)}, u32[]{:S(2)}) collective-permute-start(bf16[512,256]{1,0:T(8,128)(2,1)S(1)} %pad_maximum_fusion.4.refs_7_), channel_id=1, source_target_pairs={{0,16},{16,0},{1,17},{17,1},{2,18},{18,2},{3,19},{19,3},{4,20},{20... | collective-permute-start | bytes 786440 | tf_op jit(solution)/shard_map/ppermute | solution.py:25
  94.3 12.9 %weight_grad.1 = (f32[4,7,128,512]{3,2,1,0:T(8,128)}, f32[256,2048]{1,0:T(8,128)}) custom-call(bf16[512,512]{1,0:T(8,128)(2,1)S(1)} %copy-done.1, bf16[512,512]{1,0:T(8,128)(2,1)S(1)} %copy-done.1, bf16[512,512]{1,0:T(8,128)(2,1)S(1)} %collective-permute-done.12.refs_2_, bf16[512,512]{1,0:T(8,128)(2,1)S(1)} %copy-done.9, bf16[512,512]{1,0:T(8,128)(2,1)S(1)} %copy-done.7, ...), custom_call_target="tpu_custom_call" | custom-call | flops 1000 | bytes 1000 | tf_op jit(solution)/shard_map/weight_grad/pallas_call | solution.py:380
  107.3 2.1 %finish.1 = (bf16[512,512]{1,0:T(8,128)(2,1)}, f32[512,256]{1,0:T(8,128)}) custom-call(bf16[512,512]{1,0:T(8,128)(2,1)S(1)} %copy-done.11, bf16[512,512]{1,0:T(8,128)(2,1)S(1)} %copy-done.12, bf16[512,512]{1,0:T(8,128)(2,1)S(1)} %collective-permute-done.28.refs_2_, bf16[512,512]{1,0:T(8,128)(2,1)S(1)} %collective-permute-done.29.refs_3_, ...), custom_call_target="tpu_custom_call" | custom-call | flops 1000 | bytes 1000 | tf_op jit(solution)/shard_map/finish/pallas_call | solution.py:403
  (91 shorter events, 12.6 us)
Async XLA Ops:
  0.7 26.3 %collective-permute-start.3 = (bf16[512,512]{1,0:T(8,128)(2,1)}, bf16[512,512]{1,0:T(8,128)(2,1)S(1)}, u32[]{:S(2)}, u32[]{:S(2)}) collective-permute-start(bf16[512,512]{1,0:T(8,128)(2,1)} %refs_9_.3), channel_id=1, source_target_pairs={{0,4},{1,5},{2,6},{3,7},{4,0},{5,1},{6,2},{7,3},{8,12},{9,13},{10,... | collective-permute-start | bytes 1572872 | tf_op jit(solution)/shard_map/ppermute | solution.py:20
  3.7 25.8 %collective-permute-start.4 = (bf16[512,512]{1,0:T(8,128)(2,1)}, bf16[512,512]{1,0:T(8,128)(2,1)S(1)}, u32[]{:S(2)}, u32[]{:S(2)}) collective-permute-start(bf16[512,512]{1,0:T(8,128)(2,1)} %refs_9_.3), channel_id=1, source_target_pairs={{0,8},{1,9},{2,10},{3,11},{4,12},{5,13},{6,14},{7,15},{8,0},{9,1},... | collective-permute-start | bytes 1572872 | tf_op jit(solution)/shard_map/ppermute | solution.py:20
  7.8 4.3 %collective-permute-start = (bf16[256,256]{1,0:T(8,128)(2,1)S(1)}, bf16[256,256]{1,0:T(8,128)(2,1)S(1)}, u32[]{:S(2)}, u32[]{:S(2)}) collective-permute-start(bf16[256,256]{1,0:T(8,128)(2,1)S(1)} %dynamic-slice_convert_fusion), channel_id=1, source_target_pairs={{0,1},{1,0},{2,3},{3,2},{4,5},{5,4},{6,7},{7,6},{8,9},{9,8},{10,11... | collective-permute-start | bytes 393224 | tf_op jit(solution)/shard_map/ppermute | solution.py:20
  7.8 16.0 %collective-permute-start.2 = (bf16[512,512]{1,0:T(8,128)(2,1)}, bf16[512,512]{1,0:T(8,128)(2,1)S(1)}, u32[]{:S(2)}, u32[]{:S(2)}) collective-permute-start(bf16[512,512]{1,0:T(8,128)(2,1)} %refs_9_.3), channel_id=1, source_target_pairs={{0,2},{1,3},{2,0},{3,1},{4,6},{5,7},{6,4},{7,5},{8,10},{9,11},{10,... | collective-permute-start | bytes 1572872 | tf_op jit(solution)/shard_map/ppermute | solution.py:20
  10.6 26.7 %collective-permute-start.8 = (bf16[512,1024]{1,0:T(8,128)(2,1)}, bf16[512,1024]{1,0:T(8,128)(2,1)}, u32[]{:S(2)}, u32[]{:S(2)}) collective-permute-start(bf16[512,1024]{1,0:T(8,128)(2,1)} %pad_maximum_fusion.1), channel_id=1, source_target_pairs={{0,16},{16,0},{1,17},{17,1},{2,18},{18,2},{3,19},{19,3},{4,20},{20... | collective-permute-start | bytes 3145736 | tf_op jit(solution)/shard_map/ppermute | solution.py:25
  12.1 11.7 %collective-permute-start.1 = (bf16[128,256]{1,0:T(8,128)(2,1)S(1)}, bf16[128,256]{1,0:T(8,128)(2,1)S(1)}, u32[]{:S(2)}, u32[]{:S(2)}) collective-permute-start(bf16[128,256]{1,0:T(8,128)(2,1)S(1)} %dynamic-slice_convert_fusion.4), channel_id=1, source_target_pairs={{0,2},{1,3},{2,0},{3,1},{4,6},{5,7},{6,4},{7,5},{8,10},{9,11},{10,... | collective-permute-start | bytes 196616 | tf_op jit(solution)/shard_map/ppermute | solution.py:20
  29.5 7.5 %collective-permute-start.5 = (bf16[128,256]{1,0:T(8,128)(2,1)S(1)}, bf16[128,256]{1,0:T(8,128)(2,1)S(1)}, u32[]{:S(2)}, u32[]{:S(2)}) collective-permute-start(bf16[128,256]{1,0:T(8,128)(2,1)S(1)} %convert_element_type.64), channel_id=1, source_target_pairs={{0,12},{1,13},{2,14},{3,15},{4,8},{5,9},{6,10},{7,11},{8,4},{9,5},... | collective-permute-start | bytes 196616 | tf_op jit(solution)/shard_map/ppermute | solution.py:20
  32.1 5.2 %collective-permute-start.6 = (bf16[128,256]{1,0:T(8,128)(2,1)S(1)}, bf16[128,256]{1,0:T(8,128)(2,1)S(1)}, u32[]{:S(2)}, u32[]{:S(2)}) collective-permute-start(bf16[128,256]{1,0:T(8,128)(2,1)S(1)} %convert_element_type.64), channel_id=1, source_target_pairs={{0,8},{1,9},{2,10},{3,11},{4,12},{5,13},{6,14},{7,15},{8,0},{9,1},... | collective-permute-start | bytes 196616 | tf_op jit(solution)/shard_map/ppermute | solution.py:20
  32.1 5.2 %collective-permute-start.7 = (bf16[128,256]{1,0:T(8,128)(2,1)S(1)}, bf16[128,256]{1,0:T(8,128)(2,1)S(1)}, u32[]{:S(2)}, u32[]{:S(2)}) collective-permute-start(bf16[128,256]{1,0:T(8,128)(2,1)S(1)} %convert_element_type.64), channel_id=1, source_target_pairs={{0,4},{1,5},{2,6},{3,7},{4,0},{5,1},{6,2},{7,3},{8,12},{9,13},{10,... | collective-permute-start | bytes 196616 | tf_op jit(solution)/shard_map/ppermute | solution.py:20
  37.3 4.9 %collective-permute-start.10 = (bf16[128,256]{1,0:T(8,128)(2,1)S(1)}, bf16[128,256]{1,0:T(8,128)(2,1)S(1)}, u32[]{:S(2)}, u32[]{:S(2)}) collective-permute-start(bf16[128,256]{1,0:T(8,128)(2,1)S(1)} %convert_add_fusion.3), channel_id=1, source_target_pairs={{0,2},{1,3},{2,0},{3,1},{4,6},{5,7},{6,4},{7,5},{8,10},{9,11},{10,... | collective-permute-start | bytes 196616 | tf_op jit(solution)/shard_map/ppermute | solution.py:20
  38.9 4.2 %collective-permute-start.11 = (bf16[128,256]{1,0:T(8,128)(2,1)S(1)}, bf16[128,256]{1,0:T(8,128)(2,1)S(1)}, u32[]{:S(2)}, u32[]{:S(2)}) collective-permute-start(bf16[128,256]{1,0:T(8,128)(2,1)S(1)} %convert_add_fusion.3), channel_id=1, source_target_pairs={{0,3},{1,2},{2,1},{3,0},{4,7},{5,6},{6,5},{7,4},{8,11},{9,10},{10,... | collective-permute-start | bytes 196616 | tf_op jit(solution)/shard_map/ppermute | solution.py:20
  38.9 4.2 %collective-permute-start.9 = (bf16[128,256]{1,0:T(8,128)(2,1)S(1)}, bf16[128,256]{1,0:T(8,128)(2,1)S(1)}, u32[]{:S(2)}, u32[]{:S(2)}) collective-permute-start(bf16[128,256]{1,0:T(8,128)(2,1)S(1)} %convert_add_fusion.3), channel_id=1, source_target_pairs={{0,1},{1,0},{2,3},{3,2},{4,5},{5,4},{6,7},{7,6},{8,9},{9,8},{10,11... | collective-permute-start | bytes 196616 | tf_op jit(solution)/shard_map/ppermute | solution.py:20
  39.5 5.4 %collective-permute-start.13 = (bf16[128,256]{1,0:T(8,128)(2,1)S(1)}, bf16[128,256]{1,0:T(8,128)(2,1)S(1)}, u32[]{:S(2)}, u32[]{:S(2)}) collective-permute-start(bf16[128,256]{1,0:T(8,128)(2,1)S(1)} %convert_add_fusion.3), channel_id=1, source_target_pairs={{0,16},{16,0},{1,17},{17,1},{2,18},{18,2},{3,19},{19,3},{4,20},{20... | collective-permute-start | bytes 196616 | tf_op jit(solution)/shard_map/ppermute | solution.py:25
  42.1 4.4 %collective-permute-start.12 = (bf16[512,512]{1,0:T(8,128)(2,1)S(1)}, bf16[512,512]{1,0:T(8,128)(2,1)S(1)}, u32[]{:S(2)}, u32[]{:S(2)}) collective-permute-start(bf16[512,512]{1,0:T(8,128)(2,1)S(1)} %copy-done), channel_id=1, source_target_pairs={{0,1},{1,0},{2,3},{3,2},{4,5},{5,4},{6,7},{7,6},{8,9},{9,8},{10,11... | collective-permute-start | bytes 1572872 | tf_op jit(solution)/shard_map/ppermute | solution.py:20
  43.1 16.9 %collective-permute-start.14 = (bf16[512,512]{1,0:T(8,128)(2,1)S(1)}, bf16[512,512]{1,0:T(8,128)(2,1)}, u32[]{:S(2)}, u32[]{:S(2)}) collective-permute-start(bf16[512,512]{1,0:T(8,128)(2,1)S(1)} %slice.11.refs_9_.refs_10_.refs_15_), channel_id=1, source_target_pairs={{0,2},{1,3},{2,0},{3,1},{4,6},{5,7},{6,4},{7,5},{8,10},{9,11},{10,... | collective-permute-start | bytes 1572872 | tf_op jit(solution)/shard_map/ppermute | solution.py:20
  43.9 16.6 %collective-permute-start.15 = (bf16[512,512]{1,0:T(8,128)(2,1)S(1)}, bf16[512,512]{1,0:T(8,128)(2,1)}, u32[]{:S(2)}, u32[]{:S(2)}) collective-permute-start(bf16[512,512]{1,0:T(8,128)(2,1)S(1)} %slice.11.refs_9_.refs_10_.refs_15_), channel_id=1, source_target_pairs={{0,4},{1,5},{2,6},{3,7},{4,0},{5,1},{6,2},{7,3},{8,12},{9,13},{10,... | collective-permute-start | bytes 1572872 | tf_op jit(solution)/shard_map/ppermute | solution.py:20
  44.9 47.8 %collective-permute-start.33 = (bf16[512,2048]{1,0:T(8,128)(2,1)}, bf16[512,2048]{1,0:T(8,128)(2,1)}, u32[]{:S(2)}, u32[]{:S(2)}) collective-permute-start(bf16[512,2048]{1,0:T(8,128)(2,1)} %pad_maximum_fusion), channel_id=1, source_target_pairs={{0,16},{16,0},{1,17},{17,1},{2,18},{18,2},{3,19},{19,3},{4,20},{20... | collective-permute-start | bytes 6291464 | tf_op jit(solution)/shard_map/ppermute | solution.py:25
  58.6 4.7 %collective-permute-start.23 = (bf16[128,256]{1,0:T(8,128)(2,1)S(1)}, bf16[128,256]{1,0:T(8,128)(2,1)S(1)}, u32[]{:S(2)}, u32[]{:S(2)}) collective-permute-start(bf16[128,256]{1,0:T(8,128)(2,1)S(1)} %collective-permute-done.13), channel_id=1, source_target_pairs={{0,2},{1,3},{2,0},{3,1},{4,6},{5,7},{6,4},{7,5},{8,10},{9,11},{10,... | collective-permute-start | bytes 196616 | tf_op jit(solution)/shard_map/ppermute | solution.py:20
  60.0 4.3 %collective-permute-start.24 = (bf16[128,256]{1,0:T(8,128)(2,1)S(1)}, bf16[128,256]{1,0:T(8,128)(2,1)S(1)}, u32[]{:S(2)}, u32[]{:S(2)}) collective-permute-start(bf16[128,256]{1,0:T(8,128)(2,1)S(1)} %collective-permute-done.13), channel_id=1, source_target_pairs={{0,3},{1,2},{2,1},{3,0},{4,7},{5,6},{6,5},{7,4},{8,11},{9,10},{10,... | collective-permute-start | bytes 196616 | tf_op jit(solution)/shard_map/ppermute | solution.py:20
  62.0 4.3 %collective-permute-start.17 = (bf16[128,256]{1,0:T(8,128)(2,1)S(1)}, bf16[128,256]{1,0:T(8,128)(2,1)S(1)}, u32[]{:S(2)}, u32[]{:S(2)}) collective-permute-start(bf16[128,256]{1,0:T(8,128)(2,1)S(1)} %get-tuple-element.97), channel_id=1, source_target_pairs={{0,2},{1,3},{2,0},{3,1},{4,6},{5,7},{6,4},{7,5},{8,10},{9,11},{10,... | collective-permute-start | bytes 196616 | tf_op jit(solution)/shard_map/ppermute | solution.py:20
  63.4 4.3 %collective-permute-start.18 = (bf16[128,256]{1,0:T(8,128)(2,1)S(1)}, bf16[128,256]{1,0:T(8,128)(2,1)S(1)}, u32[]{:S(2)}, u32[]{:S(2)}) collective-permute-start(bf16[128,256]{1,0:T(8,128)(2,1)S(1)} %get-tuple-element.96), channel_id=1, source_target_pairs={{0,3},{1,2},{2,1},{3,0},{4,7},{5,6},{6,5},{7,4},{8,11},{9,10},{10,... | collective-permute-start | bytes 196616 | tf_op jit(solution)/shard_map/ppermute | solution.py:20
  68.6 6.9 %collective-permute-start.19 = (bf16[128,256]{1,0:T(8,128)(2,1)S(1)}, bf16[128,256]{1,0:T(8,128)(2,1)S(1)}, u32[]{:S(2)}, u32[]{:S(2)}) collective-permute-start(bf16[128,256]{1,0:T(8,128)(2,1)S(1)} %get-tuple-element.93), channel_id=1, source_target_pairs={{0,12},{1,13},{2,14},{3,15},{4,8},{5,9},{6,10},{7,11},{8,4},{9,5},... | collective-permute-start | bytes 196616 | tf_op jit(solution)/shard_map/ppermute | solution.py:20
  71.2 6.4 %collective-permute-start.20 = (bf16[128,256]{1,0:T(8,128)(2,1)S(1)}, bf16[128,256]{1,0:T(8,128)(2,1)S(1)}, u32[]{:S(2)}, u32[]{:S(2)}) collective-permute-start(bf16[128,256]{1,0:T(8,128)(2,1)S(1)} %get-tuple-element.93), channel_id=1, source_target_pairs={{0,8},{1,9},{2,10},{3,11},{4,12},{5,13},{6,14},{7,15},{8,0},{9,1},... | collective-permute-start | bytes 196616 | tf_op jit(solution)/shard_map/ppermute | solution.py:20
  71.2 6.4 %collective-permute-start.21 = (bf16[128,256]{1,0:T(8,128)(2,1)S(1)}, bf16[128,256]{1,0:T(8,128)(2,1)S(1)}, u32[]{:S(2)}, u32[]{:S(2)}) collective-permute-start(bf16[128,256]{1,0:T(8,128)(2,1)S(1)} %get-tuple-element.93), channel_id=1, source_target_pairs={{0,4},{1,5},{2,6},{3,7},{4,0},{5,1},{6,2},{7,3},{8,12},{9,13},{10,... | collective-permute-start | bytes 196616 | tf_op jit(solution)/shard_map/ppermute | solution.py:20
  73.1 11.4 %collective-permute-start.32 = (bf16[512,512]{1,0:T(8,128)(2,1)S(1)}, bf16[512,512]{1,0:T(8,128)(2,1)S(1)}, u32[]{:S(2)}, u32[]{:S(2)}) collective-permute-start(bf16[512,512]{1,0:T(8,128)(2,1)S(1)} %slice.11.refs_9_.refs_10_.refs_15_), channel_id=1, source_target_pairs={{0,1},{1,0},{2,3},{3,2},{4,5},{5,4},{6,7},{7,6},{8,9},{9,8},{10,11... | collective-permute-start | bytes 1572872 | tf_op jit(solution)/shard_map/ppermute | solution.py:20
  77.8 4.8 %collective-permute-start.26 = (bf16[128,256]{1,0:T(8,128)(2,1)S(1)}, bf16[128,256]{1,0:T(8,128)(2,1)S(1)}, u32[]{:S(2)}, u32[]{:S(2)}) collective-permute-start(bf16[128,256]{1,0:T(8,128)(2,1)S(1)} %convert_add_fusion.1), channel_id=1, source_target_pairs={{0,2},{1,3},{2,0},{3,1},{4,6},{5,7},{6,4},{7,5},{8,10},{9,11},{10,... | collective-permute-start | bytes 196616 | tf_op jit(solution)/shard_map/ppermute | solution.py:20
  79.0 4.4 %collective-permute-start.27 = (bf16[128,256]{1,0:T(8,128)(2,1)S(1)}, bf16[128,256]{1,0:T(8,128)(2,1)S(1)}, u32[]{:S(2)}, u32[]{:S(2)}) collective-permute-start(bf16[128,256]{1,0:T(8,128)(2,1)S(1)} %convert_add_fusion.1), channel_id=1, source_target_pairs={{0,3},{1,2},{2,1},{3,0},{4,7},{5,6},{6,5},{7,4},{8,11},{9,10},{10,... | collective-permute-start | bytes 196616 | tf_op jit(solution)/shard_map/ppermute | solution.py:20
  79.6 27.6 %collective-permute-start.31 = (bf16[512,512]{1,0:T(8,128)(2,1)}, bf16[512,512]{1,0:T(8,128)(2,1)S(1)}, u32[]{:S(2)}, u32[]{:S(2)}) collective-permute-start(bf16[512,512]{1,0:T(8,128)(2,1)} %get-tuple-element.78), channel_id=1, source_target_pairs={{0,8},{1,9},{2,10},{3,11},{4,12},{5,13},{6,14},{7,15},{8,0},{9,1},... | collective-permute-start | bytes 1572872 | tf_op jit(solution)/shard_map/ppermute | solution.py:20
  82.5 24.7 %collective-permute-start.30 = (bf16[512,512]{1,0:T(8,128)(2,1)}, bf16[512,512]{1,0:T(8,128)(2,1)S(1)}, u32[]{:S(2)}, u32[]{:S(2)}) collective-permute-start(bf16[512,512]{1,0:T(8,128)(2,1)} %get-tuple-element.76), channel_id=1, source_target_pairs={{0,4},{1,5},{2,6},{3,7},{4,0},{5,1},{6,2},{7,3},{8,12},{9,13},{10,... | collective-permute-start | bytes 1572872 | tf_op jit(solution)/shard_map/ppermute | solution.py:20
  83.4 23.8 %collective-permute-start.29 = (bf16[512,512]{1,0:T(8,128)(2,1)}, bf16[512,512]{1,0:T(8,128)(2,1)S(1)}, u32[]{:S(2)}, u32[]{:S(2)}) collective-permute-start(bf16[512,512]{1,0:T(8,128)(2,1)} %get-tuple-element.74), channel_id=1, source_target_pairs={{0,2},{1,3},{2,0},{3,1},{4,6},{5,7},{6,4},{7,5},{8,10},{9,11},{10,... | collective-permute-start | bytes 1572872 | tf_op jit(solution)/shard_map/ppermute | solution.py:20
  84.5 22.8 %collective-permute-start.28 = (bf16[512,512]{1,0:T(8,128)(2,1)}, bf16[512,512]{1,0:T(8,128)(2,1)S(1)}, u32[]{:S(2)}, u32[]{:S(2)}) collective-permute-start(bf16[512,512]{1,0:T(8,128)(2,1)} %get-tuple-element.72), channel_id=1, source_target_pairs={{0,1},{1,0},{2,3},{3,2},{4,5},{5,4},{6,7},{7,6},{8,9},{9,8},{10,11... | collective-permute-start | bytes 1572872 | tf_op jit(solution)/shard_map/ppermute | solution.py:20
  92.7 14.4 %collective-permute-start.34 = (bf16[512,256]{1,0:T(8,128)(2,1)S(1)}, bf16[512,256]{1,0:T(8,128)(2,1)S(1)}, u32[]{:S(2)}, u32[]{:S(2)}) collective-permute-start(bf16[512,256]{1,0:T(8,128)(2,1)S(1)} %pad_maximum_fusion.4.refs_7_), channel_id=1, source_target_pairs={{0,16},{16,0},{1,17},{17,1},{2,18},{18,2},{3,19},{19,3},{4,20},{20... | collective-permute-start | bytes 786440 | tf_op jit(solution)/shard_map/ppermute | solution.py:25
  (18 other events, 320.6 us)
